TPU v7x, 1024 devices: a whole 4x4x32 slice. The times are simulated.
1024 devices in a mesh: section: 64 (over y, z_lo, core), dp: 16 (over x, z_hi).
Axes of the slice: x: 4, y: 4, z: 32 (z_hi: 4, z_lo: 8; z = z_hi * 8 + z_lo), core: 2. Of those that a mesh axis runs over, the one named last changes fastest.
Arguments:
- signal: bfloat16 [16384, 4096], P('section', 'dp'), may hold values from -6 to 6
- mixing: bfloat16 [3, 4096, 4096], P(None, 'dp'), may hold values from -0.046875 to 0.046875
- taps: float32 [3, 4, 4096], P(None, None, 'dp'), may hold values from -3 to 3
- offsets: int32 [3, 4], replicated, may hold values from 0 to 63, as said below
Outputs:
- layer_outputs: bfloat16 [3, 16384, 4096], P(None, 'section', 'dp')
Inputs may be any that keep to these rules, and one draw needn't show every extreme that they name: Each layer's 4 offsets are distinct and include 0 and 63.
All inputs are finite; a program needn't handle non-finite values.
Results may differ from a plain program's by a relative error of at most 0.015.
Values may be sent and summed in bfloat16 or wider, within the bound.
No kernel may reach another device: no remote copies, remote signals or barrier semaphores. Data moves between devices by JAX's collectives and lax.ppermute only.
A program may use at most 32 MiB of HBM per device.

v0:
```python
import jax
import jax.numpy as jnp
from jax import lax
from jax.sharding import PartitionSpec as P

C = 4096
REACH = 64


def shifted(value, axis, steps):
    count = lax.axis_size(axis)
    initial, last = (max(0, -steps), min(count, count - steps))
    return lax.ppermute(value, axis, [(source, source + steps) for source in range(initial, last)])


def body(signal, mixing, taps, offsets):
    row_count = signal.shape[0]
    channel_count = signal.shape[1]
    lookback = REACH - 1
    hidden = signal
    results = []
    for layer_index in range(mixing.shape[0]):
        weights = mixing[layer_index]
        coeffs = taps[layer_index]
        shifts = offsets[layer_index]
        values = hidden.astype(jnp.float32)
        squares = lax.psum(jnp.sum(values * values, axis=-1, keepdims=True), "dp")
        normed = values * lax.rsqrt(squares / C + 1e-06)
        stored = normed.astype(jnp.bfloat16)
        previous = shifted(stored[row_count - lookback :], "section", 1)
        padded = jnp.concatenate([previous, stored], axis=0)
        conv = jnp.zeros((row_count, channel_count), jnp.float32)
        for k in range(coeffs.shape[0]):
            start = lookback - shifts[k]
            window = lax.dynamic_slice_in_dim(padded, start, row_count, 0)
            conv = conv + coeffs[k] * window.astype(jnp.float32)
        gated = (conv * jax.nn.silu(normed)).astype(jnp.bfloat16)
        terms = jnp.dot(gated, weights, preferred_element_type=jnp.float32)
        mixed_parts = lax.psum_scatter(
            terms.astype(jnp.bfloat16), "dp", scatter_dimension=1, tiled=True
        ).astype(jnp.float32)
        hidden = (values + mixed_parts).astype(jnp.bfloat16)
        results.append(hidden)
    return jnp.stack(results)


def solution(mesh):
    in_specs = (P("section", "dp"), P(None, "dp", None), P(None, None, "dp"), P())
    out_specs = P(None, "section", "dp")
    return jax.shard_map(body, mesh=mesh, in_specs=in_specs, out_specs=out_specs, check_vma=False)
```

profile of v0, /device:TPU:16, one launch (start us, length us, event | category | flops | bytes accessed | tf_op | source)
XLA Modules:
  0.0 925.4 jit_solution(15359361361358907345)
XLA Ops:
  6.5 0.0 reduce-scatter.4.cloned.1.call-start
  6.5 1.0 fusion.27
  7.6 88.8 %psum.21 = f32[256,1]{0,1:T(1,128)S(1)} all-reduce(f32[256,1]{0,1:T(1,128)S(1)} %bitcast.65), channel_id=1, replica_groups=mesh['section'=64,'dp'=16] {'dp'}, use_global_device_ids=true, to_apply=%region_1.0 | all-reduce | flops 256 | bytes 2048 | tf_op jit(solution)/shard_map/psum | solution.py:27
  96.4 1.0 fusion.8
  97.4 1.9 collective-permute-start
  99.4 0.9 fusion.81
  100.3 1.8 fusion.82
  107.1 3.0 collective-permute-done
  110.2 4.2 convolution_convert_fusion.2
  114.3 0.0 copy-start
  114.3 0.0 reduce-scatter.4.cloned.1.call-update
  114.4 0.0 reduce-scatter.6.cloned.1.call-start
  114.4 205.3 %reduce-scatter.4.cloned.1.call-done = bf16[256,256]{1,0:T(8,128)(2,1)} async-done(((bf16[256,4096]{1,0:T(8,128)(2,1)}), bf16[256,256]{1,0:T(8,128)(2,1)}) %reduce-scatter.4.cloned.1.call-update) | async-done | bytes 131088 | tf_op jit(solution)/shard_map/reduce_scatter | solution.py:39
  319.8 0.0 copy-done
  319.8 1.0 fusion.29
  320.8 75.6 %psum.22 = f32[256,1]{0,1:T(1,128)S(1)} all-reduce(f32[256,1]{0,1:T(1,128)S(1)} %bitcast.63), channel_id=1, replica_groups=mesh['section'=64,'dp'=16] {'dp'}, use_global_device_ids=true, to_apply=%region_4.5 | all-reduce | flops 256 | bytes 2048 | tf_op jit(solution)/shard_map/psum | solution.py:27
  396.4 0.1 fusion.11
  396.6 1.9 collective-permute-start.1
  403.6 5.7 collective-permute-done.1
  409.3 4.1 convolution_convert_fusion.1
  413.4 0.0 reduce-scatter.6.cloned.1.call-update
  413.5 0.0 reduce-scatter.8.cloned.1.call-start
  413.5 202.5 %reduce-scatter.6.cloned.1.call-done = bf16[256,256]{1,0:T(8,128)(2,1)} async-done(((bf16[256,4096]{1,0:T(8,128)(2,1)}), bf16[256,256]{1,0:T(8,128)(2,1)}) %reduce-scatter.6.cloned.1.call-update) | async-done | bytes 131088 | tf_op jit(solution)/shard_map/reduce_scatter | solution.py:39
  616.0 1.0 fusion.31
  617.0 75.7 %psum.23 = f32[256,1]{0,1:T(1,128)S(1)} all-reduce(f32[256,1]{0,1:T(1,128)S(1)} %bitcast.64), channel_id=1, replica_groups=mesh['section'=64,'dp'=16] {'dp'}, use_global_device_ids=true, to_apply=%region_7.8 | all-reduce | flops 256 | bytes 2048 | tf_op jit(solution)/shard_map/psum | solution.py:27
  692.7 0.1 fusion.14
  692.9 1.9 collective-permute-start.2
  699.9 5.6 collective-permute-done.2
  705.6 4.1 convolution_convert_fusion
  709.7 0.0 reduce-scatter.8.cloned.1.call-update
  709.7 207.4 %reduce-scatter.8.cloned.1.call-done = bf16[256,256]{1,0:T(8,128)(2,1)} async-done(((bf16[256,4096]{1,0:T(8,128)(2,1)}), bf16[256,256]{1,0:T(8,128)(2,1)}) %reduce-scatter.8.cloned.1.call-update) | async-done | bytes 131088 | tf_op jit(solution)/shard_map/reduce_scatter | solution.py:39
  917.2 0.9 fusion.51
  918.1 0.8 pad_maximum_fusion
  (6 shorter events, 0.1 us)
Async XLA Ops:
  6.5 313.2 %reduce-scatter.4.cloned.1.call-start = ((), (), s32[]{:S(2)}) async-start(), calls=%async_computation.3 | async-start | bytes 2228224 | tf_op jit(solution)/shard_map/reduce_scatter | solution.py:39
  97.4 12.7 %collective-permute-start = (bf16[63,256]{1,0:T(8,128)(2,1)S(1)}, bf16[63,256]{1,0:T(8,128)(2,1)S(1)}, u32[]{:S(2)}, u32[]{:S(2)}) collective-permute-start(bf16[63,256]{1,0:T(8,128)(2,1)S(1)} %slice.174), channel_id=1, source_target_pairs={{0,16},{16,32},{32,48},{48,64},{64,80},{80,96},{96,112},{112,128},... | collective-permute-start | bytes 96776 | tf_op jit(solution)/shard_map/ppermute | solution.py:13
  114.3 205.4 %copy-start = (bf16[256,256]{1,0:T(8,128)(2,1)S(1)}, bf16[256,256]{1,0:T(8,128)(2,1)}, u32[]{:S(2)}) copy-start(bf16[256,256]{1,0:T(8,128)(2,1)} %param.4) | copy-start | bytes 393220
  114.4 501.6 %reduce-scatter.6.cloned.1.call-start = ((), (), s32[]{:S(2)}) async-start(), calls=%async_computation.4 | async-start | bytes 2228224 | tf_op jit(solution)/shard_map/reduce_scatter | solution.py:39
  396.6 12.7 %collective-permute-start.1 = (bf16[63,256]{1,0:T(8,128)(2,1)S(1)}, bf16[63,256]{1,0:T(8,128)(2,1)S(1)}, u32[]{:S(2)}, u32[]{:S(2)}) collective-permute-start(bf16[63,256]{1,0:T(8,128)(2,1)S(1)} %slice.175), channel_id=1, source_target_pairs={{0,16},{16,32},{32,48},{48,64},{64,80},{80,96},{96,112},{112,128},... | collective-permute-start | bytes 96776 | tf_op jit(solution)/shard_map/ppermute | solution.py:13
  413.5 503.7 %reduce-scatter.8.cloned.1.call-start = ((), (), s32[]{:S(2)}) async-start(), calls=%async_computation.5 | async-start | bytes 2228224 | tf_op jit(solution)/shard_map/reduce_scatter | solution.py:39
  692.9 12.7 %collective-permute-start.2 = (bf16[63,256]{1,0:T(8,128)(2,1)S(1)}, bf16[63,256]{1,0:T(8,128)(2,1)S(1)}, u32[]{:S(2)}, u32[]{:S(2)}) collective-permute-start(bf16[63,256]{1,0:T(8,128)(2,1)S(1)} %slice.176), channel_id=1, source_target_pairs={{0,16},{16,32},{32,48},{48,64},{64,80},{80,96},{96,112},{112,128},... | collective-permute-start | bytes 96776 | tf_op jit(solution)/shard_map/ppermute | solution.py:13
Sparse Core Ops, SparseCore 0:
  114.5 205.2 reduce-scatter.3
  413.6 202.3 reduce-scatter.5
  709.8 207.2 reduce-scatter.7
where the time goes:
time: 925 us
  waiting for transfers between devices  630 us (68%)
  blocking collectives  240 us (26%)
  between operations  28.5 us (3%)
  matrix products  12.4 us (1%)
    reduce_scatter x3, waiting for transfers between devices, body(): lax.psum_scatter(terms.astype(jnp.bfloat16), 'dp', scatter_dimension=1, t...  615 us
    psum x3, blocking collectives, body(): squares = lax.psum(jnp.sum(values * values, axis=-1, keepdims=True), 'dp')  240 us
  transfers between devices with their start and end apart: 6, of which 6 were waited for; matrix products, arithmetic and copies ran while one was open for 0% of the time, Pallas kernels for 0%

commit v1 on v0

v1 whole, which is shorter than its diff:
```python
import jax
import jax.numpy as jnp
from jax import lax
from jax.sharding import Mesh, PartitionSpec as P

C = 4096
REACH = 64
SECTION = ("y", "zl", "c")


def tiled_weights(mixing):
    layers, depth, width = mixing.shape
    n_x, n_zh = lax.axis_size("x"), lax.axis_size("zh")
    n_row = lax.axis_size("zl") * lax.axis_size("c")
    rows, columns = depth // n_row, width // n_x
    row_at = (lax.axis_index("zl") * lax.axis_size("c") + lax.axis_index("c")) * rows
    piece = lax.dynamic_slice(mixing, (0, row_at, lax.axis_index("y") * columns), (layers, rows, columns))
    piece = piece.reshape(layers, rows, n_zh, columns // n_zh)
    piece = lax.all_to_all(piece, "zh", split_axis=2, concat_axis=1)
    piece = lax.all_gather(piece, ("zl", "c"), axis=2, tiled=True)
    piece = piece.reshape(layers, n_zh * depth, columns // n_zh)
    return lax.all_gather(piece, "y", axis=0)


def body(signal, mixing, taps, offsets):
    row_count, channel_count = signal.shape
    n_section = lax.axis_size(SECTION)
    forward = [(source, source + 1) for source in range(n_section - 1)]
    tiles = tiled_weights(mixing)
    coeffs_all = lax.all_gather(taps, "zh", axis=2, tiled=True)
    hidden = signal
    results = []
    for layer in range(mixing.shape[0]):
        wide = lax.all_gather(hidden, "zh", axis=1, tiled=True)
        before = lax.ppermute(wide[row_count - REACH :], SECTION, forward)
        values = jnp.concatenate([before, wide], axis=0).astype(jnp.float32)
        squares = lax.psum(jnp.sum(values * values, axis=-1), "x")
        normed = values * lax.rsqrt(squares / C + 1e-06)[:, None]
        stored = normed.astype(jnp.bfloat16)
        conv = jnp.zeros((row_count, values.shape[1]), jnp.float32)
        for k in range(taps.shape[1]):
            window = lax.dynamic_slice_in_dim(stored, REACH - offsets[layer, k], row_count, 0)
            conv = conv + coeffs_all[layer, k] * window.astype(jnp.float32)
        gated = (conv * jax.nn.silu(normed[REACH:])).astype(jnp.bfloat16)
        partial = jnp.einsum("tk,xkn->xtn", gated, tiles[:, layer], preferred_element_type=jnp.float32)
        terms = lax.all_to_all(partial.astype(jnp.bfloat16), "x", split_axis=0, concat_axis=0)
        mixed = jnp.sum(terms.astype(jnp.float32), axis=0)
        hidden = (hidden.astype(jnp.float32) + mixed).astype(jnp.bfloat16)
        results.append(hidden)
    return jnp.stack(results)


def solution(mesh):
    fine = Mesh(mesh.devices.reshape(4, 8, 2, 4, 4), ("y", "zl", "c", "x", "zh"))
    dp = ("x", "zh")
    in_specs = (P(SECTION, dp), P(None, dp, None), P(None, None, dp), P())
    out_specs = P(None, SECTION, dp)
    return jax.shard_map(body, mesh=fine, in_specs=in_specs, out_specs=out_specs, check_vma=False)
```

time: 925 us -> 451 us (0.49)
  the two profiles are of different devices: /device:TPU:16 before, /device:TPU:8 now
where the time goes in v1:
time: 451 us; the launch traced here: 450 us
  blocking collectives  282 us (63%)
  waiting for transfers between devices  112 us (25%)
  between operations  28.9 us (6%)
  matrix products  10.4 us (2%)
  local copies, waits for them, and re-layouts  9.04 us (2%)
  starting transfers between devices  5.8 us (1%)
    all_gather x3, blocking collectives, body(): wide = lax.all_gather(hidden, 'zh', axis=1, tiled=True)  141 us
    all_gather x1, waiting for transfers between devices, tiled_weights(): piece = lax.all_gather(piece, ('zl', 'c'), axis=2, tiled=True)  95.3 us
    all_to_all x1, blocking collectives, tiled_weights(): piece = lax.all_to_all(piece, 'zh', split_axis=2, concat_axis=1)  53.5 us
    all_to_all x3, blocking collectives, body(): lax.all_to_all(partial.astype(jnp.bfloat16), 'x', split_axis=0, concat_ax...  32.2 us
    psum x3, blocking collectives, body(): squares = lax.psum(jnp.sum(values * values, axis=-1), 'x')  27.7 us
    all_gather x1, blocking collectives, body(): coeffs_all = lax.all_gather(taps, 'zh', axis=2, tiled=True)  27 us
    ppermute x3, waiting for transfers between devices, body(): before = lax.ppermute(wide[row_count - REACH:], SECTION, forward)  16.2 us
    dot_general x3, matrix products, body(): jnp.einsum('tk,xkn->xtn', gated, tiles[:, layer], preferred_element_type=...  10.4 us
  transfers between devices with their start and end apart: 5, of which 3 were waited for; matrix products, arithmetic and copies ran while one was open for 0% of the time, Pallas kernels for 0%

profile of v1, /device:TPU:8, one launch (start us, length us, event | category | flops | bytes accessed | tf_op | source)
XLA Modules:
  0.0 450.1 jit_solution(12763571309915673184)
XLA Ops:
  6.5 0.0 all-gather.6.cloned.1.call-start
  6.5 0.9 constant_dynamic-slice_fusion
  7.5 53.5 %all_to_all.30 = bf16[3,1,16,4,256]{4,2,0,1,3:T(8,128)(2,1)} all-to-all(bf16[3,1,16,4,256]{4,2,0,1,3:T(8,128)(2,1)S(1)} %copy.7), channel_id=1, replica_groups=mesh['y'=4,'zl'=8,'c'=2,'x'=4,'zh'=4] {'zh'}, dimensions={3} | all-to-all | bytes 196608 | tf_op jit(solution)/shard_map/all_to_all | solution.py:19
  61.0 0.0 all-gather.6.cloned.1.call-update
  61.0 0.0 all-gather.4.cloned.1.call-start
  61.1 95.3 %all-gather.6.cloned.1.call-done = bf16[3,4,1,256,1,256]{5,3,0,1,4,2:T(8,128)(2,1)} async-done(((bf16[3,4,1,16,1,256]{5,3,0,1,4,2:T(8,128)(2,1)}), bf16[3,4,1,256,1,256]{5,3,0,1,4,2:T(8,128)(2,1)}) %all-gather.6.cloned.1.call-update) | async-done | bytes 1572880 | tf_op jit(solution)/shard_map/all_gather | solution.py:20
  156.3 2.7 copy.8
  159.1 2.3 all_gather_reshape.3
  161.4 0.0 copy-start
  161.4 0.0 copy-start.1
  161.4 0.0 copy-start.2
  161.4 0.0 all-gather.4.cloned.1.call-update
  161.4 0.9 copy-done
  162.3 0.1 copy.6
  162.4 45.8 %all_gather.21 = bf16[256,1024]{0,1:T(8,128)(2,1)S(1)} all-gather(bf16[256,256]{0,1:T(8,128)(2,1)S(1)} %copy.6), channel_id=1, replica_groups=mesh['y'=4,'zl'=8,'c'=2,'x'=4,'zh'=4] {'zh'}, dimensions={1}, use_global_device_ids=true | all-gather | bytes 655360 | tf_op jit(solution)/shard_map/all_gather | solution.py:34
  208.2 0.1 slice.134
  208.4 1.9 collective-permute-start
  210.3 0.0 copy-done.1
  210.3 0.7 fusion.50
  216.0 0.0 copy-done.2
  216.0 27.0 %all_gather.20 = f32[3,4,1024]{2,1,0:T(4,128)S(1)} all-gather(f32[3,4,256]{2,1,0:T(4,128)S(1)} %copy-done.2), channel_id=1, replica_groups=mesh['y'=4,'zl'=8,'c'=2,'x'=4,'zh'=4] {'zh'}, dimensions={2}, use_global_device_ids=true | all-gather | bytes 61440 | tf_op jit(solution)/shard_map/all_gather | solution.py:30
  243.0 0.0 collective-permute-done
  243.1 0.4 fusion.3
  243.5 10.6 %psum.21 = f32[320]{0:T(512)S(1)} all-reduce(f32[320]{0:T(512)S(1)} %fusion.3), channel_id=1, replica_groups=mesh['y'=4,'zl'=8,'c'=2,'x'=4,'zh'=4] {'x'}, use_global_device_ids=true, to_apply=%region_1.0 | all-reduce | flops 320 | bytes 2560 | tf_op jit(solution)/shard_map/psum | solution.py:37
  254.1 0.4 fusion.40
  254.5 0.0 all-gather.4.cloned.1.call-done
  254.5 3.4 fusion.11
  258.0 10.5 %all_to_all.31 = bf16[4,256,256]{1,2,0:T(8,128)(2,1)S(1)} all-to-all(bf16[4,256,256]{1,2,0:T(8,128)(2,1)S(1)} %fusion.11), channel_id=1, replica_groups=mesh['y'=4,'zl'=8,'c'=2,'x'=4,'zh'=4] {'x'}, dimensions={0} | all-to-all | bytes 1048576 | tf_op jit(solution)/shard_map/all_to_all | solution.py:46
  268.4 0.1 convert_reduce_fusion.2
  268.6 54.2 %all_gather.22 = bf16[256,1024]{0,1:T(8,128)(2,1)S(1)} all-gather(bf16[256,256]{0,1:T(8,128)(2,1)S(1)} %add_convert_fusion.2), channel_id=1, replica_groups=mesh['y'=4,'zl'=8,'c'=2,'x'=4,'zh'=4] {'zh'}, dimensions={1}, use_global_device_ids=true | all-gather | bytes 655360 | tf_op jit(solution)/shard_map/all_gather | solution.py:34
  322.8 0.1 slice.141
  322.9 1.9 collective-permute-start.1
  330.2 7.9 %collective-permute-done.1 = bf16[64,1024]{0,1:T(8,128)(2,1)S(1)} collective-permute-done((bf16[64,1024]{0,1:T(8,128)(2,1)S(1)}, bf16[64,1024]{0,1:T(8,128)(2,1)S(1)}, u32[]{:S(2)}, u32[]{:S(2)}) %collective-permute-start.1) | collective-permute-done | bytes 131104 | tf_op jit(solution)/shard_map/ppermute | solution.py:35
  338.1 0.4 fusion.4
  338.6 9.3 %psum.22 = f32[320]{0:T(512)S(1)} all-reduce(f32[320]{0:T(512)S(1)} %fusion.4), channel_id=1, replica_groups=mesh['y'=4,'zl'=8,'c'=2,'x'=4,'zh'=4] {'x'}, use_global_device_ids=true, to_apply=%region_4.5 | all-reduce | flops 320 | bytes 2560 | tf_op jit(solution)/shard_map/psum | solution.py:37
  347.9 0.4 fusion.41
  348.3 3.5 fusion.10
  351.8 10.5 %all_to_all.32 = bf16[4,256,256]{1,2,0:T(8,128)(2,1)S(1)} all-to-all(bf16[4,256,256]{1,2,0:T(8,128)(2,1)S(1)} %fusion.10), channel_id=1, replica_groups=mesh['y'=4,'zl'=8,'c'=2,'x'=4,'zh'=4] {'x'}, dimensions={0} | all-to-all | bytes 1048576 | tf_op jit(solution)/shard_map/all_to_all | solution.py:46
  362.3 0.1 convert_reduce_fusion.1
  362.4 41.1 %all_gather.23 = bf16[256,1024]{0,1:T(8,128)(2,1)S(1)} all-gather(bf16[256,256]{0,1:T(8,128)(2,1)S(1)} %add_convert_fusion.1), channel_id=1, replica_groups=mesh['y'=4,'zl'=8,'c'=2,'x'=4,'zh'=4] {'zh'}, dimensions={1}, use_global_device_ids=true | all-gather | bytes 655360 | tf_op jit(solution)/shard_map/all_gather | solution.py:34
  403.5 0.1 slice.148
  403.6 1.9 collective-permute-start.2
  410.5 8.4 %collective-permute-done.2 = bf16[64,1024]{0,1:T(8,128)(2,1)S(1)} collective-permute-done((bf16[64,1024]{0,1:T(8,128)(2,1)S(1)}, bf16[64,1024]{0,1:T(8,128)(2,1)S(1)}, u32[]{:S(2)}, u32[]{:S(2)}) %collective-permute-start.2) | collective-permute-done | bytes 131104 | tf_op jit(solution)/shard_map/ppermute | solution.py:35
  418.8 0.4 fusion.5
  419.3 7.8 %psum.23 = f32[320]{0:T(512)S(1)} all-reduce(f32[320]{0:T(512)S(1)} %fusion.5), channel_id=1, replica_groups=mesh['y'=4,'zl'=8,'c'=2,'x'=4,'zh'=4] {'x'}, use_global_device_ids=true, to_apply=%region_7.8 | all-reduce | flops 320 | bytes 2560 | tf_op jit(solution)/shard_map/psum | solution.py:37
  427.0 0.4 fusion.42
  427.4 3.5 fusion.9
  430.9 11.2 %all_to_all.33 = bf16[4,256,256]{1,2,0:T(8,128)(2,1)S(1)} all-to-all(bf16[4,256,256]{1,2,0:T(8,128)(2,1)S(1)} %fusion.9), channel_id=1, replica_groups=mesh['y'=4,'zl'=8,'c'=2,'x'=4,'zh'=4] {'x'}, dimensions={0} | all-to-all | bytes 1048576 | tf_op jit(solution)/shard_map/all_to_all | solution.py:46
  442.1 0.1 convert_reduce_fusion
  442.3 0.9 copy.13
  (10 shorter events, 0.3 us)
Async XLA Ops:
  6.5 149.8 %all-gather.6.cloned.1.call-start = ((), (), s32[]{:S(2)}) async-start(), calls=%async_computation.5 | async-start | bytes 1671168 | tf_op jit(solution)/shard_map/all_gather | solution.py:20
  61.0 193.5 %all-gather.4.cloned.1.call-start = ((), (), s32[]{:S(2)}) async-start(), calls=%async_computation.4 | async-start | bytes 7864320 | tf_op jit(solution)/shard_map/all_gather | solution.py:22
  161.4 0.9 copy-start
  161.4 48.9 %copy-start.1 = (s32[3,4]{1,0:T(4,128)S(1)}, s32[3,4]{1,0:T(4,128)}, u32[]{:S(2)}) copy-start(s32[3,4]{1,0:T(4,128)} %param.7) | copy-start | bytes 148
  161.4 54.6 %copy-start.2 = (f32[3,4,256]{2,1,0:T(4,128)S(1)}, f32[3,4,256]{2,1,0:T(4,128)}, u32[]{:S(2)}) copy-start(f32[3,4,256]{2,1,0:T(4,128)} %param.6) | copy-start | bytes 36868
  208.4 34.7 %collective-permute-start = (bf16[64,1024]{0,1:T(8,128)(2,1)S(1)}, bf16[64,1024]{0,1:T(8,128)(2,1)S(1)}, u32[]{:S(2)}, u32[]{:S(2)}) collective-permute-start(bf16[64,1024]{0,1:T(8,128)(2,1)S(1)} %slice.134), channel_id=1, source_target_pairs={{0,16},{16,32},{32,48},{48,64},{64,80},{80,96},{96,112},{112,128},... | collective-permute-start | bytes 393224 | tf_op jit(solution)/shard_map/ppermute | solution.py:35
  322.9 15.2 %collective-permute-start.1 = (bf16[64,1024]{0,1:T(8,128)(2,1)S(1)}, bf16[64,1024]{0,1:T(8,128)(2,1)S(1)}, u32[]{:S(2)}, u32[]{:S(2)}) collective-permute-start(bf16[64,1024]{0,1:T(8,128)(2,1)S(1)} %slice.141), channel_id=1, source_target_pairs={{0,16},{16,32},{32,48},{48,64},{64,80},{80,96},{96,112},{112,128},... | collective-permute-start | bytes 393224 | tf_op jit(solution)/shard_map/ppermute | solution.py:35
  403.6 15.2 %collective-permute-start.2 = (bf16[64,1024]{0,1:T(8,128)(2,1)S(1)}, bf16[64,1024]{0,1:T(8,128)(2,1)S(1)}, u32[]{:S(2)}, u32[]{:S(2)}) collective-permute-start(bf16[64,1024]{0,1:T(8,128)(2,1)S(1)} %slice.148), channel_id=1, source_target_pairs={{0,16},{16,32},{32,48},{48,64},{64,80},{80,96},{96,112},{112,128},... | collective-permute-start | bytes 393224 | tf_op jit(solution)/shard_map/ppermute | solution.py:35
Sparse Core Ops, SparseCore 0:
  61.1 95.1 all-gather.5
  161.5 84.8 all-gather.3

commit v2 on v1

v2 whole, which is shorter than its diff:
```python
import jax
import jax.numpy as jnp
from jax import lax
from jax.sharding import Mesh, PartitionSpec as P

C = 4096
REACH = 64
SECTION = ("y", "zl", "c")


def rotated(value, axis, steps):
    count = lax.axis_size(axis)
    return lax.ppermute(value, axis, [(source, (source + steps) % count) for source in range(count)])


def crossed_weights(mixing):
    layers, depth, width = mixing.shape
    n_y, n_c, n_zh = lax.axis_size("y"), lax.axis_size("c"), lax.axis_size("zh")
    y, c = lax.axis_index("y"), lax.axis_index("c")
    columns = width // n_y
    rows = depth // n_c
    first = lax.dynamic_slice(mixing, (0, c * rows, y * columns), (1, rows, columns))
    first = first.reshape(rows, n_zh, columns // n_zh).transpose(1, 0, 2)
    few = depth // (lax.axis_size("zl") * n_c)
    rest = lax.dynamic_slice(
        mixing, (1, (lax.axis_index("zl") * n_c + c) * few, y * columns), (layers - 1, few, columns)
    )
    rest = rest.reshape(layers - 1, few, n_zh, columns // n_zh).transpose(2, 0, 1, 3)
    rest = rest.reshape(n_zh, (layers - 1) * few, columns // n_zh)
    got = lax.all_to_all(jnp.concatenate([first, rest], axis=1), "zh", split_axis=0, concat_axis=0)
    return got[:, :rows], got[:, rows:]


def later_tiles(rest, layers):
    n_zh, rows, columns = rest.shape
    few = rows // layers
    n_y = lax.axis_size("y")
    n_row = lax.axis_size("zl") * lax.axis_size("c")
    gathered = lax.all_gather(rest, SECTION, axis=0)
    gathered = gathered.reshape(n_y, n_row, n_zh, layers, few, columns).transpose(3, 0, 2, 1, 4, 5)
    return gathered.reshape(layers, n_y, n_zh * n_row * few, columns)


def body(signal, mixing, taps, offsets):
    row_count, channel_count = signal.shape
    layers, n_taps = taps.shape[:2]
    n_section = lax.axis_size(SECTION)
    n_y = lax.axis_size("y")
    forward = [(source, source + 1) for source in range(n_section - 1)]
    first, rest = crossed_weights(mixing)
    signal, first, rest = lax.optimization_barrier((signal, first, rest))
    later = later_tiles(rest, layers - 1)
    own = lax.all_gather(first, "c", axis=1, tiled=True).reshape(-1, channel_count)
    turned = jnp.stack([own] + [rotated(own, "y", k) for k in range(1, n_y)])
    high = lax.reduce_precision(taps, 8, 7)
    low = (taps - high).astype(jnp.bfloat16)
    tap_rows = jnp.concatenate(
        [high.astype(jnp.bfloat16).reshape(-1, channel_count), low.reshape(-1, channel_count)], axis=0
    )
    n_tap_rows = layers * n_taps
    tap_rows = jnp.pad(tap_rows, ((0, -2 * n_tap_rows % 16), (0, 0)))
    hidden = signal
    results = []
    for layer in range(layers):
        if layer == 0:
            wide = lax.all_gather(jnp.concatenate([hidden, tap_rows], axis=0), "zh", axis=1, tiled=True)
            coeffs = wide[row_count : row_count + 2 * n_tap_rows].astype(jnp.float32)
            coeffs = (coeffs[:n_tap_rows] + coeffs[n_tap_rows:]).reshape(layers, n_taps, -1)
            wide = wide[:row_count]
        else:
            wide = lax.all_gather(hidden, "zh", axis=1, tiled=True)
        before = lax.ppermute(wide[row_count - REACH :], SECTION, forward)
        values = jnp.concatenate([before, wide], axis=0).astype(jnp.float32)
        squares = lax.psum(jnp.sum(values * values, axis=-1), "x")
        normed = values * lax.rsqrt(squares / C + 1e-06)[:, None]
        stored = normed.astype(jnp.bfloat16)
        conv = jnp.zeros((row_count, values.shape[1]), jnp.float32)
        for k in range(n_taps):
            window = lax.dynamic_slice_in_dim(stored, REACH - offsets[layer, k], row_count, 0)
            conv = conv + coeffs[layer, k] * window.astype(jnp.float32)
        gated = (conv * jax.nn.silu(normed[REACH:])).astype(jnp.bfloat16)
        tile = turned if layer == 0 else later[layer - 1]
        partial = jnp.einsum("tk,xkn->xtn", gated, tile, preferred_element_type=jnp.float32).astype(jnp.bfloat16)
        if layer == 0:
            partial = partial[(lax.axis_index("y") - jnp.arange(n_y)) % n_y]
        terms = lax.all_to_all(partial, "x", split_axis=0, concat_axis=0)
        mixed = jnp.sum(terms.astype(jnp.float32), axis=0)
        hidden = (hidden.astype(jnp.float32) + mixed).astype(jnp.bfloat16)
        results.append(hidden)
    return jnp.stack(results)


def solution(mesh):
    fine = Mesh(mesh.devices.reshape(4, 8, 2, 4, 4), ("y", "zl", "c", "x", "zh"))
    dp = ("x", "zh")
    in_specs = (P(SECTION, dp), P(None, dp, None), P(None, None, dp), P())
    out_specs = P(None, SECTION, dp)
    return jax.shard_map(body, mesh=fine, in_specs=in_specs, out_specs=out_specs, check_vma=False)
```

time: 451 us -> 375 us (0.83)
  the two profiles are of different devices: /device:TPU:8 before, /device:TPU:24 now
where the time goes in v2:
time: 375 us; the launch traced here: 374 us
  blocking collectives  276 us (74%)
  between operations  28.7 us (8%)
  waiting for transfers between devices  28.6 us (8%)
  starting transfers between devices  15.4 us (4%)
  local copies, waits for them, and re-layouts  13.4 us (4%)
  matrix products  8.03 us (2%)
  other arithmetic  4.44 us (1%)
    all_gather x2, blocking collectives, body(): wide = lax.all_gather(hidden, 'zh', axis=1, tiled=True)  88.1 us
    all_to_all x1, blocking collectives, crossed_weights(): lax.all_to_all(jnp.concatenate([first, rest], axis=1), 'zh', split_axis=0...  64 us
    all_gather x1, blocking collectives, body(): lax.all_gather(jnp.concatenate([hidden, tap_rows], axis=0), 'zh', axis=1,...  57.7 us
    all_to_all x3, blocking collectives, body(): terms = lax.all_to_all(partial, 'x', split_axis=0, concat_axis=0)  31.9 us
    psum x3, blocking collectives, body(): squares = lax.psum(jnp.sum(values * values, axis=-1), 'x')  31.8 us
    ppermute x3, waiting for transfers between devices, body(): before = lax.ppermute(wide[row_count - REACH:], SECTION, forward)  28.6 us
    ppermute x3, starting transfers between devices, rotated(): lax.ppermute(value, axis, [(source, (source + steps) % count) for source...  9.59 us
    dot_general x3, matrix products, body(): jnp.einsum('tk,xkn->xtn', gated, tile, preferred_element_type=jnp.float32)  8.03 us
  transfers between devices with their start and end apart: 7, of which 3 were waited for; matrix products, arithmetic and copies ran while one was open for 3% of the time, Pallas kernels for 0%

profile of v2, /device:TPU:24, one launch (start us, length us, event | category | flops | bytes accessed | tf_op | source)
XLA Modules:
  0.0 374.2 jit_solution(8672458296212704229)
XLA Ops:
  6.5 0.8 constant_dynamic-slice_fusion.1
  7.4 0.2 copy.55
  7.6 1.0 constant_dynamic-slice_fusion
  8.6 0.2 copy.83
  8.8 0.0 copy-start.3
  8.8 0.0 copy-start.4
  8.8 0.1 pad_maximum_fusion.3
  8.9 0.2 copy.56
  9.1 0.0 copy-start.2
  9.1 64.0 %all_to_all.20 = bf16[4,160,256]{2,1,0:T(8,128)(2,1)S(1)} all-to-all(bf16[4,160,256]{2,1,0:T(8,128)(2,1)S(1)} %copy.56), channel_id=1, replica_groups=mesh['y'=4,'zl'=8,'c'=2,'x'=4,'zh'=4] {'zh'}, dimensions={0} | all-to-all | bytes 655360 | tf_op jit(solution)/shard_map/all_to_all | solution.py:30
  73.1 0.6 slice.158
  73.8 0.0 all-gather.3.cloned.1.call-update
  73.8 0.7 fusion.64
  79.5 0.0 copy-done.4
  79.6 0.1 copy.60
  79.8 2.2 all_gather.18
  81.9 0.2 copy.79
  82.2 2.7 collective-permute-start.2
  84.8 2.9 collective-permute-start.1
  87.7 4.1 %collective-permute-start = (bf16[1024,256]{0,1:T(8,128)(2,1)S(1)}, bf16[1024,256]{0,1:T(8,128)(2,1)}, u32[]{:S(2)}, u32[]{:S(2)}) collective-permute-start(bf16[1024,256]{0,1:T(8,128)(2,1)S(1)} %copy.79), channel_id=1, source_target_pairs={{0,256},{256,512},{512,768},{768,0},{1,257},{257,513},{513,769},{7... | collective-permute-start | bytes 1572872 | tf_op jit(solution)/shard_map/ppermute | solution.py:13
  91.8 0.1 copy.57
  91.9 57.7 %all_gather.19 = bf16[288,1024]{0,1:T(8,128)(2,1)S(1)} all-gather(bf16[288,256]{0,1:T(8,128)(2,1)S(1)} %fusion.47), channel_id=1, replica_groups=mesh['y'=4,'zl'=8,'c'=2,'x'=4,'zh'=4] {'zh'}, dimensions={1}, use_global_device_ids=true | all-gather | bytes 737280 | tf_op jit(solution)/shard_map/all_gather | solution.py:66
  149.6 0.1 slice.163
  149.8 0.2 copy.78
  150.0 1.9 collective-permute-start.3
  151.9 0.2 slice_add_fusion
  152.1 0.2 copy.62
  152.4 13.6 %collective-permute-done.3 = bf16[64,1024]{0,1:T(8,128)(2,1)S(1)} collective-permute-done((bf16[64,1024]{0,1:T(8,128)(2,1)S(1)}, bf16[64,1024]{0,1:T(8,128)(2,1)S(1)}, u32[]{:S(2)}, u32[]{:S(2)}) %collective-permute-start.3) | collective-permute-done | bytes 131104 | tf_op jit(solution)/shard_map/ppermute | solution.py:72
  166.0 0.4 fusion.8
  166.4 13.3 %psum.21 = f32[320]{0:T(512)S(1)} all-reduce(f32[320]{0:T(512)S(1)} %fusion.8), channel_id=1, replica_groups=mesh['y'=4,'zl'=8,'c'=2,'x'=4,'zh'=4] {'x'}, use_global_device_ids=true, to_apply=%region_1.2 | all-reduce | flops 320 | bytes 2560 | tf_op jit(solution)/shard_map/psum | solution.py:74
  179.8 0.4 fusion.49
  180.2 0.0 collective-permute-done.2
  180.2 0.0 collective-permute-done.1
  180.2 0.0 collective-permute-done
  180.2 3.3 fusion.14
  183.5 0.6 gather_fusion
  184.1 10.9 %all_to_all.21 = bf16[4,256,256]{1,2,0:T(8,128)(2,1)S(1)} all-to-all(bf16[4,256,256]{1,2,0:T(8,128)(2,1)S(1)} %gather_fusion), channel_id=1, replica_groups=mesh['y'=4,'zl'=8,'c'=2,'x'=4,'zh'=4] {'x'}, dimensions={0} | all-to-all | bytes 1048576 | tf_op jit(solution)/shard_map/all_to_all | solution.py:86
  195.0 0.1 convert_reduce_fusion.2
  195.1 44.8 %all_gather.22 = bf16[256,1024]{0,1:T(8,128)(2,1)S(1)} all-gather(bf16[256,256]{0,1:T(8,128)(2,1)S(1)} %add_convert_fusion.2), channel_id=1, replica_groups=mesh['y'=4,'zl'=8,'c'=2,'x'=4,'zh'=4] {'zh'}, dimensions={1}, use_global_device_ids=true | all-gather | bytes 655360 | tf_op jit(solution)/shard_map/all_gather | solution.py:71
  239.9 0.1 slice.171
  240.0 1.9 collective-permute-start.4
  247.0 8.2 %collective-permute-done.4 = bf16[64,1024]{0,1:T(8,128)(2,1)S(1)} collective-permute-done((bf16[64,1024]{0,1:T(8,128)(2,1)S(1)}, bf16[64,1024]{0,1:T(8,128)(2,1)S(1)}, u32[]{:S(2)}, u32[]{:S(2)}) %collective-permute-start.4) | collective-permute-done | bytes 131104 | tf_op jit(solution)/shard_map/ppermute | solution.py:72
  255.2 0.4 fusion.9
  255.7 9.7 %psum.22 = f32[320]{0:T(512)S(1)} all-reduce(f32[320]{0:T(512)S(1)} %fusion.9), channel_id=1, replica_groups=mesh['y'=4,'zl'=8,'c'=2,'x'=4,'zh'=4] {'x'}, use_global_device_ids=true, to_apply=%region_4.5 | all-reduce | flops 320 | bytes 2560 | tf_op jit(solution)/shard_map/psum | solution.py:74
  265.4 1.6 fusion.50
  267.0 2.6 fusion.62
  269.6 0.2 copy.64
  269.8 1.2 copy-done.1
  271.0 2.4 fusion.17
  273.3 10.5 %all_to_all.22 = bf16[4,256,256]{1,2,0:T(8,128)(2,1)S(1)} all-to-all(bf16[4,256,256]{1,2,0:T(8,128)(2,1)S(1)} %fusion.17), channel_id=1, replica_groups=mesh['y'=4,'zl'=8,'c'=2,'x'=4,'zh'=4] {'x'}, dimensions={0} | all-to-all | bytes 1048576 | tf_op jit(solution)/shard_map/all_to_all | solution.py:86
  283.8 0.1 convert_reduce_fusion.1
  283.9 43.3 %all_gather.23 = bf16[256,1024]{0,1:T(8,128)(2,1)S(1)} all-gather(bf16[256,256]{0,1:T(8,128)(2,1)S(1)} %add_convert_fusion.1), channel_id=1, replica_groups=mesh['y'=4,'zl'=8,'c'=2,'x'=4,'zh'=4] {'zh'}, dimensions={1}, use_global_device_ids=true | all-gather | bytes 655360 | tf_op jit(solution)/shard_map/all_gather | solution.py:71
  327.2 0.1 slice.178
  327.4 1.9 collective-permute-start.5
  334.2 1.6 copy.67
  335.8 6.8 %collective-permute-done.5 = bf16[64,1024]{0,1:T(8,128)(2,1)S(1)} collective-permute-done((bf16[64,1024]{0,1:T(8,128)(2,1)S(1)}, bf16[64,1024]{0,1:T(8,128)(2,1)S(1)}, u32[]{:S(2)}, u32[]{:S(2)}) %collective-permute-start.5) | collective-permute-done | bytes 131104 | tf_op jit(solution)/shard_map/ppermute | solution.py:72
  342.6 0.4 fusion.10
  343.0 8.8 %psum.23 = f32[320]{0:T(512)S(1)} all-reduce(f32[320]{0:T(512)S(1)} %fusion.10), channel_id=1, replica_groups=mesh['y'=4,'zl'=8,'c'=2,'x'=4,'zh'=4] {'x'}, use_global_device_ids=true, to_apply=%region_7.8 | all-reduce | flops 320 | bytes 2560 | tf_op jit(solution)/shard_map/psum | solution.py:74
  351.8 0.4 fusion.51
  352.2 1.2 copy-done
  353.4 2.4 fusion.18
  355.8 10.5 %all_to_all.23 = bf16[4,256,256]{1,2,0:T(8,128)(2,1)S(1)} all-to-all(bf16[4,256,256]{1,2,0:T(8,128)(2,1)S(1)} %fusion.18), channel_id=1, replica_groups=mesh['y'=4,'zl'=8,'c'=2,'x'=4,'zh'=4] {'x'}, dimensions={0} | all-to-all | bytes 1048576 | tf_op jit(solution)/shard_map/all_to_all | solution.py:86
  366.3 0.1 convert_reduce_fusion
  366.5 0.9 copy.70
  (26 shorter events, 0.5 us)
Async XLA Ops:
  6.5 260.4 %all-gather.3.cloned.1.call-start = ((), (), s32[]{:S(2)}) async-start(), calls=%async_computation.4 | async-start | bytes 4259840 | tf_op jit(solution)/shard_map/all_gather | solution.py:39
  8.8 65.1 %copy-start.3 = (s32[3,4]{1,0:T(4,128)S(1)}, s32[3,4]{1,0:T(4,128)}, u32[]{:S(2)}) copy-start(s32[3,4]{1,0:T(4,128)} %param.7) | copy-start | bytes 148
  8.8 70.7 %copy-start.4 = (f32[3,4,256]{2,1,0:T(4,128)S(1)}, f32[3,4,256]{2,1,0:T(4,128)}, u32[]{:S(2)}) copy-start(f32[3,4,256]{2,1,0:T(4,128)} %param.6) | copy-start | bytes 36868
  9.1 82.7 %copy-start.2 = (bf16[256,256]{1,0:T(8,128)(2,1)S(1)}, bf16[256,256]{1,0:T(8,128)(2,1)}, u32[]{:S(2)}) copy-start(bf16[256,256]{1,0:T(8,128)(2,1)} %param.4) | copy-start | bytes 393220
  82.2 98.0 %collective-permute-start.2 = (bf16[1024,256]{0,1:T(8,128)(2,1)S(1)}, bf16[1024,256]{0,1:T(8,128)(2,1)}, u32[]{:S(2)}, u32[]{:S(2)}) collective-permute-start(bf16[1024,256]{0,1:T(8,128)(2,1)S(1)} %copy.79), channel_id=1, source_target_pairs={{0,768},{256,0},{512,256},{768,512},{1,769},{257,1},{513,257},{769... | collective-permute-start | bytes 1572872 | tf_op jit(solution)/shard_map/ppermute | solution.py:13
  84.8 95.4 %collective-permute-start.1 = (bf16[1024,256]{0,1:T(8,128)(2,1)S(1)}, bf16[1024,256]{0,1:T(8,128)(2,1)}, u32[]{:S(2)}, u32[]{:S(2)}) collective-permute-start(bf16[1024,256]{0,1:T(8,128)(2,1)S(1)} %copy.79), channel_id=1, source_target_pairs={{0,512},{256,768},{512,0},{768,256},{1,513},{257,769},{513,1},{769... | collective-permute-start | bytes 1572872 | tf_op jit(solution)/shard_map/ppermute | solution.py:13
  87.7 92.5 %collective-permute-start = (bf16[1024,256]{0,1:T(8,128)(2,1)S(1)}, bf16[1024,256]{0,1:T(8,128)(2,1)}, u32[]{:S(2)}, u32[]{:S(2)}) collective-permute-start(bf16[1024,256]{0,1:T(8,128)(2,1)S(1)} %copy.79), channel_id=1, source_target_pairs={{0,256},{256,512},{512,768},{768,0},{1,257},{257,513},{513,769},{7... | collective-permute-start | bytes 1572872 | tf_op jit(solution)/shard_map/ppermute | solution.py:13
  150.0 16.0 %collective-permute-start.3 = (bf16[64,1024]{0,1:T(8,128)(2,1)S(1)}, bf16[64,1024]{0,1:T(8,128)(2,1)S(1)}, u32[]{:S(2)}, u32[]{:S(2)}) collective-permute-start(bf16[64,1024]{0,1:T(8,128)(2,1)S(1)} %slice.163), channel_id=1, source_target_pairs={{0,16},{16,32},{32,48},{48,64},{64,80},{80,96},{96,112},{112,128},... | collective-permute-start | bytes 393224 | tf_op jit(solution)/shard_map/ppermute | solution.py:72
  240.0 15.2 %collective-permute-start.4 = (bf16[64,1024]{0,1:T(8,128)(2,1)S(1)}, bf16[64,1024]{0,1:T(8,128)(2,1)S(1)}, u32[]{:S(2)}, u32[]{:S(2)}) collective-permute-start(bf16[64,1024]{0,1:T(8,128)(2,1)S(1)} %slice.171), channel_id=1, source_target_pairs={{0,16},{16,32},{32,48},{48,64},{64,80},{80,96},{96,112},{112,128},... | collective-permute-start | bytes 393224 | tf_op jit(solution)/shard_map/ppermute | solution.py:72
  269.5 1.4 copy-start.1
  327.4 15.2 %collective-permute-start.5 = (bf16[64,1024]{0,1:T(8,128)(2,1)S(1)}, bf16[64,1024]{0,1:T(8,128)(2,1)S(1)}, u32[]{:S(2)}, u32[]{:S(2)}) collective-permute-start(bf16[64,1024]{0,1:T(8,128)(2,1)S(1)} %slice.178), channel_id=1, source_target_pairs={{0,16},{16,32},{32,48},{48,64},{64,80},{80,96},{96,112},{112,128},... | collective-permute-start | bytes 393224 | tf_op jit(solution)/shard_map/ppermute | solution.py:72
  351.8 1.6 copy-start
Sparse Core Ops, SparseCore 0:
  74.0 173.3 all-gather.2

commit v3 on v1

v3 whole, which is shorter than its diff:
```python
import jax
import jax.numpy as jnp
from jax import lax
from jax.sharding import Mesh, PartitionSpec as P

REACH = 64
SECTION = ("y", "zl", "c")
TURNED = ("y", "zl", "zh")
PLACE = ("zl", "c", "zh")


def turn_pairs(n_y, n_zl, n_zh):
    pairs = []
    for y in range(n_y):
        for zl in range(n_zl):
            for zh in range(n_zh):
                q, r = divmod(zl, 2)
                source = (y * n_zl + zl) * n_zh + zh
                target = (zh * n_zl + 2 * y + r) * n_zh + q
                pairs.append((source, target))
    return pairs


def halo_pairs(n_y, n_zl, n_c, n_zh):
    places = []
    for y in range(n_y):
        for zl in range(n_zl):
            for c in range(n_c):
                q, r = divmod(zl, 2)
                places.append(((2 * y + r) * n_c + c) * n_zh + q)
    return list(zip(places[:-1], places[1:]))


def crossed(value, axis, bit):
    return lax.ppermute(value, axis, [(i, i ^ bit) for i in range(lax.axis_size(axis))])


def after(value, *others):
    return lax.optimization_barrier((value, *others))[0]


def body(signal, mixing, taps, offsets):
    row_count, width = signal.shape
    layers, n_taps = taps.shape[:2]
    n_x, n_y, n_zl, n_c, n_zh = (lax.axis_size(a) for a in ("x", "y", "zl", "c", "zh"))
    y, zl, c = lax.axis_index("y"), lax.axis_index("zl"), lax.axis_index("c")
    total_channels = n_x * n_zh * width
    there = turn_pairs(n_y, n_zl, n_zh)
    back = [(target, source) for source, target in there]
    forward = halo_pairs(n_y, n_zl, n_c, n_zh)

    hidden = lax.ppermute(signal, TURNED, there)

    low_bits = zl % n_x
    half = width // n_c
    share = lax.dynamic_slice(mixing, (0, c * half, (low_bits * n_y + y) * width), (layers, half, width))
    high = lax.reduce_precision(taps, 8, 7)
    low = (taps - high).astype(jnp.bfloat16)
    n_tap_rows = layers * n_taps
    sent = jnp.concatenate(
        [
            share.reshape(layers * half, width),
            high.astype(jnp.bfloat16).reshape(n_tap_rows, width),
            low.reshape(n_tap_rows, width),
            jnp.zeros((-2 * n_tap_rows % 16, width), jnp.bfloat16),
        ],
        axis=0,
    )
    got = lax.all_gather(sent, "zh", axis=0)
    hidden, got = lax.optimization_barrier((hidden, got))
    coeffs = got[:, layers * half :].astype(jnp.float32)
    coeffs = coeffs[:, :n_tap_rows] + coeffs[:, n_tap_rows : 2 * n_tap_rows]
    coeffs = coeffs.transpose(1, 0, 2).reshape(layers, n_taps, n_zh * width)
    shares = got[:, : layers * half].reshape(n_zh, layers, half, width).transpose(1, 0, 2, 3)
    first = shares[:1].reshape(1, 1, n_zh * half, width)
    rest = shares[1:].reshape(1, layers - 1, n_zh * half, width)

    first = jnp.concatenate([first, crossed(first, "zl", 2)], axis=0)
    order = jnp.array([0, 2, 1, 3])
    entry_of = order[jnp.arange(n_x) ^ low_bits]
    results = []
    own = other = None
    for layer in range(layers):
        if layer == layers - 1:
            earlier = lax.ppermute(jnp.stack(results), TURNED, back)
        wide = lax.all_gather(hidden, "y", axis=1, tiled=True)
        if layer == 0:
            wide, first = lax.optimization_barrier((wide, first))
            first = jnp.concatenate([first, crossed(first, "zl", 1)], axis=0)
        else:
            own = rest[:, layer - 1]
            other = crossed(after(own, wide), "c", 1)
        before = lax.ppermute(wide[row_count - REACH :], PLACE, forward)
        values = jnp.concatenate([before, wide], axis=0).astype(jnp.float32)
        squares = lax.psum(jnp.sum(values * values, axis=-1), "x")
        if layer == 0:
            squares, first, rest = lax.optimization_barrier((squares, first, rest))
            own = first[:, 0]
            other = crossed(own, "c", 1)
            rest = jnp.concatenate([rest, crossed(rest, "zl", 2)], axis=0)
        if layer == layers - 1:
            squares, earlier = lax.optimization_barrier((squares, earlier))
        normed = values * lax.rsqrt(squares / total_channels + 1e-06)[:, None]
        stored = normed.astype(jnp.bfloat16)
        conv = jnp.zeros((row_count, values.shape[1]), jnp.float32)
        for k in range(n_taps):
            window = lax.dynamic_slice_in_dim(stored, REACH - offsets[layer, k], row_count, 0)
            conv = conv + coeffs[layer, k] * window.astype(jnp.float32)
        gated = (conv * jax.nn.silu(normed[REACH:])).astype(jnp.bfloat16)
        halves = [
            jnp.concatenate([gated[:, z * width + i * half : z * width + (i + 1) * half] for z in range(n_zh)], axis=1)
            for i in range(n_c)
        ]
        mine = jnp.where(c == 0, halves[0], halves[1])
        its = jnp.where(c == 0, halves[1], halves[0])
        partial = jnp.einsum("tk,xkn->xtn", mine, own, preferred_element_type=jnp.float32)
        partial = partial + jnp.einsum("tk,xkn->xtn", its, other, preferred_element_type=jnp.float32)
        partial = partial.astype(jnp.bfloat16)[entry_of]
        terms = lax.all_to_all(partial, "x", split_axis=0, concat_axis=0)
        mixed = jnp.sum(terms.astype(jnp.float32), axis=0)
        hidden = (hidden.astype(jnp.float32) + mixed).astype(jnp.bfloat16)
        if layer == 0:
            hidden, rest = lax.optimization_barrier((hidden, rest))
            rest = jnp.concatenate([rest, crossed(rest, "zl", 1)], axis=0)
        results.append(hidden)
    last = lax.ppermute(results[-1], TURNED, back)
    return jnp.concatenate([earlier, last[None]], axis=0)


def solution(mesh):
    fine = Mesh(mesh.devices.reshape(4, 8, 2, 4, 4), ("y", "zl", "c", "x", "zh"))
    dp = ("x", "zh")
    in_specs = (P(SECTION, dp), P(None, dp, None), P(None, None, dp), P())
    out_specs = P(None, SECTION, dp)
    return jax.shard_map(body, mesh=fine, in_specs=in_specs, out_specs=out_specs, check_vma=False)
```

time: 451 us -> 435 us (0.965)
  the two profiles are of different devices: /device:TPU:8 before, /device:TPU:88 now
where the time goes in v3:
time: 435 us; the launch traced here: 434 us
  waiting for transfers between devices  168 us (39%)
  blocking collectives  159 us (37%)
  starting transfers between devices  61.4 us (14%)
  between operations  15.1 us (3%)
  local copies, waits for them, and re-layouts  13.9 us (3%)
  other arithmetic  12.3 us (3%)
    ppermute x3, waiting for transfers between devices, body(): before = lax.ppermute(wide[row_count - REACH:], PLACE, forward)  138 us
    all_gather x1, blocking collectives, body(): got = lax.all_gather(sent, 'zh', axis=0)  67.5 us
    all_gather x3, blocking collectives, body(): wide = lax.all_gather(hidden, 'y', axis=1, tiled=True)  41.1 us
    psum x3, blocking collectives, body(): squares = lax.psum(jnp.sum(values * values, axis=-1), 'x')  27.4 us
    all_to_all x2, blocking collectives, body(): terms = lax.all_to_all(partial, 'x', split_axis=0, concat_axis=0)  23.3 us
    ppermute x1, starting transfers between devices, body(): hidden = lax.ppermute(signal, TURNED, there)  22 us
    ppermute x1, waiting for transfers between devices, body(): last = lax.ppermute(results[-1], TURNED, back)  20.6 us
    ppermute x7, starting transfers between devices, crossed(): lax.ppermute(value, axis, [(i, i ^ bit) for i in range(lax.axis_size(axis...  19.7 us
  transfers between devices with their start and end apart: 14, of which 7 were waited for; matrix products, arithmetic and copies ran while one was open for 4% of the time, Pallas kernels for 0%

profile of v3, /device:TPU:88, one launch (start us, length us, event | category | flops | bytes accessed | tf_op | source)
XLA Modules:
  0.0 433.9 jit_solution(4870778331928522843)
XLA Ops:
  0.0 1.0 copy.9
  1.0 22.0 %collective-permute-start = (bf16[256,256]{0,1:T(8,128)(2,1)S(1)}, bf16[256,256]{0,1:T(8,128)(2,1)S(1)}, u32[]{:S(2)}, u32[]{:S(2)}) collective-permute-start(bf16[256,256]{0,1:T(8,128)(2,1)S(1)} %copy.9), channel_id=1, source_target_pairs={{0,0},{1,256},{2,512},{3,768},{32,32},{33,288},{34,544},{35,800},{... | collective-permute-start | bytes 393224 | tf_op jit(solution)/shard_map/ppermute | solution.py:52
  23.1 1.8 fusion.48
  29.6 0.7 reduce-precision_convert_fusion
  30.5 0.9 constant_dynamic-slice_fusion
  31.5 67.5 %all-gather = bf16[1664,256]{1,0:T(8,128)(2,1)S(1)} all-gather(bf16[416,256]{1,0:T(8,128)(2,1)S(1)} %maximum_maximum_fusion), channel_id=2, replica_groups=mesh['y'=4,'zl'=8,'c'=2,'x'=4,'zh'=4] {'zh'}, dimensions={0}, use_global_device_ids=true | all-gather | bytes 1064960 | tf_op jit(solution)/shard_map/all_gather | solution.py:69
  99.0 0.6 gather_fusion
  99.7 0.1 copy.26
  99.9 1.9 collective-permute-start.1
  101.8 13.5 %all_gather.17 = bf16[256,1024]{0,1:T(8,128)(2,1)S(1)} all-gather(bf16[256,256]{0,1:T(8,128)(2,1)S(1)} %collective-permute-done), channel_id=1, replica_groups=mesh['y'=4,'zl'=8,'c'=2,'x'=4,'zh'=4] {'y'}, dimensions={1}, use_global_device_ids=true | all-gather | bytes 655360 | tf_op jit(solution)/shard_map/all_gather | solution.py:86
  115.4 4.8 %collective-permute-start.3 = (bf16[2,1,512,256]{2,3,0,1:T(8,128)(2,1)S(1)}, bf16[2,1,512,256]{2,3,0,1:T(8,128)(2,1)}, u32[]{:S(2)}, u32[]{:S(2)}) collective-permute-start(bf16[2,1,512,256]{2,3,0,1:T(8,128)(2,1)S(1)} %pad_maximum_fusion.5), channel_id=1, source_target_pairs={{0,32},{32,0},{64,96},{96,64},{128,160},{160,128},{192,224},{224,1... | collective-permute-start | bytes 1572872 | tf_op jit(solution)/shard_map/ppermute | solution.py:35
  120.4 0.3 copy.11
  120.7 0.2 reshape.118
  121.0 1.9 collective-permute-start.2
  123.0 15.5 %collective-permute-done.2 = bf16[64,1024]{0,1:T(8,128)(2,1)S(1)} collective-permute-done((bf16[64,1024]{0,1:T(8,128)(2,1)S(1)}, bf16[64,1024]{0,1:T(8,128)(2,1)S(1)}, u32[]{:S(2)}, u32[]{:S(2)}) %collective-permute-start.2) | collective-permute-done | bytes 131104 | tf_op jit(solution)/shard_map/ppermute | solution.py:93
  138.6 0.4 fusion
  139.0 10.5 %psum.21 = f32[320]{0:T(512)S(1)} all-reduce(f32[320]{0:T(512)S(1)} %fusion), channel_id=1, replica_groups=mesh['y'=4,'zl'=8,'c'=2,'x'=4,'zh'=4] {'x'}, use_global_device_ids=true, to_apply=%region_1.2 | all-reduce | flops 320 | bytes 2560 | tf_op jit(solution)/shard_map/psum | solution.py:95
  149.5 1.1 pad_maximum_fusion
  150.6 1.9 collective-permute-start.5
  152.6 1.9 collective-permute-start.4
  154.5 0.4 fusion.31
  154.9 1.8 multiply_convert_fusion.2
  156.8 0.5 fusion.16
  157.3 0.5 fusion.8
  157.8 1.4 gather_fusion.1
  159.2 3.5 all-to-all-start
  162.7 8.9 %collective-permute-done.5 = bf16[1,2,512,256]{2,3,0,1:T(8,128)(2,1)S(1)} collective-permute-done((bf16[1,2,512,256]{2,3,0,1:T(8,128)(2,1)S(1)}, bf16[1,2,512,256]{2,3,0,1:T(8,128)(2,1)S(1)}, u32[]{:S(2)}, u32[]{:S(2)}) %collective-permute-start.5) | collective-permute-done | bytes 524320 | tf_op jit(solution)/shard_map/ppermute | solution.py:35
  171.5 1.1 pad_maximum_fusion.1
  172.6 0.4 all-to-all-done
  173.1 5.3 %collective-permute-start.6 = (bf16[2,2,512,256]{2,3,0,1:T(8,128)(2,1)}, bf16[2,2,512,256]{2,3,0,1:T(8,128)(2,1)}, u32[]{:S(2)}, u32[]{:S(2)}) collective-permute-start(bf16[2,2,512,256]{2,3,0,1:T(8,128)(2,1)} %pad_maximum_fusion.1), channel_id=1, source_target_pairs={{0,32},{32,0},{64,96},{96,64},{128,160},{160,128},{192,224},{224,1... | collective-permute-start | bytes 3145736 | tf_op jit(solution)/shard_map/ppermute | solution.py:35
  183.4 12.8 %all_gather.18 = bf16[256,1024]{0,1:T(8,128)(2,1)S(1)} all-gather(bf16[256,256]{0,1:T(8,128)(2,1)S(1)} %add_convert_fusion.2), channel_id=1, replica_groups=mesh['y'=4,'zl'=8,'c'=2,'x'=4,'zh'=4] {'y'}, dimensions={1}, use_global_device_ids=true | all-gather | bytes 655360 | tf_op jit(solution)/shard_map/all_gather | solution.py:86
  196.4 1.9 collective-permute-start.7
  198.3 1.3 constant_dynamic-update-slice_fusion.1
  199.6 14.2 %collective-permute-done.7 = bf16[64,1024]{0,1:T(8,128)(2,1)S(1)} collective-permute-done((bf16[64,1024]{0,1:T(8,128)(2,1)S(1)}, bf16[64,1024]{0,1:T(8,128)(2,1)S(1)}, u32[]{:S(2)}, u32[]{:S(2)}) %collective-permute-start.7) | collective-permute-done | bytes 131104 | tf_op jit(solution)/shard_map/ppermute | solution.py:93
  213.8 0.4 fusion.1
  214.3 7.9 %psum.22 = f32[320]{0:T(512)S(1)} all-reduce(f32[320]{0:T(512)S(1)} %fusion.1), channel_id=1, replica_groups=mesh['y'=4,'zl'=8,'c'=2,'x'=4,'zh'=4] {'x'}, use_global_device_ids=true, to_apply=%region_4.5 | all-reduce | flops 320 | bytes 2560 | tf_op jit(solution)/shard_map/psum | solution.py:95
  222.1 1.3 constant_dynamic-update-slice_fusion
  223.4 1.2 slice_bitcast_fusion.1
  224.6 1.9 collective-permute-start.8
  226.6 0.4 fusion.32
  227.0 1.8 multiply_convert_fusion.1
  228.9 0.3 collective-permute-done.8
  229.2 0.5 fusion.12
  229.6 0.5 fusion.7
  230.1 0.6 gather_fusion.2
  230.7 12.8 %all_to_all.15 = bf16[4,256,256]{1,2,0:T(8,128)(2,1)S(1)} all-to-all(bf16[4,256,256]{1,2,0:T(8,128)(2,1)S(1)} %gather_fusion.2), channel_id=1, replica_groups=mesh['y'=4,'zl'=8,'c'=2,'x'=4,'zh'=4] {'x'}, dimensions={0} | all-to-all | bytes 1048576 | tf_op jit(solution)/shard_map/all_to_all | solution.py:119
  243.6 0.8 pad_maximum_fusion.11
  244.4 8.6 %collective-permute-start.10 = (bf16[2,256,256]{1,2,0:T(8,128)(2,1)}, bf16[2,256,256]{1,2,0:T(8,128)(2,1)S(1)}, u32[]{:S(2)}, u32[]{:S(2)}) collective-permute-start(bf16[2,256,256]{1,2,0:T(8,128)(2,1)} %pad_maximum_fusion.11), channel_id=1, source_target_pairs={{0,0},{256,1},{512,2},{768,3},{32,32},{288,33},{544,34},{800,35},{... | collective-permute-start | bytes 786440 | tf_op jit(solution)/shard_map/ppermute | solution.py:85
  252.9 14.8 %all_gather.19 = bf16[256,1024]{0,1:T(8,128)(2,1)S(1)} all-gather(bf16[256,256]{0,1:T(8,128)(2,1)S(1)} %add_convert_fusion.1), channel_id=1, replica_groups=mesh['y'=4,'zl'=8,'c'=2,'x'=4,'zh'=4] {'y'}, dimensions={1}, use_global_device_ids=true | all-gather | bytes 655360 | tf_op jit(solution)/shard_map/all_gather | solution.py:86
  267.7 0.8 slice.288
  268.6 1.9 collective-permute-start.9
  275.4 1.9 collective-permute-start.11
  277.3 108.0 %collective-permute-done.9 = bf16[64,1024]{0,1:T(8,128)(2,1)S(1)} collective-permute-done((bf16[64,1024]{0,1:T(8,128)(2,1)}, bf16[64,1024]{0,1:T(8,128)(2,1)S(1)}, u32[]{:S(2)}, u32[]{:S(2)}) %collective-permute-start.9) | collective-permute-done | bytes 131104 | tf_op jit(solution)/shard_map/ppermute | solution.py:93
  385.3 0.4 fusion.2
  385.7 9.1 %psum.23 = f32[320]{0:T(512)S(1)} all-reduce(f32[320]{0:T(512)S(1)} %fusion.2), channel_id=1, replica_groups=mesh['y'=4,'zl'=8,'c'=2,'x'=4,'zh'=4] {'x'}, use_global_device_ids=true, to_apply=%region_7.8 | all-reduce | flops 320 | bytes 2560 | tf_op jit(solution)/shard_map/psum | solution.py:95
  394.8 0.4 fusion.33
  395.2 1.8 multiply_convert_fusion
  397.1 1.7 fusion.9
  398.8 0.5 fusion.6
  399.3 0.6 gather_fusion.3
  399.8 10.5 %all_to_all.16 = bf16[4,256,256]{1,2,0:T(8,128)(2,1)S(1)} all-to-all(bf16[4,256,256]{1,2,0:T(8,128)(2,1)S(1)} %gather_fusion.3), channel_id=1, replica_groups=mesh['y'=4,'zl'=8,'c'=2,'x'=4,'zh'=4] {'x'}, dimensions={0} | all-to-all | bytes 1048576 | tf_op jit(solution)/shard_map/all_to_all | solution.py:119
  410.4 1.9 collective-permute-start.12
  412.4 20.6 %collective-permute-done.12 = bf16[256,256]{0,1:T(8,128)(2,1)S(1)} collective-permute-done((bf16[256,256]{0,1:T(8,128)(2,1)S(1)}, bf16[256,256]{0,1:T(8,128)(2,1)S(1)}, u32[]{:S(2)}, u32[]{:S(2)}) %collective-permute-start.12) | collective-permute-done | bytes 131104 | tf_op jit(solution)/shard_map/ppermute | solution.py:126
  433.0 0.9 copy.19
  (42 shorter events, 1.3 us)
Async XLA Ops:
  0.0 99.0 %copy-start = (s32[4]{0:T(128)S(1)}, s32[4]{0:T(128)}, u32[]{:S(2)}) copy-start(s32[4]{0:T(128)} %constant.98.clone) | copy-start | bytes 52
  1.0 98.6 %collective-permute-start = (bf16[256,256]{0,1:T(8,128)(2,1)S(1)}, bf16[256,256]{0,1:T(8,128)(2,1)S(1)}, u32[]{:S(2)}, u32[]{:S(2)}) collective-permute-start(bf16[256,256]{0,1:T(8,128)(2,1)S(1)} %copy.9), channel_id=1, source_target_pairs={{0,0},{1,256},{2,512},{3,768},{32,32},{33,288},{34,544},{35,800},{... | collective-permute-start | bytes 393224 | tf_op jit(solution)/shard_map/ppermute | solution.py:52
  99.9 15.5 %collective-permute-start.1 = (bf16[1,1,512,256]{2,3,0,1:T(8,128)(2,1)S(1)}, bf16[1,1,512,256]{2,3,0,1:T(8,128)(2,1)S(1)}, u32[]{:S(2)}, u32[]{:S(2)}) collective-permute-start(bf16[1,1,512,256]{2,3,0,1:T(8,128)(2,1)S(1)} %copy.26), channel_id=1, source_target_pairs={{0,64},{32,96},{64,0},{96,32},{128,192},{160,224},{192,128},{224,1... | collective-permute-start | bytes 786440 | tf_op jit(solution)/shard_map/ppermute | solution.py:35
  115.4 34.1 %collective-permute-start.3 = (bf16[2,1,512,256]{2,3,0,1:T(8,128)(2,1)S(1)}, bf16[2,1,512,256]{2,3,0,1:T(8,128)(2,1)}, u32[]{:S(2)}, u32[]{:S(2)}) collective-permute-start(bf16[2,1,512,256]{2,3,0,1:T(8,128)(2,1)S(1)} %pad_maximum_fusion.5), channel_id=1, source_target_pairs={{0,32},{32,0},{64,96},{96,64},{128,160},{160,128},{192,224},{224,1... | collective-permute-start | bytes 1572872 | tf_op jit(solution)/shard_map/ppermute | solution.py:35
  121.0 17.5 %collective-permute-start.2 = (bf16[64,1024]{0,1:T(8,128)(2,1)S(1)}, bf16[64,1024]{0,1:T(8,128)(2,1)S(1)}, u32[]{:S(2)}, u32[]{:S(2)}) collective-permute-start(bf16[64,1024]{0,1:T(8,128)(2,1)S(1)} %slice.188), channel_id=1, source_target_pairs={{0,16},{16,32},{32,48},{48,1},{1,17},{17,33},{33,49},{49,2},{2,18}... | collective-permute-start | bytes 393224 | tf_op jit(solution)/shard_map/ppermute | solution.py:93
  150.6 20.9 %collective-permute-start.5 = (bf16[1,2,512,256]{2,3,0,1:T(8,128)(2,1)S(1)}, bf16[1,2,512,256]{2,3,0,1:T(8,128)(2,1)S(1)}, u32[]{:S(2)}, u32[]{:S(2)}) collective-permute-start(bf16[1,2,512,256]{2,3,0,1:T(8,128)(2,1)S(1)} %reshape.118), channel_id=1, source_target_pairs={{0,64},{32,96},{64,0},{96,32},{128,192},{160,224},{192,128},{224,1... | collective-permute-start | bytes 1572872 | tf_op jit(solution)/shard_map/ppermute | solution.py:35
  152.6 4.7 %collective-permute-start.4 = (bf16[4,512,256]{1,2,0:T(8,128)(2,1)S(1)}, bf16[4,512,256]{1,2,0:T(8,128)(2,1)S(1)}, u32[]{:S(2)}, u32[]{:S(2)}) collective-permute-start(bf16[4,512,256]{1,2,0:T(8,128)(2,1)S(1)} %bitcast.97), channel_id=1, source_target_pairs={{0,16},{16,0},{1,17},{17,1},{2,18},{18,2},{3,19},{19,3},{4,20},{20... | collective-permute-start | bytes 3145736 | tf_op jit(solution)/shard_map/ppermute | solution.py:35
  159.2 13.9 %all-to-all-start = ((bf16[4,256,256]{1,2,0:T(8,128)(2,1)}), bf16[4,256,256]{1,2,0:T(8,128)(2,1)S(1)}, u32[]{:S(2)}, u32[]{:S(2)}) async-start(bf16[4,256,256]{1,2,0:T(8,128)(2,1)} %gather_fusion.1), calls=%async_computation | async-start | bytes 1048576 | tf_op jit(solution)/shard_map/all_to_all | solution.py:119
  173.1 49.0 %collective-permute-start.6 = (bf16[2,2,512,256]{2,3,0,1:T(8,128)(2,1)}, bf16[2,2,512,256]{2,3,0,1:T(8,128)(2,1)}, u32[]{:S(2)}, u32[]{:S(2)}) collective-permute-start(bf16[2,2,512,256]{2,3,0,1:T(8,128)(2,1)} %pad_maximum_fusion.1), channel_id=1, source_target_pairs={{0,32},{32,0},{64,96},{96,64},{128,160},{160,128},{192,224},{224,1... | collective-permute-start | bytes 3145736 | tf_op jit(solution)/shard_map/ppermute | solution.py:35
  196.4 17.5 %collective-permute-start.7 = (bf16[64,1024]{0,1:T(8,128)(2,1)S(1)}, bf16[64,1024]{0,1:T(8,128)(2,1)S(1)}, u32[]{:S(2)}, u32[]{:S(2)}) collective-permute-start(bf16[64,1024]{0,1:T(8,128)(2,1)S(1)} %slice.275), channel_id=1, source_target_pairs={{0,16},{16,32},{32,48},{48,1},{1,17},{17,33},{33,49},{49,2},{2,18}... | collective-permute-start | bytes 393224 | tf_op jit(solution)/shard_map/ppermute | solution.py:93
  224.6 4.5 %collective-permute-start.8 = (bf16[4,512,256]{1,2,0:T(8,128)(2,1)S(1)}, bf16[4,512,256]{1,2,0:T(8,128)(2,1)S(1)}, u32[]{:S(2)}, u32[]{:S(2)}) collective-permute-start(bf16[4,512,256]{1,2,0:T(8,128)(2,1)S(1)} %get-tuple-element.27), channel_id=1, source_target_pairs={{0,16},{16,0},{1,17},{17,1},{2,18},{18,2},{3,19},{19,3},{4,20},{20... | collective-permute-start | bytes 3145736 | tf_op jit(solution)/shard_map/ppermute | solution.py:35
  244.4 150.4 %collective-permute-start.10 = (bf16[2,256,256]{1,2,0:T(8,128)(2,1)}, bf16[2,256,256]{1,2,0:T(8,128)(2,1)S(1)}, u32[]{:S(2)}, u32[]{:S(2)}) collective-permute-start(bf16[2,256,256]{1,2,0:T(8,128)(2,1)} %pad_maximum_fusion.11), channel_id=1, source_target_pairs={{0,0},{256,1},{512,2},{768,3},{32,32},{288,33},{544,34},{800,35},{... | collective-permute-start | bytes 786440 | tf_op jit(solution)/shard_map/ppermute | solution.py:85
  268.6 116.7 %collective-permute-start.9 = (bf16[64,1024]{0,1:T(8,128)(2,1)}, bf16[64,1024]{0,1:T(8,128)(2,1)S(1)}, u32[]{:S(2)}, u32[]{:S(2)}) collective-permute-start(bf16[64,1024]{0,1:T(8,128)(2,1)} %slice.288), channel_id=1, source_target_pairs={{0,16},{16,32},{32,48},{48,1},{1,17},{17,33},{33,49},{49,2},{2,18}... | collective-permute-start | bytes 393224 | tf_op jit(solution)/shard_map/ppermute | solution.py:93
  275.4 121.7 %collective-permute-start.11 = (bf16[4,512,256]{1,2,0:T(8,128)(2,1)}, bf16[4,512,256]{1,2,0:T(8,128)(2,1)}, u32[]{:S(2)}, u32[]{:S(2)}) collective-permute-start(bf16[4,512,256]{1,2,0:T(8,128)(2,1)} %get-tuple-element.30), channel_id=1, source_target_pairs={{0,16},{16,0},{1,17},{17,1},{2,18},{18,2},{3,19},{19,3},{4,20},{20... | collective-permute-start | bytes 3145736 | tf_op jit(solution)/shard_map/ppermute | solution.py:35
  410.4 22.5 %collective-permute-start.12 = (bf16[256,256]{0,1:T(8,128)(2,1)S(1)}, bf16[256,256]{0,1:T(8,128)(2,1)S(1)}, u32[]{:S(2)}, u32[]{:S(2)}) collective-permute-start(bf16[256,256]{0,1:T(8,128)(2,1)S(1)} %add_convert_fusion), channel_id=1, source_target_pairs={{0,0},{256,1},{512,2},{768,3},{32,32},{288,33},{544,34},{800,35},{... | collective-permute-start | bytes 393224 | tf_op jit(solution)/shard_map/ppermute | solution.py:126

commit v4 on v3

v4 whole, which is shorter than its diff:
```python
import jax
import jax.numpy as jnp
from jax import lax
from jax.sharding import Mesh, PartitionSpec as P

REACH = 64
SECTION = ("y", "zl", "c")
TURNED = ("y", "zl", "zh")
PLACE = ("zl", "c", "zh")


def turn_pairs(n_y, n_zl, n_zh):
    pairs = []
    for y in range(n_y):
        for zl in range(n_zl):
            for zh in range(n_zh):
                q, r = divmod(zl, 2)
                source = (y * n_zl + zl) * n_zh + zh
                target = ((zh + y) % n_y * n_zl + y + n_y * r) * n_zh + q
                pairs.append((source, target))
    return pairs


def halo_pairs(n_y, n_zl, n_c, n_zh):
    places = []
    for y in range(n_y):
        for zl in range(n_zl):
            for c in range(n_c):
                q, r = divmod(zl, 2)
                places.append(((y + n_y * r) * n_c + c) * n_zh + q)
    return list(zip(places[:-1], places[1:]))


def swap_pairs(n_y, n_zl, bit):
    pairs = []
    for y in range(n_y):
        for zl in range(n_zl):
            other = zl ^ bit
            pairs.append((y * n_zl + zl, (y + other - zl) % n_y * n_zl + other))
    return pairs


def split_rows(gated, rotation, c, n_zh, n_c):
    half = gated.shape[1] // (n_zh * n_c)
    choices = []
    for turn in range(n_zh):
        for i in range(n_c):
            starts = [((z + turn) % n_zh * n_c + i) * half for z in range(n_zh)]
            choices.append(jnp.concatenate([gated[:, start : start + half] for start in starts], axis=1))
    swapped = [choices[k ^ 1] for k in range(len(choices))]
    which = rotation * n_c + c
    return lax.select_n(which, *choices), lax.select_n(which, *swapped)


def after(value, *others):
    return lax.optimization_barrier((value, *others))[0]


def body(signal, mixing, taps, offsets):
    row_count, width = signal.shape
    layers, n_taps = taps.shape[:2]
    n_x, n_y, n_zl, n_c, n_zh = (lax.axis_size(a) for a in ("x", "y", "zl", "c", "zh"))
    y, zl, c = lax.axis_index("y"), lax.axis_index("zl"), lax.axis_index("c")
    total_channels = n_x * n_zh * width
    there = turn_pairs(n_y, n_zl, n_zh)
    back = [(target, source) for source, target in there]
    forward = halo_pairs(n_y, n_zl, n_c, n_zh)

    hidden = lax.ppermute(signal, TURNED, there)

    low_bits = zl % n_y
    block = (y - low_bits) % n_y
    half = width // n_c
    share = lax.dynamic_slice(mixing, (0, c * half, (low_bits * n_zh + block) * width), (layers, half, width))
    high = lax.reduce_precision(taps, 8, 7)
    low = (taps - high).astype(jnp.bfloat16)
    n_tap_rows = layers * n_taps
    sent = jnp.concatenate(
        [
            share.reshape(layers * half, width),
            high.astype(jnp.bfloat16).reshape(n_tap_rows, width),
            low.reshape(n_tap_rows, width),
            jnp.zeros((-2 * n_tap_rows % 16, width), jnp.bfloat16),
        ],
        axis=0,
    )
    got = lax.all_gather(sent, "zh", axis=0)
    hidden, got = lax.optimization_barrier((hidden, got))
    coeffs = got[:, layers * half :][(jnp.arange(n_zh) - low_bits) % n_zh].astype(jnp.float32)
    coeffs = coeffs[:, :n_tap_rows] + coeffs[:, n_tap_rows : 2 * n_tap_rows]
    coeffs = coeffs.transpose(1, 0, 2).reshape(layers, n_taps, n_zh * width)
    shares = got[:, : layers * half].reshape(n_zh, layers, half, width).transpose(1, 0, 2, 3)
    first = shares[:1].reshape(1, 1, n_zh * half, width)
    rest = shares[1:].reshape(1, layers - 1, n_zh * half, width)

    swap1, swap2 = swap_pairs(n_y, n_zl, 1), swap_pairs(n_y, n_zl, 2)
    first = jnp.concatenate([first, lax.ppermute(first, ("y", "zl"), swap2)], axis=0)
    order = jnp.array([0, 2, 1, 3])
    entry_of = order[jnp.arange(n_x) ^ low_bits]
    new_y = (lax.axis_index("zh") == 0) & (zl < n_y) & (c == 0)
    returned = []
    own = other = None
    for layer in range(layers):
        wide = lax.all_gather(hidden, "y", axis=1, tiled=True)
        if layer == 0:
            wide, first = lax.optimization_barrier((wide, first))
            first = jnp.concatenate([first, lax.ppermute(first, ("y", "zl"), swap1)], axis=0)
        else:
            own = rest[:, layer - 1]
            other = lax.ppermute(after(own, wide), "c", [(0, 1), (1, 0)])
        before = lax.ppermute(wide[row_count - REACH :], PLACE, forward)
        before = jnp.where(new_y, jnp.roll(before, width, axis=1), before)
        values = jnp.concatenate([before, wide], axis=0).astype(jnp.float32)
        squares = lax.psum(jnp.sum(values * values, axis=-1), "x")
        if layer == 0:
            squares, first, rest = lax.optimization_barrier((squares, first, rest))
            own = first[:, 0]
            other = lax.ppermute(own, "c", [(0, 1), (1, 0)])
            rest = jnp.concatenate([rest, lax.ppermute(rest, ("y", "zl"), swap2)], axis=0)
        normed = values * lax.rsqrt(squares / total_channels + 1e-06)[:, None]
        stored = normed.astype(jnp.bfloat16)
        conv = jnp.zeros((row_count, values.shape[1]), jnp.float32)
        for k in range(n_taps):
            window = lax.dynamic_slice_in_dim(stored, REACH - offsets[layer, k], row_count, 0)
            conv = conv + coeffs[layer, k] * window.astype(jnp.float32)
        gated = (conv * jax.nn.silu(normed[REACH:])).astype(jnp.bfloat16)
        mine, its = split_rows(gated, low_bits, c, n_zh, n_c)
        partial = jnp.einsum("tk,xkn->xtn", mine, own, preferred_element_type=jnp.float32)
        partial = partial + jnp.einsum("tk,xkn->xtn", its, other, preferred_element_type=jnp.float32)
        partial = partial.astype(jnp.bfloat16)[entry_of]
        if layer > 0:
            returned.append(lax.ppermute(hidden, TURNED, back))
            partial, returned[-1] = lax.optimization_barrier((partial, returned[-1]))
        terms = lax.all_to_all(partial, "x", split_axis=0, concat_axis=0)
        mixed = jnp.sum(terms.astype(jnp.float32), axis=0)
        hidden = (hidden.astype(jnp.float32) + mixed).astype(jnp.bfloat16)
        if layer == 0:
            hidden, rest = lax.optimization_barrier((hidden, rest))
            rest = jnp.concatenate([rest, lax.ppermute(rest, ("y", "zl"), swap1)], axis=0)
    returned.append(lax.ppermute(hidden, TURNED, back))
    return jnp.stack(returned)


def solution(mesh):
    fine = Mesh(mesh.devices.reshape(4, 8, 2, 4, 4), ("y", "zl", "c", "x", "zh"))
    dp = ("x", "zh")
    in_specs = (P(SECTION, dp), P(None, dp, None), P(None, None, dp), P())
    out_specs = P(None, SECTION, dp)
    return jax.shard_map(body, mesh=fine, in_specs=in_specs, out_specs=out_specs, check_vma=False)
```

time: 435 us -> 383 us (0.88)
  the two profiles are of different devices: /device:TPU:88 before, /device:TPU:128 now
where the time goes in v4:
time: 383 us; the launch traced here: 382 us
  blocking collectives  192 us (50%)
  waiting for transfers between devices  80.9 us (21%)
  starting transfers between devices  63 us (16%)
  between operations  15.6 us (4%)
  local copies, waits for them, and re-layouts  13.5 us (4%)
  other arithmetic  11.8 us (3%)
  matrix products  5.03 us (1%)
    all_gather x3, blocking collectives, body(): wide = lax.all_gather(hidden, 'y', axis=1, tiled=True)  76.2 us
    all_gather x1, blocking collectives, body(): got = lax.all_gather(sent, 'zh', axis=0)  62.2 us
    ppermute x3, waiting for transfers between devices, body(): before = lax.ppermute(wide[row_count - REACH:], PLACE, forward)  39.3 us
    ppermute x3, waiting for transfers between devices, body(): returned.append(lax.ppermute(hidden, TURNED, back))  32 us
    psum x3, blocking collectives, body(): squares = lax.psum(jnp.sum(values * values, axis=-1), 'x')  28.3 us
    all_to_all x2, blocking collectives, body(): terms = lax.all_to_all(partial, 'x', split_axis=0, concat_axis=0)  25.7 us
    ppermute x1, starting transfers between devices, body(): hidden = lax.ppermute(signal, TURNED, there)  22.3 us
    ppermute x3, starting transfers between devices, body(): returned.append(lax.ppermute(hidden, TURNED, back))  13 us
  transfers between devices with their start and end apart: 15, of which 8 were waited for; matrix products, arithmetic and copies ran while one was open for 7% of the time, Pallas kernels for 0%

profile of v4, /device:TPU:128, one launch (start us, length us, event | category | flops | bytes accessed | tf_op | source)
XLA Modules:
  0.0 382.3 jit_solution(9893305880445008683)
XLA Ops:
  0.0 1.0 copy.9
  1.0 22.3 %collective-permute-start = (bf16[256,256]{0,1:T(8,128)(2,1)S(1)}, bf16[256,256]{0,1:T(8,128)(2,1)S(1)}, u32[]{:S(2)}, u32[]{:S(2)}) collective-permute-start(bf16[256,256]{0,1:T(8,128)(2,1)S(1)} %copy.9), channel_id=1, source_target_pairs={{0,0},{1,256},{2,512},{3,768},{32,128},{33,384},{34,640},{35,896},... | collective-permute-start | bytes 393224 | tf_op jit(solution)/shard_map/ppermute | solution.py:69
  23.5 1.3 gather_fusion.1
  24.8 0.7 reduce-precision_convert_fusion
  25.6 0.9 constant_dynamic-slice_fusion
  26.7 62.2 %all-gather = bf16[1664,256]{1,0:T(8,128)(2,1)S(1)} all-gather(bf16[416,256]{1,0:T(8,128)(2,1)S(1)} %maximum_maximum_fusion), channel_id=2, replica_groups=mesh['y'=4,'zl'=8,'c'=2,'x'=4,'zh'=4] {'zh'}, dimensions={0}, use_global_device_ids=true | all-gather | bytes 1064960 | tf_op jit(solution)/shard_map/all_gather | solution.py:87
  88.9 0.7 fusion.122
  94.9 1.9 collective-permute-start.1
  96.9 0.6 gather_fusion
  97.5 30.1 %all_gather.17 = bf16[256,1024]{0,1:T(8,128)(2,1)S(1)} all-gather(bf16[256,256]{0,1:T(8,128)(2,1)S(1)} %collective-permute-done), channel_id=1, replica_groups=mesh['y'=4,'zl'=8,'c'=2,'x'=4,'zh'=4] {'y'}, dimensions={1}, use_global_device_ids=true | all-gather | bytes 655360 | tf_op jit(solution)/shard_map/all_gather | solution.py:104
  127.6 4.8 %collective-permute-start.3 = (bf16[2,1,512,256]{2,3,0,1:T(8,128)(2,1)S(1)}, bf16[2,1,512,256]{2,3,0,1:T(8,128)(2,1)S(1)}, u32[]{:S(2)}, u32[]{:S(2)}) collective-permute-start(bf16[2,1,512,256]{2,3,0,1:T(8,128)(2,1)S(1)} %pad_maximum_fusion.5), channel_id=1, source_target_pairs={{0,288},{32,768},{64,352},{96,832},{128,416},{160,896},{192,480},{... | collective-permute-start | bytes 1572872 | tf_op jit(solution)/shard_map/ppermute | solution.py:107
  132.6 0.3 copy.11
  132.9 0.2 reshape.167
  133.3 1.9 collective-permute-start.2
  135.2 22.9 %collective-permute-done.2 = bf16[64,1024]{0,1:T(8,128)(2,1)S(1)} collective-permute-done((bf16[64,1024]{0,1:T(8,128)(2,1)S(1)}, bf16[64,1024]{0,1:T(8,128)(2,1)S(1)}, u32[]{:S(2)}, u32[]{:S(2)}) %collective-permute-start.2) | collective-permute-done | bytes 131104 | tf_op jit(solution)/shard_map/ppermute | solution.py:111
  158.2 0.4 fusion
  158.7 10.5 %psum.21 = f32[320]{0:T(512)S(1)} all-reduce(f32[320]{0:T(512)S(1)} %fusion), channel_id=1, replica_groups=mesh['y'=4,'zl'=8,'c'=2,'x'=4,'zh'=4] {'x'}, use_global_device_ids=true, to_apply=%region_1.2 | all-reduce | flops 320 | bytes 2560 | tf_op jit(solution)/shard_map/psum | solution.py:114
  169.3 3.0 collective-permute-start.5
  172.2 1.9 collective-permute-start.4
  174.2 0.4 fusion.103
  174.6 1.9 multiply_convert_fusion.2
  176.5 0.7 fusion.16
  177.2 0.6 fusion.8
  177.8 1.4 gather_fusion.2
  179.2 3.5 all-to-all-start
  182.7 3.4 collective-permute-done.5
  186.1 1.1 pad_maximum_fusion.1
  187.2 5.9 %all-to-all-done = bf16[4,256,256]{1,2,0:T(8,128)(2,1)S(1)} async-done(((bf16[4,256,256]{1,2,0:T(8,128)(2,1)}), bf16[4,256,256]{1,2,0:T(8,128)(2,1)S(1)}, u32[]{:S(2)}, u32[]{:S(2)}) %all-to-all-start) | async-done | bytes 524320 | tf_op jit(solution)/shard_map/all_to_all | solution.py:134
  193.2 1.9 collective-permute-start.6
  200.4 5.3 %collective-permute-start.9 = (bf16[256,256]{0,1:T(8,128)(2,1)S(1)}, bf16[256,256]{0,1:T(8,128)(2,1)S(1)}, u32[]{:S(2)}, u32[]{:S(2)}) collective-permute-start(bf16[256,256]{0,1:T(8,128)(2,1)S(1)} %add_convert_fusion.2), channel_id=1, source_target_pairs={{0,0},{256,1},{512,2},{768,3},{128,32},{384,33},{640,34},{896,35},... | collective-permute-start | bytes 393224 | tf_op jit(solution)/shard_map/ppermute | solution.py:132
  205.6 31.0 %all_gather.18 = bf16[256,1024]{0,1:T(8,128)(2,1)S(1)} all-gather(bf16[256,256]{0,1:T(8,128)(2,1)S(1)} %add_convert_fusion.2), channel_id=1, replica_groups=mesh['y'=4,'zl'=8,'c'=2,'x'=4,'zh'=4] {'y'}, dimensions={1}, use_global_device_ids=true | all-gather | bytes 655360 | tf_op jit(solution)/shard_map/all_gather | solution.py:104
  236.8 1.9 collective-permute-start.7
  238.7 1.3 constant_dynamic-update-slice_fusion.1
  240.0 12.0 %collective-permute-done.7 = bf16[64,1024]{0,1:T(8,128)(2,1)S(1)} collective-permute-done((bf16[64,1024]{0,1:T(8,128)(2,1)S(1)}, bf16[64,1024]{0,1:T(8,128)(2,1)S(1)}, u32[]{:S(2)}, u32[]{:S(2)}) %collective-permute-start.7) | collective-permute-done | bytes 131104 | tf_op jit(solution)/shard_map/ppermute | solution.py:111
  252.1 0.4 fusion.1
  252.5 8.9 %psum.22 = f32[320]{0:T(512)S(1)} all-reduce(f32[320]{0:T(512)S(1)} %fusion.1), channel_id=1, replica_groups=mesh['y'=4,'zl'=8,'c'=2,'x'=4,'zh'=4] {'x'}, use_global_device_ids=true, to_apply=%region_4.5 | all-reduce | flops 320 | bytes 2560 | tf_op jit(solution)/shard_map/psum | solution.py:114
  261.4 1.3 constant_dynamic-update-slice_fusion
  262.7 1.2 slice_bitcast_fusion.1
  263.9 1.9 collective-permute-start.8
  265.9 0.4 fusion.104
  266.3 1.9 multiply_convert_fusion.1
  268.2 0.2 collective-permute-done.8
  268.5 0.7 fusion.12
  269.1 0.6 fusion.7
  269.8 0.7 gather_fusion.3
  270.5 12.6 %all_to_all.15 = bf16[4,256,256]{1,2,0:T(8,128)(2,1)S(1)} all-to-all(bf16[4,256,256]{1,2,0:T(8,128)(2,1)S(1)} %gather_fusion.3), channel_id=1, replica_groups=mesh['y'=4,'zl'=8,'c'=2,'x'=4,'zh'=4] {'x'}, dimensions={0} | all-to-all | bytes 1048576 | tf_op jit(solution)/shard_map/all_to_all | solution.py:134
  283.2 15.1 %all_gather.19 = bf16[256,1024]{0,1:T(8,128)(2,1)S(1)} all-gather(bf16[256,256]{0,1:T(8,128)(2,1)S(1)} %add_convert_fusion.1), channel_id=1, replica_groups=mesh['y'=4,'zl'=8,'c'=2,'x'=4,'zh'=4] {'y'}, dimensions={1}, use_global_device_ids=true | all-gather | bytes 655360 | tf_op jit(solution)/shard_map/all_gather | solution.py:104
  298.4 1.9 collective-permute-start.10
  305.1 5.8 %collective-permute-start.12 = (bf16[256,256]{0,1:T(8,128)(2,1)S(1)}, bf16[256,256]{0,1:T(8,128)(2,1)}, u32[]{:S(2)}, u32[]{:S(2)}) collective-permute-start(bf16[256,256]{0,1:T(8,128)(2,1)S(1)} %add_convert_fusion.1), channel_id=1, source_target_pairs={{0,0},{256,1},{512,2},{768,3},{128,32},{384,33},{640,34},{896,35},... | collective-permute-start | bytes 393224 | tf_op jit(solution)/shard_map/ppermute | solution.py:132
  310.9 2.9 collective-permute-start.11
  313.8 4.4 %collective-permute-done.10 = bf16[64,1024]{0,1:T(8,128)(2,1)S(1)} collective-permute-done((bf16[64,1024]{0,1:T(8,128)(2,1)S(1)}, bf16[64,1024]{0,1:T(8,128)(2,1)S(1)}, u32[]{:S(2)}, u32[]{:S(2)}) %collective-permute-start.10) | collective-permute-done | bytes 131104 | tf_op jit(solution)/shard_map/ppermute | solution.py:111
  318.3 0.4 fusion.2
  318.7 8.9 %psum.23 = f32[320]{0:T(512)S(1)} all-reduce(f32[320]{0:T(512)S(1)} %fusion.2), channel_id=1, replica_groups=mesh['y'=4,'zl'=8,'c'=2,'x'=4,'zh'=4] {'x'}, use_global_device_ids=true, to_apply=%region_7.8 | all-reduce | flops 320 | bytes 2560 | tf_op jit(solution)/shard_map/psum | solution.py:114
  327.6 0.4 fusion.105
  328.0 1.9 multiply_convert_fusion
  330.0 1.9 fusion.9
  331.9 0.6 fusion.6
  332.5 0.7 gather_fusion.4
  333.2 4.0 %collective-permute-done.12 = bf16[256,256]{0,1:T(8,128)(2,1)} collective-permute-done((bf16[256,256]{0,1:T(8,128)(2,1)S(1)}, bf16[256,256]{0,1:T(8,128)(2,1)}, u32[]{:S(2)}, u32[]{:S(2)}) %collective-permute-start.12) | collective-permute-done | bytes 131104 | tf_op jit(solution)/shard_map/ppermute | solution.py:132
  337.2 13.1 %all_to_all.16 = bf16[4,256,256]{1,2,0:T(8,128)(2,1)S(1)} all-to-all(bf16[4,256,256]{1,2,0:T(8,128)(2,1)S(1)} %gather_fusion.4), channel_id=1, replica_groups=mesh['y'=4,'zl'=8,'c'=2,'x'=4,'zh'=4] {'x'}, dimensions={0} | all-to-all | bytes 1048576 | tf_op jit(solution)/shard_map/all_to_all | solution.py:134
  350.4 1.9 collective-permute-start.13
  352.3 28.1 %collective-permute-done.13 = bf16[256,256]{0,1:T(8,128)(2,1)S(1)} collective-permute-done((bf16[256,256]{0,1:T(8,128)(2,1)S(1)}, bf16[256,256]{0,1:T(8,128)(2,1)S(1)}, u32[]{:S(2)}, u32[]{:S(2)}) %collective-permute-start.13) | collective-permute-done | bytes 131104 | tf_op jit(solution)/shard_map/ppermute | solution.py:140
  380.4 0.9 pad_maximum_fusion.6
  381.4 0.9 copy.19
  (57 shorter events, 2.0 us)
Async XLA Ops:
  0.0 88.9 %copy-start = (s32[3,4]{1,0:T(4,128)S(1)}, s32[3,4]{1,0:T(4,128)}, u32[]{:S(2)}) copy-start(s32[3,4]{1,0:T(4,128)} %param.8) | copy-start | bytes 148
  1.0 93.7 %collective-permute-start = (bf16[256,256]{0,1:T(8,128)(2,1)S(1)}, bf16[256,256]{0,1:T(8,128)(2,1)S(1)}, u32[]{:S(2)}, u32[]{:S(2)}) collective-permute-start(bf16[256,256]{0,1:T(8,128)(2,1)S(1)} %copy.9), channel_id=1, source_target_pairs={{0,0},{1,256},{2,512},{3,768},{32,128},{33,384},{34,640},{35,896},... | collective-permute-start | bytes 393224 | tf_op jit(solution)/shard_map/ppermute | solution.py:69
  94.9 32.7 %collective-permute-start.1 = (bf16[1,1,512,256]{2,3,0,1:T(8,128)(2,1)S(1)}, bf16[1,1,512,256]{2,3,0,1:T(8,128)(2,1)S(1)}, u32[]{:S(2)}, u32[]{:S(2)}) collective-permute-start(bf16[1,1,512,256]{2,3,0,1:T(8,128)(2,1)S(1)} %copy.26), channel_id=1, source_target_pairs={{0,576},{32,608},{64,512},{96,544},{128,704},{160,736},{192,640},{... | collective-permute-start | bytes 786440 | tf_op jit(solution)/shard_map/ppermute | solution.py:97
  96.9 81.0 %copy-start.1 = (s32[1024]{0:T(1024)}, s32[1024]{0:T(1024)S(1)}, u32[]{:S(2)}) copy-start(s32[1024]{0:T(1024)S(1)} %pad_clamp_fusion) | copy-start | bytes 12292
  127.6 41.5 %collective-permute-start.3 = (bf16[2,1,512,256]{2,3,0,1:T(8,128)(2,1)S(1)}, bf16[2,1,512,256]{2,3,0,1:T(8,128)(2,1)S(1)}, u32[]{:S(2)}, u32[]{:S(2)}) collective-permute-start(bf16[2,1,512,256]{2,3,0,1:T(8,128)(2,1)S(1)} %pad_maximum_fusion.5), channel_id=1, source_target_pairs={{0,288},{32,768},{64,352},{96,832},{128,416},{160,896},{192,480},{... | collective-permute-start | bytes 1572872 | tf_op jit(solution)/shard_map/ppermute | solution.py:107
  133.3 24.9 %collective-permute-start.2 = (bf16[64,1024]{0,1:T(8,128)(2,1)S(1)}, bf16[64,1024]{0,1:T(8,128)(2,1)S(1)}, u32[]{:S(2)}, u32[]{:S(2)}) collective-permute-start(bf16[64,1024]{0,1:T(8,128)(2,1)S(1)} %slice.280), channel_id=1, source_target_pairs={{0,16},{16,128},{128,144},{144,1},{1,17},{17,129},{129,145},{145,2... | collective-permute-start | bytes 393224 | tf_op jit(solution)/shard_map/ppermute | solution.py:111
  169.3 16.8 %collective-permute-start.5 = (bf16[1,2,512,256]{2,3,0,1:T(8,128)(2,1)S(1)}, bf16[1,2,512,256]{2,3,0,1:T(8,128)(2,1)S(1)}, u32[]{:S(2)}, u32[]{:S(2)}) collective-permute-start(bf16[1,2,512,256]{2,3,0,1:T(8,128)(2,1)S(1)} %reshape.167), channel_id=1, source_target_pairs={{0,576},{32,608},{64,512},{96,544},{128,704},{160,736},{192,640},{... | collective-permute-start | bytes 1572872 | tf_op jit(solution)/shard_map/ppermute | solution.py:119
  172.2 5.0 %collective-permute-start.4 = (bf16[4,512,256]{1,2,0:T(8,128)(2,1)S(1)}, bf16[4,512,256]{1,2,0:T(8,128)(2,1)S(1)}, u32[]{:S(2)}, u32[]{:S(2)}) collective-permute-start(bf16[4,512,256]{1,2,0:T(8,128)(2,1)S(1)} %bitcast.97), channel_id=1, source_target_pairs={{0,16},{16,0},{1,17},{17,1},{2,18},{18,2},{3,19},{19,3},{4,20},{20... | collective-permute-start | bytes 3145736 | tf_op jit(solution)/shard_map/ppermute | solution.py:118
  179.2 13.9 %all-to-all-start = ((bf16[4,256,256]{1,2,0:T(8,128)(2,1)}), bf16[4,256,256]{1,2,0:T(8,128)(2,1)S(1)}, u32[]{:S(2)}, u32[]{:S(2)}) async-start(bf16[4,256,256]{1,2,0:T(8,128)(2,1)} %gather_fusion.2), calls=%async_computation | async-start | bytes 1048576 | tf_op jit(solution)/shard_map/all_to_all | solution.py:134
  193.2 68.2 %collective-permute-start.6 = (bf16[2,2,512,256]{2,3,0,1:T(8,128)(2,1)}, bf16[2,2,512,256]{2,3,0,1:T(8,128)(2,1)}, u32[]{:S(2)}, u32[]{:S(2)}) collective-permute-start(bf16[2,2,512,256]{2,3,0,1:T(8,128)(2,1)} %pad_maximum_fusion.1), channel_id=1, source_target_pairs={{0,288},{32,768},{64,352},{96,832},{128,416},{160,896},{192,480},{... | collective-permute-start | bytes 3145736 | tf_op jit(solution)/shard_map/ppermute | solution.py:139
  200.4 70.1 %collective-permute-start.9 = (bf16[256,256]{0,1:T(8,128)(2,1)S(1)}, bf16[256,256]{0,1:T(8,128)(2,1)S(1)}, u32[]{:S(2)}, u32[]{:S(2)}) collective-permute-start(bf16[256,256]{0,1:T(8,128)(2,1)S(1)} %add_convert_fusion.2), channel_id=1, source_target_pairs={{0,0},{256,1},{512,2},{768,3},{128,32},{384,33},{640,34},{896,35},... | collective-permute-start | bytes 393224 | tf_op jit(solution)/shard_map/ppermute | solution.py:132
  236.8 15.2 %collective-permute-start.7 = (bf16[64,1024]{0,1:T(8,128)(2,1)S(1)}, bf16[64,1024]{0,1:T(8,128)(2,1)S(1)}, u32[]{:S(2)}, u32[]{:S(2)}) collective-permute-start(bf16[64,1024]{0,1:T(8,128)(2,1)S(1)} %slice.377), channel_id=1, source_target_pairs={{0,16},{16,128},{128,144},{144,1},{1,17},{17,129},{129,145},{145,2... | collective-permute-start | bytes 393224 | tf_op jit(solution)/shard_map/ppermute | solution.py:111
  263.9 4.5 %collective-permute-start.8 = (bf16[4,512,256]{1,2,0:T(8,128)(2,1)S(1)}, bf16[4,512,256]{1,2,0:T(8,128)(2,1)S(1)}, u32[]{:S(2)}, u32[]{:S(2)}) collective-permute-start(bf16[4,512,256]{1,2,0:T(8,128)(2,1)S(1)} %get-tuple-element.29), channel_id=1, source_target_pairs={{0,16},{16,0},{1,17},{17,1},{2,18},{18,2},{3,19},{19,3},{4,20},{20... | collective-permute-start | bytes 3145736 | tf_op jit(solution)/shard_map/ppermute | solution.py:110
  298.4 19.8 %collective-permute-start.10 = (bf16[64,1024]{0,1:T(8,128)(2,1)S(1)}, bf16[64,1024]{0,1:T(8,128)(2,1)S(1)}, u32[]{:S(2)}, u32[]{:S(2)}) collective-permute-start(bf16[64,1024]{0,1:T(8,128)(2,1)S(1)} %slice.394), channel_id=1, source_target_pairs={{0,16},{16,128},{128,144},{144,1},{1,17},{17,129},{129,145},{145,2... | collective-permute-start | bytes 393224 | tf_op jit(solution)/shard_map/ppermute | solution.py:111
  305.1 32.1 %collective-permute-start.12 = (bf16[256,256]{0,1:T(8,128)(2,1)S(1)}, bf16[256,256]{0,1:T(8,128)(2,1)}, u32[]{:S(2)}, u32[]{:S(2)}) collective-permute-start(bf16[256,256]{0,1:T(8,128)(2,1)S(1)} %add_convert_fusion.1), channel_id=1, source_target_pairs={{0,0},{256,1},{512,2},{768,3},{128,32},{384,33},{640,34},{896,35},... | collective-permute-start | bytes 393224 | tf_op jit(solution)/shard_map/ppermute | solution.py:132
  310.9 19.1 %collective-permute-start.11 = (bf16[4,512,256]{1,2,0:T(8,128)(2,1)}, bf16[4,512,256]{1,2,0:T(8,128)(2,1)}, u32[]{:S(2)}, u32[]{:S(2)}) collective-permute-start(bf16[4,512,256]{1,2,0:T(8,128)(2,1)} %get-tuple-element.32), channel_id=1, source_target_pairs={{0,16},{16,0},{1,17},{17,1},{2,18},{18,2},{3,19},{19,3},{4,20},{20... | collective-permute-start | bytes 3145736 | tf_op jit(solution)/shard_map/ppermute | solution.py:110
  350.4 30.0 %collective-permute-start.13 = (bf16[256,256]{0,1:T(8,128)(2,1)S(1)}, bf16[256,256]{0,1:T(8,128)(2,1)S(1)}, u32[]{:S(2)}, u32[]{:S(2)}) collective-permute-start(bf16[256,256]{0,1:T(8,128)(2,1)S(1)} %add_convert_fusion), channel_id=1, source_target_pairs={{0,0},{256,1},{512,2},{768,3},{128,32},{384,33},{640,34},{896,35},... | collective-permute-start | bytes 393224 | tf_op jit(solution)/shard_map/ppermute | solution.py:140

commit v5 on v3

v5 whole, which is shorter than its diff:
```python
import jax
import jax.numpy as jnp
from jax import lax
from jax.sharding import Mesh, PartitionSpec as P

REACH = 64
SECTION = ("y", "zq", "zp", "c")
MOVED = ("zq", "zp", "zh")
PLACE = ("y", "zq", "c", "zh")


def moved_pairs(n_zl, n_zh):
    pairs = []
    for zl in range(n_zl):
        for zh in range(n_zh):
            pairs.append((zl * n_zh + zh, (zl % 2 * n_zh + zh) * n_zh + zl // 2))
    return pairs


def halo_pairs(n_y, n_zl, n_c, n_zh):
    places = []
    for y in range(n_y):
        for zl in range(n_zl):
            for c in range(n_c):
                places.append(((y * 2 + zl % 2) * n_c + c) * n_zh + zl // 2)
    return list(zip(places[:-1], places[1:]))


def rotated(value, axis, steps):
    count = lax.axis_size(axis)
    return lax.ppermute(value, axis, [(source, (source + steps) % count) for source in range(count)])


def body(signal, mixing, taps, offsets):
    row_count, width = signal.shape
    layers, n_taps = taps.shape[:2]
    n_x, n_y, n_c, n_zh = (lax.axis_size(a) for a in ("x", "y", "c", "zh"))
    n_zl = lax.axis_size(("zq", "zp"))
    y, zp, c = lax.axis_index("y"), lax.axis_index("zp"), lax.axis_index("c")
    total_channels = n_x * n_zh * width
    there = moved_pairs(n_zl, n_zh)
    back = [(target, source) for source, target in there]
    forward = halo_pairs(n_y, n_zl, n_c, n_zh)

    hidden = lax.ppermute(signal, MOVED, there)

    half = width // n_c
    share = lax.dynamic_slice(mixing, (0, c * half, (y * n_zh + zp) * width), (layers, half, width))
    high = lax.reduce_precision(taps, 8, 7)
    low = (taps - high).astype(jnp.bfloat16)
    n_tap_rows = layers * n_taps
    sent = jnp.concatenate(
        [
            share.reshape(layers * half, width),
            high.astype(jnp.bfloat16).reshape(n_tap_rows, width),
            low.reshape(n_tap_rows, width),
            jnp.zeros((-2 * n_tap_rows % 16, width), jnp.bfloat16),
        ],
        axis=0,
    )
    got = lax.all_gather(sent, "zh", axis=0)
    hidden, got = lax.optimization_barrier((hidden, got))
    coeffs = got[:, layers * half :].astype(jnp.float32)
    coeffs = coeffs[:, :n_tap_rows] + coeffs[:, n_tap_rows : 2 * n_tap_rows]
    coeffs = coeffs.transpose(1, 0, 2).reshape(layers, n_taps, n_zh * width)
    first = lax.all_gather(got[:, :half], "c", axis=1, tiled=True).reshape(n_zh * width, width)
    hidden, first = lax.optimization_barrier((hidden, first))
    first = jnp.stack([first] + [rotated(first, "y", k) for k in range(1, n_y)])
    rest = [got[:, layer * half : (layer + 1) * half] for layer in range(1, layers)]
    entry_of = (y - jnp.arange(n_x)) % n_y
    returned = []
    for layer in range(layers):
        wide = lax.all_gather(hidden, "zp", axis=1, tiled=True)
        before = lax.ppermute(wide[row_count - REACH :], PLACE, forward)
        values = jnp.concatenate([before, wide], axis=0).astype(jnp.float32)
        squares = lax.psum(jnp.sum(values * values, axis=-1), "x")
        if layer == 0:
            squares, rest = lax.optimization_barrier((squares, rest))
            rest = [lax.all_gather(part, "c", axis=1, tiled=True).reshape(n_zh * width, width) for part in rest]
            later = lax.all_gather(jnp.stack(rest), "y", axis=0)
        normed = values * lax.rsqrt(squares / total_channels + 1e-06)[:, None]
        stored = normed.astype(jnp.bfloat16)
        conv = jnp.zeros((row_count, values.shape[1]), jnp.float32)
        for k in range(n_taps):
            window = lax.dynamic_slice_in_dim(stored, REACH - offsets[layer, k], row_count, 0)
            conv = conv + coeffs[layer, k] * window.astype(jnp.float32)
        gated = (conv * jax.nn.silu(normed[REACH:])).astype(jnp.bfloat16)
        tile = first if layer == 0 else later[:, layer - 1]
        partial = jnp.einsum("tk,xkn->xtn", gated, tile, preferred_element_type=jnp.float32).astype(jnp.bfloat16)
        if layer == 0:
            partial = partial[entry_of]
        else:
            returned.append(lax.ppermute(hidden, MOVED, back))
            partial, returned[-1] = lax.optimization_barrier((partial, returned[-1]))
        terms = lax.all_to_all(partial, "x", split_axis=0, concat_axis=0)
        mixed = jnp.sum(terms.astype(jnp.float32), axis=0)
        hidden = (hidden.astype(jnp.float32) + mixed).astype(jnp.bfloat16)
    returned.append(lax.ppermute(hidden, MOVED, back))
    return jnp.stack(returned)


def solution(mesh):
    fine = Mesh(mesh.devices.reshape(4, 2, 4, 2, 4, 4), ("y", "zq", "zp", "c", "x", "zh"))
    dp = ("x", "zh")
    in_specs = (P(SECTION, dp), P(None, dp, None), P(None, None, dp), P())
    out_specs = P(None, SECTION, dp)
    return jax.shard_map(body, mesh=fine, in_specs=in_specs, out_specs=out_specs, check_vma=False)
```

time: 435 us -> 397 us (0.913)
  the two profiles are of different devices: /device:TPU:88 before, /device:TPU:240 now
where the time goes in v5:
time: 397 us; the launch traced here: 396 us
  blocking collectives  209 us (53%)
  waiting for transfers between devices  96.2 us (24%)
  starting transfers between devices  41.7 us (11%)
  between operations  28.9 us (7%)
  matrix products  10.8 us (3%)
  local copies, waits for them, and re-layouts  5.01 us (1%)
  other arithmetic  4.81 us (1%)
    all_gather x1, blocking collectives, body(): got = lax.all_gather(sent, 'zh', axis=0)  82.6 us
    all_gather x3, blocking collectives, body(): wide = lax.all_gather(hidden, 'zp', axis=1, tiled=True)  59.3 us
    ppermute x3, waiting for transfers between devices, body(): before = lax.ppermute(wide[row_count - REACH:], PLACE, forward)  46.2 us
    ppermute x3, waiting for transfers between devices, rotated(): lax.ppermute(value, axis, [(source, (source + steps) % count) for source...  33.7 us
    all_to_all x3, blocking collectives, body(): terms = lax.all_to_all(partial, 'x', split_axis=0, concat_axis=0)  31.9 us
    psum x3, blocking collectives, body(): squares = lax.psum(jnp.sum(values * values, axis=-1), 'x')  28.4 us
    ppermute x1, starting transfers between devices, body(): hidden = lax.ppermute(signal, MOVED, there)  16.8 us
    ppermute x3, waiting for transfers between devices, body(): returned.append(lax.ppermute(hidden, MOVED, back))  16.3 us
  transfers between devices with their start and end apart: 11, of which 7 were waited for; matrix products, arithmetic and copies ran while one was open for 4% of the time, Pallas kernels for 0%

profile of v5, /device:TPU:240, one launch (start us, length us, event | category | flops | bytes accessed | tf_op | source)
XLA Modules:
  0.0 396.2 jit_solution(16666307547435591868)
XLA Ops:
  6.5 0.0 all-gather.4.cloned.1.call-start
  6.5 1.0 copy.11
  7.5 16.8 %collective-permute-start = (bf16[256,256]{0,1:T(8,128)(2,1)S(1)}, bf16[256,256]{0,1:T(8,128)(2,1)S(1)}, u32[]{:S(2)}, u32[]{:S(2)}) collective-permute-start(bf16[256,256]{0,1:T(8,128)(2,1)S(1)} %copy.11), channel_id=1, source_target_pairs={{0,0},{1,32},{2,64},{3,96},{32,128},{33,160},{34,192},{35,224},{64... | collective-permute-start | bytes 393224 | tf_op jit(solution)/shard_map/ppermute | solution.py:45
  24.4 0.7 reduce-precision_convert_fusion
  25.1 0.1 pad.18.clone
  25.2 0.9 constant_dynamic-slice_fusion
  26.2 0.1 maximum_maximum_fusion
  26.3 82.6 %all-gather = bf16[1664,256]{1,0:T(8,128)(2,1)S(1)} all-gather(bf16[416,256]{1,0:T(8,128)(2,1)S(1)} %maximum_maximum_fusion), channel_id=2, replica_groups=mesh['y'=4,'zq'=2,'zp'=4,'c'=2,'x'=4,'zh'=4] {'zh'}, dimensions={0}, use_global_device_ids=true | all-gather | bytes 1064960 | tf_op jit(solution)/shard_map/all_gather | solution.py:61
  108.9 0.0 collective-permute-done
  109.0 0.1 fusion.64
  109.0 2.2 all_gather.32
  111.2 0.2 copy.23
  111.4 16.4 %all_gather.33 = bf16[256,1024]{0,1:T(8,128)(2,1)S(1)} all-gather(bf16[256,256]{0,1:T(8,128)(2,1)S(1)} %collective-permute-done), channel_id=1, replica_groups=mesh['y'=4,'zq'=2,'zp'=4,'c'=2,'x'=4,'zh'=4] {'zp'}, dimensions={1}, use_global_device_ids=true | all-gather | bytes 655360 | tf_op jit(solution)/shard_map/all_gather | solution.py:73
  127.8 0.1 slice.154
  127.9 1.9 collective-permute-start.1
  129.9 11.1 %collective-permute-done.1 = bf16[64,1024]{0,1:T(8,128)(2,1)S(1)} collective-permute-done((bf16[64,1024]{0,1:T(8,128)(2,1)S(1)}, bf16[64,1024]{0,1:T(8,128)(2,1)S(1)}, u32[]{:S(2)}, u32[]{:S(2)}) %collective-permute-start.1) | collective-permute-done | bytes 131104 | tf_op jit(solution)/shard_map/ppermute | solution.py:74
  140.9 0.4 fusion.10
  141.3 10.5 %psum.21 = f32[320]{0:T(512)S(1)} all-reduce(f32[320]{0:T(512)S(1)} %fusion.10), channel_id=1, replica_groups=mesh['y'=4,'zq'=2,'zp'=4,'c'=2,'x'=4,'zh'=4] {'x'}, use_global_device_ids=true, to_apply=%region_1.2 | all-reduce | flops 320 | bytes 2560 | tf_op jit(solution)/shard_map/psum | solution.py:76
  151.8 2.2 all_gather.34
  154.0 2.2 all_gather.35
  156.2 0.0 copy-start
  156.2 1.1 pad_maximum_fusion
  157.2 0.0 all-gather.4.cloned.1.call-update
  157.3 0.0 copy-done
  157.3 0.7 fusion.66
  163.1 8.0 %collective-permute-start.2 = (bf16[1024,256]{0,1:T(8,128)(2,1)S(1)}, bf16[1024,256]{0,1:T(8,128)(2,1)S(1)}, u32[]{:S(2)}, u32[]{:S(2)}) collective-permute-start(bf16[1024,256]{0,1:T(8,128)(2,1)S(1)} %copy.23), channel_id=1, source_target_pairs={{0,256},{256,512},{512,768},{768,0},{1,257},{257,513},{513,769},{7... | collective-permute-start | bytes 1572872 | tf_op jit(solution)/shard_map/ppermute | solution.py:31
  171.1 1.9 collective-permute-start.3
  173.0 3.4 collective-permute-start.4
  176.6 0.4 fusion.51
  177.0 9.0 %collective-permute-done.2 = bf16[1024,256]{0,1:T(8,128)(2,1)S(1)} collective-permute-done((bf16[1024,256]{0,1:T(8,128)(2,1)S(1)}, bf16[1024,256]{0,1:T(8,128)(2,1)S(1)}, u32[]{:S(2)}, u32[]{:S(2)}) %collective-permute-start.2) | collective-permute-done | bytes 524320 | tf_op jit(solution)/shard_map/ppermute | solution.py:31
  186.0 21.7 %collective-permute-done.3 = bf16[1024,256]{0,1:T(8,128)(2,1)S(1)} collective-permute-done((bf16[1024,256]{0,1:T(8,128)(2,1)S(1)}, bf16[1024,256]{0,1:T(8,128)(2,1)S(1)}, u32[]{:S(2)}, u32[]{:S(2)}) %collective-permute-start.3) | collective-permute-done | bytes 524320 | tf_op jit(solution)/shard_map/ppermute | solution.py:31
  207.7 3.0 collective-permute-done.4
  210.6 3.0 fusion.18
  213.6 0.6 gather_fusion
  214.2 11.0 %all_to_all.15 = bf16[4,256,256]{1,2,0:T(8,128)(2,1)S(1)} all-to-all(bf16[4,256,256]{1,2,0:T(8,128)(2,1)S(1)} %gather_fusion), channel_id=1, replica_groups=mesh['y'=4,'zq'=2,'zp'=4,'c'=2,'x'=4,'zh'=4] {'x'}, dimensions={0} | all-to-all | bytes 1048576 | tf_op jit(solution)/shard_map/all_to_all | solution.py:95
  225.2 0.1 convert_reduce_fusion.2
  225.3 23.4 %all_gather.38 = bf16[256,1024]{0,1:T(8,128)(2,1)S(1)} all-gather(bf16[256,256]{0,1:T(8,128)(2,1)S(1)} %add_convert_fusion.2), channel_id=1, replica_groups=mesh['y'=4,'zq'=2,'zp'=4,'c'=2,'x'=4,'zh'=4] {'zp'}, dimensions={1}, use_global_device_ids=true | all-gather | bytes 655360 | tf_op jit(solution)/shard_map/all_gather | solution.py:73
  248.7 0.1 slice.164
  248.9 1.9 collective-permute-start.5
  255.8 1.9 collective-permute-start.6
  257.8 17.7 %collective-permute-done.5 = bf16[64,1024]{0,1:T(8,128)(2,1)S(1)} collective-permute-done((bf16[64,1024]{0,1:T(8,128)(2,1)S(1)}, bf16[64,1024]{0,1:T(8,128)(2,1)S(1)}, u32[]{:S(2)}, u32[]{:S(2)}) %collective-permute-start.5) | collective-permute-done | bytes 131104 | tf_op jit(solution)/shard_map/ppermute | solution.py:74
  275.5 0.4 fusion.11
  275.9 8.9 %psum.22 = f32[320]{0:T(512)S(1)} all-reduce(f32[320]{0:T(512)S(1)} %fusion.11), channel_id=1, replica_groups=mesh['y'=4,'zq'=2,'zp'=4,'c'=2,'x'=4,'zh'=4] {'x'}, use_global_device_ids=true, to_apply=%region_4.5 | all-reduce | flops 320 | bytes 2560 | tf_op jit(solution)/shard_map/psum | solution.py:76
  284.8 0.4 fusion.52
  285.2 0.0 all-gather.4.cloned.1.call-done
  285.3 3.9 fusion.22
  289.2 0.0 collective-permute-done.6
  289.2 10.5 %all_to_all.16 = bf16[4,256,256]{1,2,0:T(8,128)(2,1)S(1)} all-to-all(bf16[4,256,256]{1,2,0:T(8,128)(2,1)S(1)} %fusion.22), channel_id=1, replica_groups=mesh['y'=4,'zq'=2,'zp'=4,'c'=2,'x'=4,'zh'=4] {'x'}, dimensions={0} | all-to-all | bytes 1048576 | tf_op jit(solution)/shard_map/all_to_all | solution.py:95
  299.7 0.1 convert_reduce_fusion.1
  299.8 19.4 %all_gather.39 = bf16[256,1024]{0,1:T(8,128)(2,1)S(1)} all-gather(bf16[256,256]{0,1:T(8,128)(2,1)S(1)} %add_convert_fusion.1), channel_id=1, replica_groups=mesh['y'=4,'zq'=2,'zp'=4,'c'=2,'x'=4,'zh'=4] {'zp'}, dimensions={1}, use_global_device_ids=true | all-gather | bytes 655360 | tf_op jit(solution)/shard_map/all_gather | solution.py:73
  319.2 0.1 slice.171
  319.4 1.9 collective-permute-start.7
  326.3 1.9 collective-permute-start.8
  328.3 17.4 %collective-permute-done.7 = bf16[64,1024]{0,1:T(8,128)(2,1)S(1)} collective-permute-done((bf16[64,1024]{0,1:T(8,128)(2,1)S(1)}, bf16[64,1024]{0,1:T(8,128)(2,1)S(1)}, u32[]{:S(2)}, u32[]{:S(2)}) %collective-permute-start.7) | collective-permute-done | bytes 131104 | tf_op jit(solution)/shard_map/ppermute | solution.py:74
  345.7 0.4 fusion.12
  346.1 9.0 %psum.23 = f32[320]{0:T(512)S(1)} all-reduce(f32[320]{0:T(512)S(1)} %fusion.12), channel_id=1, replica_groups=mesh['y'=4,'zq'=2,'zp'=4,'c'=2,'x'=4,'zh'=4] {'x'}, use_global_device_ids=true, to_apply=%region_7.8 | all-reduce | flops 320 | bytes 2560 | tf_op jit(solution)/shard_map/psum | solution.py:76
  355.1 0.4 fusion.53
  355.6 4.0 %fusion.21 = bf16[4,256,256]{1,2,0:T(8,128)(2,1)S(1)} fusion(bf16[4,2,1024,256]{3,2,1,0:T(8,128)(2,1)} %bitcast.107, f32[320,1024]{0,1:T(8,128)S(1)} %get-tuple-element.31, bf16[320,1024]{0,1:T(8,128)(2,1)S(1)} %get-tuple-element.30, s32[]{:T(128)S(6)} %select_n.81, f32[1024]{0:T(1024)S(1)} %bitcast.95, s32[]{:T(128)S(6)} %select_n.80, ...), kind=kOutput, calls=%fused_computation.26 | convolution fusion | flops 541589504 | bytes 5783568 | tf_op jit(solution)/shard_map/tk,xkn->xtn/dot_general | solution.py:89
  359.5 0.0 collective-permute-done.8
  359.5 10.5 %all_to_all.17 = bf16[4,256,256]{1,2,0:T(8,128)(2,1)S(1)} all-to-all(bf16[4,256,256]{1,2,0:T(8,128)(2,1)S(1)} %fusion.21), channel_id=1, replica_groups=mesh['y'=4,'zq'=2,'zp'=4,'c'=2,'x'=4,'zh'=4] {'x'}, dimensions={0} | all-to-all | bytes 1048576 | tf_op jit(solution)/shard_map/all_to_all | solution.py:95
  370.0 0.1 convert_reduce_fusion
  370.1 1.9 collective-permute-start.9
  372.1 16.3 %collective-permute-done.9 = bf16[256,256]{0,1:T(8,128)(2,1)S(1)} collective-permute-done((bf16[256,256]{0,1:T(8,128)(2,1)S(1)}, bf16[256,256]{0,1:T(8,128)(2,1)S(1)}, u32[]{:S(2)}, u32[]{:S(2)}) %collective-permute-start.9) | collective-permute-done | bytes 131104 | tf_op jit(solution)/shard_map/ppermute | solution.py:98
  388.4 0.9 copy.19
  (17 shorter events, 0.3 us)
Async XLA Ops:
  6.5 278.7 %all-gather.4.cloned.1.call-start = ((), (), s32[]{:S(2)}) async-start(), calls=%async_computation.3 | async-start | bytes 5242880 | tf_op jit(solution)/shard_map/all_gather | solution.py:80
  7.5 101.4 %collective-permute-start = (bf16[256,256]{0,1:T(8,128)(2,1)S(1)}, bf16[256,256]{0,1:T(8,128)(2,1)S(1)}, u32[]{:S(2)}, u32[]{:S(2)}) collective-permute-start(bf16[256,256]{0,1:T(8,128)(2,1)S(1)} %copy.11), channel_id=1, source_target_pairs={{0,0},{1,32},{2,64},{3,96},{32,128},{33,160},{34,192},{35,224},{64... | collective-permute-start | bytes 393224 | tf_op jit(solution)/shard_map/ppermute | solution.py:45
  127.9 13.0 %collective-permute-start.1 = (bf16[64,1024]{0,1:T(8,128)(2,1)S(1)}, bf16[64,1024]{0,1:T(8,128)(2,1)S(1)}, u32[]{:S(2)}, u32[]{:S(2)}) collective-permute-start(bf16[64,1024]{0,1:T(8,128)(2,1)S(1)} %slice.154), channel_id=1, source_target_pairs={{0,16},{16,128},{128,144},{144,1},{1,17},{17,129},{129,145},{145,2... | collective-permute-start | bytes 393224 | tf_op jit(solution)/shard_map/ppermute | solution.py:74
  156.2 1.1 copy-start
  163.1 23.0 %collective-permute-start.2 = (bf16[1024,256]{0,1:T(8,128)(2,1)S(1)}, bf16[1024,256]{0,1:T(8,128)(2,1)S(1)}, u32[]{:S(2)}, u32[]{:S(2)}) collective-permute-start(bf16[1024,256]{0,1:T(8,128)(2,1)S(1)} %copy.23), channel_id=1, source_target_pairs={{0,256},{256,512},{512,768},{768,0},{1,257},{257,513},{513,769},{7... | collective-permute-start | bytes 1572872 | tf_op jit(solution)/shard_map/ppermute | solution.py:31
  171.1 36.6 %collective-permute-start.3 = (bf16[1024,256]{0,1:T(8,128)(2,1)S(1)}, bf16[1024,256]{0,1:T(8,128)(2,1)S(1)}, u32[]{:S(2)}, u32[]{:S(2)}) collective-permute-start(bf16[1024,256]{0,1:T(8,128)(2,1)S(1)} %copy.23), channel_id=1, source_target_pairs={{0,512},{256,768},{512,0},{768,256},{1,513},{257,769},{513,1},{769... | collective-permute-start | bytes 1572872 | tf_op jit(solution)/shard_map/ppermute | solution.py:31
  173.0 37.6 %collective-permute-start.4 = (bf16[1024,256]{0,1:T(8,128)(2,1)S(1)}, bf16[1024,256]{0,1:T(8,128)(2,1)}, u32[]{:S(2)}, u32[]{:S(2)}) collective-permute-start(bf16[1024,256]{0,1:T(8,128)(2,1)S(1)} %copy.23), channel_id=1, source_target_pairs={{0,768},{256,0},{512,256},{768,512},{1,769},{257,1},{513,257},{769... | collective-permute-start | bytes 1572872 | tf_op jit(solution)/shard_map/ppermute | solution.py:31
  248.9 26.6 %collective-permute-start.5 = (bf16[64,1024]{0,1:T(8,128)(2,1)S(1)}, bf16[64,1024]{0,1:T(8,128)(2,1)S(1)}, u32[]{:S(2)}, u32[]{:S(2)}) collective-permute-start(bf16[64,1024]{0,1:T(8,128)(2,1)S(1)} %slice.164), channel_id=1, source_target_pairs={{0,16},{16,128},{128,144},{144,1},{1,17},{17,129},{129,145},{145,2... | collective-permute-start | bytes 393224 | tf_op jit(solution)/shard_map/ppermute | solution.py:74
  255.8 33.3 %collective-permute-start.6 = (bf16[256,256]{0,1:T(8,128)(2,1)S(1)}, bf16[256,256]{0,1:T(8,128)(2,1)S(1)}, u32[]{:S(2)}, u32[]{:S(2)}) collective-permute-start(bf16[256,256]{0,1:T(8,128)(2,1)S(1)} %add_convert_fusion.2), channel_id=1, source_target_pairs={{0,0},{32,1},{64,2},{96,3},{128,32},{160,33},{192,34},{224,35},{1,... | collective-permute-start | bytes 393224 | tf_op jit(solution)/shard_map/ppermute | solution.py:93
  319.4 26.3 %collective-permute-start.7 = (bf16[64,1024]{0,1:T(8,128)(2,1)S(1)}, bf16[64,1024]{0,1:T(8,128)(2,1)S(1)}, u32[]{:S(2)}, u32[]{:S(2)}) collective-permute-start(bf16[64,1024]{0,1:T(8,128)(2,1)S(1)} %slice.171), channel_id=1, source_target_pairs={{0,16},{16,128},{128,144},{144,1},{1,17},{17,129},{129,145},{145,2... | collective-permute-start | bytes 393224 | tf_op jit(solution)/shard_map/ppermute | solution.py:74
  326.3 33.2 %collective-permute-start.8 = (bf16[256,256]{0,1:T(8,128)(2,1)S(1)}, bf16[256,256]{0,1:T(8,128)(2,1)S(1)}, u32[]{:S(2)}, u32[]{:S(2)}) collective-permute-start(bf16[256,256]{0,1:T(8,128)(2,1)S(1)} %add_convert_fusion.1), channel_id=1, source_target_pairs={{0,0},{32,1},{64,2},{96,3},{128,32},{160,33},{192,34},{224,35},{1,... | collective-permute-start | bytes 393224 | tf_op jit(solution)/shard_map/ppermute | solution.py:93
  370.1 18.3 %collective-permute-start.9 = (bf16[256,256]{0,1:T(8,128)(2,1)S(1)}, bf16[256,256]{0,1:T(8,128)(2,1)S(1)}, u32[]{:S(2)}, u32[]{:S(2)}) collective-permute-start(bf16[256,256]{0,1:T(8,128)(2,1)S(1)} %add_convert_fusion), channel_id=1, source_target_pairs={{0,0},{32,1},{64,2},{96,3},{128,32},{160,33},{192,34},{224,35},{1,... | collective-permute-start | bytes 393224 | tf_op jit(solution)/shard_map/ppermute | solution.py:98
Sparse Core Ops, SparseCore 0:
  157.4 73.1 all-gather.3

commit v6 on v2

--- a/solution.py
+++ b/solution.py
@@ -6,6 +6,7 @@
 C = 4096
 REACH = 64
 SECTION = ("y", "zl", "c")
+PLACE = ("y", "zl", "c", "zh")
 
 
 def rotated(value, axis, steps):
@@ -13,43 +14,41 @@
     return lax.ppermute(value, axis, [(source, (source + steps) % count) for source in range(count)])
 
 
+def halo_pairs(n_y, n_zl, n_c, n_zh):
+    n_section = n_y * n_zl * n_c
+    pairs = []
+    for section in range(n_section - 1):
+        step = 1 if (section + 1) % (n_zl * n_c) == 0 else 0
+        for zh in range(n_zh):
+            pairs.append((section * n_zh + zh, (section + 1) * n_zh + (zh + step) % n_zh))
+    return pairs
+
+
 def crossed_weights(mixing):
     layers, depth, width = mixing.shape
     n_y, n_c, n_zh = lax.axis_size("y"), lax.axis_size("c"), lax.axis_size("zh")
-    y, c = lax.axis_index("y"), lax.axis_index("c")
+    y, c, parity = lax.axis_index("y"), lax.axis_index("c"), lax.axis_index("zl") % 2
     columns = width // n_y
     rows = depth // n_c
     first = lax.dynamic_slice(mixing, (0, c * rows, y * columns), (1, rows, columns))
     first = first.reshape(rows, n_zh, columns // n_zh).transpose(1, 0, 2)
-    few = depth // (lax.axis_size("zl") * n_c)
-    rest = lax.dynamic_slice(
-        mixing, (1, (lax.axis_index("zl") * n_c + c) * few, y * columns), (layers - 1, few, columns)
-    )
+    few = rows // 2
+    rest = lax.dynamic_slice(mixing, (1, c * rows + parity * few, y * columns), (layers - 1, few, columns))
     rest = rest.reshape(layers - 1, few, n_zh, columns // n_zh).transpose(2, 0, 1, 3)
     rest = rest.reshape(n_zh, (layers - 1) * few, columns // n_zh)
     got = lax.all_to_all(jnp.concatenate([first, rest], axis=1), "zh", split_axis=0, concat_axis=0)
-    return got[:, :rows], got[:, rows:]
-
-
-def later_tiles(rest, layers):
-    n_zh, rows, columns = rest.shape
-    few = rows // layers
-    n_y = lax.axis_size("y")
-    n_row = lax.axis_size("zl") * lax.axis_size("c")
-    gathered = lax.all_gather(rest, SECTION, axis=0)
-    gathered = gathered.reshape(n_y, n_row, n_zh, layers, few, columns).transpose(3, 0, 2, 1, 4, 5)
-    return gathered.reshape(layers, n_y, n_zh * n_row * few, columns)
+    return got[:, :rows], got[:, rows:].reshape(n_zh, layers - 1, few, columns // n_zh)
 
 
 def body(signal, mixing, taps, offsets):
     row_count, channel_count = signal.shape
     layers, n_taps = taps.shape[:2]
-    n_section = lax.axis_size(SECTION)
-    n_y = lax.axis_size("y")
-    forward = [(source, source + 1) for source in range(n_section - 1)]
+    n_y, n_zl, n_c, n_zh = (lax.axis_size(a) for a in ("y", "zl", "c", "zh"))
+    forward = halo_pairs(n_y, n_zl, n_c, n_zh)
     first, rest = crossed_weights(mixing)
     signal, first, rest = lax.optimization_barrier((signal, first, rest))
-    later = later_tiles(rest, layers - 1)
+    partner = lax.ppermute(rest, "zl", [(i, i ^ 1) for i in range(n_zl)])
+    even = lax.axis_index("zl") % 2 == 0
     own = lax.all_gather(first, "c", axis=1, tiled=True).reshape(-1, channel_count)
     turned = jnp.stack([own] + [rotated(own, "y", k) for k in range(1, n_y)])
     high = lax.reduce_precision(taps, 8, 7)
@@ -67,9 +66,16 @@
             coeffs = wide[row_count : row_count + 2 * n_tap_rows].astype(jnp.float32)
             coeffs = (coeffs[:n_tap_rows] + coeffs[n_tap_rows:]).reshape(layers, n_taps, -1)
             wide = wide[:row_count]
+            wide, turned, partner = lax.optimization_barrier((wide, turned, partner))
+            pair = jnp.stack([jnp.where(even, rest, partner), jnp.where(even, partner, rest)], axis=2)
+            pair = pair.reshape(n_zh, layers - 1, -1, channel_count)
+            whole = [lax.all_gather(pair[:, i], "c", axis=1, tiled=True) for i in range(layers - 1)]
+            wide, whole = lax.optimization_barrier((wide, whole))
+            whole = jnp.stack([part.reshape(-1, channel_count) for part in whole])
+            later = lax.all_gather(whole, "y", axis=0)
         else:
             wide = lax.all_gather(hidden, "zh", axis=1, tiled=True)
-        before = lax.ppermute(wide[row_count - REACH :], SECTION, forward)
+        before = lax.ppermute(wide[row_count - REACH :], PLACE, forward)
         values = jnp.concatenate([before, wide], axis=0).astype(jnp.float32)
         squares = lax.psum(jnp.sum(values * values, axis=-1), "x")
         normed = values * lax.rsqrt(squares / C + 1e-06)[:, None]
@@ -79,7 +85,7 @@
             window = lax.dynamic_slice_in_dim(stored, REACH - offsets[layer, k], row_count, 0)
             conv = conv + coeffs[layer, k] * window.astype(jnp.float32)
         gated = (conv * jax.nn.silu(normed[REACH:])).astype(jnp.bfloat16)
-        tile = turned if layer == 0 else later[layer - 1]
+        tile = turned if layer == 0 else later[:, layer - 1]
         partial = jnp.einsum("tk,xkn->xtn", gated, tile, preferred_element_type=jnp.float32).astype(jnp.bfloat16)
         if layer == 0:
             partial = partial[(lax.axis_index("y") - jnp.arange(n_y)) % n_y]

time: 375 us -> 399 us (1.064)
  the two profiles are of different devices: /device:TPU:24 before, /device:TPU:32 now
where the time goes in v6:
time: 399 us; the launch traced here: 398 us
  blocking collectives  316 us (79%)
  between operations  28.9 us (7%)
  starting transfers between devices  19.4 us (5%)
  matrix products  10.2 us (3%)
  waiting for transfers between devices  8.2 us (2%)
  local copies, waits for them, and re-layouts  8.02 us (2%)
  other arithmetic  7.07 us (2%)
    all_gather x2, blocking collectives, body(): wide = lax.all_gather(hidden, 'zh', axis=1, tiled=True)  94.6 us
    all_to_all x1, blocking collectives, crossed_weights(): lax.all_to_all(jnp.concatenate([first, rest], axis=1), 'zh', split_axis=0...  91.8 us
    all_gather x1, blocking collectives, body(): lax.all_gather(jnp.concatenate([hidden, tap_rows], axis=0), 'zh', axis=1,...  62.6 us
    all_to_all x3, blocking collectives, body(): terms = lax.all_to_all(partial, 'x', split_axis=0, concat_axis=0)  31.4 us
    psum x3, blocking collectives, body(): squares = lax.psum(jnp.sum(values * values, axis=-1), 'x')  29.3 us
    ppermute x3, starting transfers between devices, rotated(): lax.ppermute(value, axis, [(source, (source + steps) % count) for source...  11.6 us
    dot_general x3, matrix products, body(): jnp.einsum('tk,xkn->xtn', gated, tile, preferred_element_type=jnp.float32)  10.2 us
    ppermute x3, waiting for transfers between devices, body(): before = lax.ppermute(wide[row_count - REACH:], PLACE, forward)  8.16 us
  transfers between devices with their start and end apart: 8, of which 3 were waited for; matrix products, arithmetic and copies ran while one was open for 2% of the time, Pallas kernels for 0%

profile of v6, /device:TPU:32, one launch (start us, length us, event | category | flops | bytes accessed | tf_op | source)
XLA Modules:
  0.0 398.0 jit_solution(5047769516387131457)
XLA Ops:
  6.5 1.0 constant_dynamic-slice_fusion.1
  7.5 0.2 reshape.140
  7.7 0.2 copy.61
  7.9 1.0 constant_dynamic-slice_fusion
  8.9 0.2 copy.86
  9.1 0.1 pad_maximum_fusion.5
  9.2 91.8 %all_to_all.20 = bf16[4,256,256]{1,2,0:T(8,128)(2,1)S(1)} all-to-all(bf16[4,256,256]{1,2,0:T(8,128)(2,1)S(1)} %pad_maximum_fusion.5), channel_id=1, replica_groups=mesh['y'=4,'zl'=8,'c'=2,'x'=4,'zh'=4] {'zh'}, dimensions={0} | all-to-all | bytes 1048576 | tf_op jit(solution)/shard_map/all_to_all | solution.py:39
  100.9 0.1 fusion.53
  101.0 0.8 copy.62
  101.9 2.2 all_gather.25
  104.1 0.2 copy.66
  104.3 3.5 collective-permute-start
  107.8 4.8 %collective-permute-start.1 = (bf16[1024,256]{1,0:T(8,128)(2,1)S(1)}, bf16[1024,256]{1,0:T(8,128)(2,1)}, u32[]{:S(2)}, u32[]{:S(2)}) collective-permute-start(bf16[1024,256]{1,0:T(8,128)(2,1)S(1)} %bitcast.102), channel_id=1, source_target_pairs={{0,512},{256,768},{512,0},{768,256},{1,513},{257,769},{513,1},{769... | collective-permute-start | bytes 1572872 | tf_op jit(solution)/shard_map/ppermute | solution.py:14
  112.6 3.3 collective-permute-start.2
  115.9 0.1 copy.64
  116.0 0.1 copy.63
  116.2 1.9 collective-permute-start.3
  118.1 62.6 %all_gather.24 = bf16[288,1024]{0,1:T(8,128)(2,1)S(1)} all-gather(bf16[288,256]{0,1:T(8,128)(2,1)S(1)} %fusion.38), channel_id=1, replica_groups=mesh['y'=4,'zl'=8,'c'=2,'x'=4,'zh'=4] {'zh'}, dimensions={1}, use_global_device_ids=true | all-gather | bytes 737280 | tf_op jit(solution)/shard_map/all_gather | solution.py:65
  180.8 1.8 pad_maximum_fusion
  182.6 1.0 select_bitcast_fusion.1
  183.6 0.1 pad_maximum_fusion.6
  183.7 2.2 all-gather
  185.9 2.2 all-gather.1
  188.1 1.1 pad_maximum_fusion.1
  189.1 0.0 all-gather.5.cloned.1.call-update
  189.1 0.7 fusion.55
  195.0 0.2 slice_add_fusion
  195.2 0.2 copy.68
  195.4 0.1 slice.129
  195.5 2.0 collective-permute-start.4
  197.6 0.6 fusion.54
  198.2 6.7 %collective-permute-done.4 = bf16[64,1024]{0,1:T(8,128)(2,1)S(1)} collective-permute-done((bf16[64,1024]{0,1:T(8,128)(2,1)S(1)}, bf16[64,1024]{0,1:T(8,128)(2,1)S(1)}, u32[]{:S(2)}, u32[]{:S(2)}) %collective-permute-start.4) | collective-permute-done | bytes 131104 | tf_op jit(solution)/shard_map/ppermute | solution.py:78
  205.0 0.4 fusion.2
  205.4 10.5 %psum.21 = f32[320]{0:T(512)S(1)} all-reduce(f32[320]{0:T(512)S(1)} %fusion.2), channel_id=1, replica_groups=mesh['y'=4,'zl'=8,'c'=2,'x'=4,'zh'=4] {'x'}, use_global_device_ids=true, to_apply=%region_1.2 | all-reduce | flops 320 | bytes 2560 | tf_op jit(solution)/shard_map/psum | solution.py:80
  215.9 0.4 fusion.40
  216.3 2.4 fusion.7
  218.7 0.6 gather_fusion
  219.3 10.5 %all_to_all.21 = bf16[4,256,256]{1,2,0:T(8,128)(2,1)S(1)} all-to-all(bf16[4,256,256]{1,2,0:T(8,128)(2,1)S(1)} %gather_fusion), channel_id=1, replica_groups=mesh['y'=4,'zl'=8,'c'=2,'x'=4,'zh'=4] {'x'}, dimensions={0} | all-to-all | bytes 1048576 | tf_op jit(solution)/shard_map/all_to_all | solution.py:92
  229.8 0.1 convert_reduce_fusion.2
  229.9 44.9 %all_gather.30 = bf16[256,1024]{0,1:T(8,128)(2,1)S(1)} all-gather(bf16[256,256]{0,1:T(8,128)(2,1)S(1)} %add_convert_fusion.2), channel_id=1, replica_groups=mesh['y'=4,'zl'=8,'c'=2,'x'=4,'zh'=4] {'zh'}, dimensions={1}, use_global_device_ids=true | all-gather | bytes 655360 | tf_op jit(solution)/shard_map/all_gather | solution.py:77
  274.8 0.1 slice.177
  274.9 1.9 collective-permute-start.5
  281.9 0.7 collective-permute-done.5
  282.6 0.4 fusion.3
  283.1 9.7 %psum.22 = f32[320]{0:T(512)S(1)} all-reduce(f32[320]{0:T(512)S(1)} %fusion.3), channel_id=1, replica_groups=mesh['y'=4,'zl'=8,'c'=2,'x'=4,'zh'=4] {'x'}, use_global_device_ids=true, to_apply=%region_4.5 | all-reduce | flops 320 | bytes 2560 | tf_op jit(solution)/shard_map/psum | solution.py:80
  292.8 0.4 fusion.41
  293.2 0.0 all-gather.5.cloned.1.call-done
  293.2 0.2 copy-done.5
  293.4 0.0 copy-done.6
  293.5 3.9 fusion.9
  297.4 10.5 %all_to_all.22 = bf16[4,256,256]{1,2,0:T(8,128)(2,1)S(1)} all-to-all(bf16[4,256,256]{1,2,0:T(8,128)(2,1)S(1)} %fusion.9), channel_id=1, replica_groups=mesh['y'=4,'zl'=8,'c'=2,'x'=4,'zh'=4] {'x'}, dimensions={0} | all-to-all | bytes 1048576 | tf_op jit(solution)/shard_map/all_to_all | solution.py:92
  307.8 0.1 convert_reduce_fusion.1
  307.9 49.7 %all_gather.31 = bf16[256,1024]{0,1:T(8,128)(2,1)S(1)} all-gather(bf16[256,256]{0,1:T(8,128)(2,1)S(1)} %add_convert_fusion.1), channel_id=1, replica_groups=mesh['y'=4,'zl'=8,'c'=2,'x'=4,'zh'=4] {'zh'}, dimensions={1}, use_global_device_ids=true | all-gather | bytes 655360 | tf_op jit(solution)/shard_map/all_gather | solution.py:77
  357.6 0.1 slice.184
  357.8 1.9 collective-permute-start.6
  364.7 0.7 collective-permute-done.6
  365.4 0.4 fusion.4
  365.9 9.1 %psum.23 = f32[320]{0:T(512)S(1)} all-reduce(f32[320]{0:T(512)S(1)} %fusion.4), channel_id=1, replica_groups=mesh['y'=4,'zl'=8,'c'=2,'x'=4,'zh'=4] {'x'}, use_global_device_ids=true, to_apply=%region_7.8 | all-reduce | flops 320 | bytes 2560 | tf_op jit(solution)/shard_map/psum | solution.py:80
  375.0 0.4 fusion.42
  375.4 0.3 copy-done.4
  375.7 3.9 fusion.8
  379.6 10.5 %all_to_all.23 = bf16[4,256,256]{1,2,0:T(8,128)(2,1)S(1)} all-to-all(bf16[4,256,256]{1,2,0:T(8,128)(2,1)S(1)} %fusion.8), channel_id=1, replica_groups=mesh['y'=4,'zl'=8,'c'=2,'x'=4,'zh'=4] {'x'}, dimensions={0} | all-to-all | bytes 1048576 | tf_op jit(solution)/shard_map/all_to_all | solution.py:92
  390.1 0.1 convert_reduce_fusion
  390.3 0.9 copy.76
  (39 shorter events, 0.5 us)
Async XLA Ops:
  6.5 286.7 %all-gather.5.cloned.1.call-start = ((), (), s32[]{:S(2)}) async-start(), calls=%async_computation.4 | async-start | bytes 5242880 | tf_op jit(solution)/shard_map/all_gather | solution.py:75
  100.9 14.9 %copy-start.3 = (f32[3,4,256]{2,1,0:T(4,128)S(1)}, f32[3,4,256]{2,1,0:T(4,128)}, u32[]{:S(2)}) copy-start(f32[3,4,256]{2,1,0:T(4,128)} %param.6) | copy-start | bytes 36868
  100.9 15.1 %copy-start.1 = (bf16[256,256]{1,0:T(8,128)(2,1)S(1)}, bf16[256,256]{1,0:T(8,128)(2,1)}, u32[]{:S(2)}) copy-start(bf16[256,256]{1,0:T(8,128)(2,1)} %param.4) | copy-start | bytes 393220
  104.3 76.5 %copy-start = (bf16[4,256,256]{2,1,0:T(8,128)(2,1)}, bf16[4,256,256]{2,1,0:T(8,128)(2,1)S(1)}, u32[]{:S(2)}) copy-start(bf16[4,256,256]{2,1,0:T(8,128)(2,1)S(1)} %copy.66) | copy-start | bytes 1572868
  104.3 76.5 %collective-permute-start = (bf16[1024,256]{1,0:T(8,128)(2,1)S(1)}, bf16[1024,256]{1,0:T(8,128)(2,1)}, u32[]{:S(2)}, u32[]{:S(2)}) collective-permute-start(bf16[1024,256]{1,0:T(8,128)(2,1)S(1)} %bitcast.101), channel_id=1, source_target_pairs={{0,256},{256,512},{512,768},{768,0},{1,257},{257,513},{513,769},{7... | collective-permute-start | bytes 1572872 | tf_op jit(solution)/shard_map/ppermute | solution.py:14
  107.8 73.0 %collective-permute-start.1 = (bf16[1024,256]{1,0:T(8,128)(2,1)S(1)}, bf16[1024,256]{1,0:T(8,128)(2,1)}, u32[]{:S(2)}, u32[]{:S(2)}) collective-permute-start(bf16[1024,256]{1,0:T(8,128)(2,1)S(1)} %bitcast.102), channel_id=1, source_target_pairs={{0,512},{256,768},{512,0},{768,256},{1,513},{257,769},{513,1},{769... | collective-permute-start | bytes 1572872 | tf_op jit(solution)/shard_map/ppermute | solution.py:14
  112.6 68.2 %collective-permute-start.2 = (bf16[1024,256]{1,0:T(8,128)(2,1)S(1)}, bf16[1024,256]{1,0:T(8,128)(2,1)}, u32[]{:S(2)}, u32[]{:S(2)}) collective-permute-start(bf16[1024,256]{1,0:T(8,128)(2,1)S(1)} %bitcast.103), channel_id=1, source_target_pairs={{0,768},{256,0},{512,256},{768,512},{1,769},{257,1},{513,257},{769... | collective-permute-start | bytes 1572872 | tf_op jit(solution)/shard_map/ppermute | solution.py:14
  116.2 66.4 %collective-permute-start.3 = (bf16[4,2,64,256]{3,2,1,0:T(8,128)(2,1)}, bf16[4,2,64,256]{3,2,1,0:T(8,128)(2,1)S(1)}, u32[]{:S(2)}, u32[]{:S(2)}) collective-permute-start(bf16[4,2,64,256]{3,2,1,0:T(8,128)(2,1)} %bitcast.4), channel_id=1, source_target_pairs={{0,32},{32,0},{64,96},{96,64},{128,160},{160,128},{192,224},{224,1... | collective-permute-start | bytes 786440 | tf_op jit(solution)/shard_map/ppermute | solution.py:50
  188.1 1.1 copy-start.2
  195.5 9.4 %collective-permute-start.4 = (bf16[64,1024]{0,1:T(8,128)(2,1)S(1)}, bf16[64,1024]{0,1:T(8,128)(2,1)S(1)}, u32[]{:S(2)}, u32[]{:S(2)}) collective-permute-start(bf16[64,1024]{0,1:T(8,128)(2,1)S(1)} %slice.129), channel_id=1, source_target_pairs={{0,16},{1,17},{2,18},{3,19},{16,32},{17,33},{18,34},{19,35},{32,48... | collective-permute-start | bytes 393224 | tf_op jit(solution)/shard_map/ppermute | solution.py:78
  274.9 7.7 %collective-permute-start.5 = (bf16[64,1024]{0,1:T(8,128)(2,1)S(1)}, bf16[64,1024]{0,1:T(8,128)(2,1)S(1)}, u32[]{:S(2)}, u32[]{:S(2)}) collective-permute-start(bf16[64,1024]{0,1:T(8,128)(2,1)S(1)} %slice.177), channel_id=1, source_target_pairs={{0,16},{1,17},{2,18},{3,19},{16,32},{17,33},{18,34},{19,35},{32,48... | collective-permute-start | bytes 393224 | tf_op jit(solution)/shard_map/ppermute | solution.py:78
  292.8 0.7 copy-start.5
  292.8 0.7 copy-start.6
  292.8 0.7 copy-start.7
  292.8 0.7 copy-start.8
  357.8 7.7 %collective-permute-start.6 = (bf16[64,1024]{0,1:T(8,128)(2,1)S(1)}, bf16[64,1024]{0,1:T(8,128)(2,1)S(1)}, u32[]{:S(2)}, u32[]{:S(2)}) collective-permute-start(bf16[64,1024]{0,1:T(8,128)(2,1)S(1)} %slice.184), channel_id=1, source_target_pairs={{0,16},{1,17},{2,18},{3,19},{16,32},{17,33},{18,34},{19,35},{32,48... | collective-permute-start | bytes 393224 | tf_op jit(solution)/shard_map/ppermute | solution.py:78
  375.0 0.7 copy-start.4
Sparse Core Ops, SparseCore 0:
  189.3 63.8 all-gather.4

commit v7 on v5

--- a/solution.py
+++ b/solution.py
@@ -26,6 +26,18 @@
     return list(zip(places[:-1], places[1:]))
 
 
+def first_halo_pairs(n_y, n_zl, n_c, n_zh):
+    n_zp = n_zl // 2
+    pairs = []
+    for section in range(n_y * n_zl * n_c - 1):
+        zl, c = (section + 1) // n_c % n_zl, (section + 1) % n_c
+        y = (section + 1) // (n_c * n_zl)
+        for zh in range(n_zh):
+            target = (((y * 2 + zl % 2) * n_zp + zh) * n_c + c) * n_zh + zl // 2
+            pairs.append((section * n_zh + zh, target))
+    return pairs
+
+
 def rotated(value, axis, steps):
     count = lax.axis_size(axis)
     return lax.ppermute(value, axis, [(source, (source + steps) % count) for source in range(count)])
@@ -43,6 +55,8 @@
     forward = halo_pairs(n_y, n_zl, n_c, n_zh)
 
     hidden = lax.ppermute(signal, MOVED, there)
+    before = lax.ppermute(signal[row_count - REACH :], SECTION + ("zh",), first_halo_pairs(n_y, n_zl, n_c, n_zh))
+    starts = (REACH - offsets).astype(jnp.uint32)
 
     half = width // n_c
     share = lax.dynamic_slice(mixing, (0, c * half, (y * n_zh + zp) * width), (layers, half, width))
@@ -59,30 +73,36 @@
         axis=0,
     )
     got = lax.all_gather(sent, "zh", axis=0)
-    hidden, got = lax.optimization_barrier((hidden, got))
+    hidden, before, got = lax.optimization_barrier((hidden, before, got))
     coeffs = got[:, layers * half :].astype(jnp.float32)
     coeffs = coeffs[:, :n_tap_rows] + coeffs[:, n_tap_rows : 2 * n_tap_rows]
     coeffs = coeffs.transpose(1, 0, 2).reshape(layers, n_taps, n_zh * width)
-    first = lax.all_gather(got[:, :half], "c", axis=1, tiled=True).reshape(n_zh * width, width)
-    hidden, first = lax.optimization_barrier((hidden, first))
-    first = jnp.stack([first] + [rotated(first, "y", k) for k in range(1, n_y)])
-    rest = [got[:, layer * half : (layer + 1) * half] for layer in range(1, layers)]
+    whole = [
+        lax.all_gather(got[:, layer * half : (layer + 1) * half], "c", axis=1, tiled=True).reshape(n_zh * width, width)
+        for layer in range(layers)
+    ]
+    hidden, whole = lax.optimization_barrier((hidden, whole))
+    turned = [whole[0]] + [rotated(whole[0], "y", k) for k in range(1, n_y)]
+    rest = jnp.stack(whole[1:])
     entry_of = (y - jnp.arange(n_x)) % n_y
     returned = []
     for layer in range(layers):
-        wide = lax.all_gather(hidden, "zp", axis=1, tiled=True)
-        before = lax.ppermute(wide[row_count - REACH :], PLACE, forward)
-        values = jnp.concatenate([before, wide], axis=0).astype(jnp.float32)
+        if layer > 0:
+            before = lax.ppermute(hidden[row_count - REACH :], PLACE, forward)
+        wide = lax.all_gather(jnp.concatenate([before, hidden], axis=0), "zp", axis=1, tiled=True)
+        if layer == 0:
+            wide, turned[1], turned[3], rest = lax.optimization_barrier((wide, turned[1], turned[3], rest))
+            later = lax.all_gather(rest, "y", axis=0)
+        values = wide.astype(jnp.float32)
         squares = lax.psum(jnp.sum(values * values, axis=-1), "x")
         if layer == 0:
-            squares, rest = lax.optimization_barrier((squares, rest))
-            rest = [lax.all_gather(part, "c", axis=1, tiled=True).reshape(n_zh * width, width) for part in rest]
-            later = lax.all_gather(jnp.stack(rest), "y", axis=0)
+            squares, turned[2] = lax.optimization_barrier((squares, turned[2]))
+            first = jnp.stack(turned)
         normed = values * lax.rsqrt(squares / total_channels + 1e-06)[:, None]
         stored = normed.astype(jnp.bfloat16)
         conv = jnp.zeros((row_count, values.shape[1]), jnp.float32)
         for k in range(n_taps):
-            window = lax.dynamic_slice_in_dim(stored, REACH - offsets[layer, k], row_count, 0)
+            window = lax.dynamic_slice(stored, (starts[layer, k], jnp.uint32(0)), (row_count, stored.shape[1]))
             conv = conv + coeffs[layer, k] * window.astype(jnp.float32)
         gated = (conv * jax.nn.silu(normed[REACH:])).astype(jnp.bfloat16)
         tile = first if layer == 0 else later[:, layer - 1]
@@ -90,8 +110,9 @@
         if layer == 0:
             partial = partial[entry_of]
         else:
-            returned.append(lax.ppermute(hidden, MOVED, back))
-            partial, returned[-1] = lax.optimization_barrier((partial, returned[-1]))
+            ready, _ = lax.optimization_barrier((hidden, before))
+            partial, home = lax.optimization_barrier((partial, lax.ppermute(ready, MOVED, back)))
+            returned.append(home)
         terms = lax.all_to_all(partial, "x", split_axis=0, concat_axis=0)
         mixed = jnp.sum(terms.astype(jnp.float32), axis=0)
         hidden = (hidden.astype(jnp.float32) + mixed).astype(jnp.bfloat16)

time: 397 us -> 360 us (0.907)
  the two profiles are of different devices: /device:TPU:240 before, /device:TPU:136 now
where the time goes in v7:
time: 360 us
  blocking collectives  233 us (65%)
  starting transfers between devices  44.9 us (12%)
  waiting for transfers between devices  40.3 us (11%)
  matrix products  18.5 us (5%)
  between operations  13.7 us (4%)
  local copies, waits for them, and re-layouts  4.87 us (1%)
  other arithmetic  3.95 us (1%)
    all_gather x3, blocking collectives, body(): lax.all_gather(jnp.concatenate([before, hidden], axis=0), 'zp', axis=1, t...  105 us
    all_gather x1, blocking collectives, body(): got = lax.all_gather(sent, 'zh', axis=0)  62.4 us
    all_to_all x3, blocking collectives, body(): terms = lax.all_to_all(partial, 'x', split_axis=0, concat_axis=0)  31.4 us
    psum x3, blocking collectives, body(): squares = lax.psum(jnp.sum(values * values, axis=-1), 'x')  28.3 us
    ppermute x1, waiting for transfers between devices, body(): returned.append(lax.ppermute(hidden, MOVED, back))  25 us
    ppermute x1, starting transfers between devices, body(): hidden = lax.ppermute(signal, MOVED, there)  22.3 us
    dot_general x3, matrix products, body(): jnp.einsum('tk,xkn->xtn', gated, tile, preferred_element_type=jnp.float32)  18.5 us
    ppermute x2, waiting for transfers between devices, body(): before = lax.ppermute(hidden[row_count - REACH:], PLACE, forward)  15.2 us
  transfers between devices with their start and end apart: 11, of which 3 were waited for; matrix products, arithmetic and copies ran while one was open for 7% of the time, Pallas kernels for 0%

profile of v7, /device:TPU:136, one launch (start us, length us, event | category | flops | bytes accessed | tf_op | source)
XLA Modules:
  0.0 359.6 jit_solution(9841815391578173711)
XLA Ops:
  6.5 1.0 copy.11
  7.5 22.3 %collective-permute-start = (bf16[256,256]{0,1:T(8,128)(2,1)S(1)}, bf16[256,256]{0,1:T(8,128)(2,1)S(1)}, u32[]{:S(2)}, u32[]{:S(2)}) collective-permute-start(bf16[256,256]{0,1:T(8,128)(2,1)S(1)} %copy.11), channel_id=1, source_target_pairs={{0,0},{1,32},{2,64},{3,96},{32,128},{33,160},{34,192},{35,224},{64... | collective-permute-start | bytes 393224 | tf_op jit(solution)/shard_map/ppermute | solution.py:57
  29.9 0.1 slice.154
  30.0 1.9 collective-permute-start.1
  31.9 0.7 reduce-precision_convert_fusion
  32.7 0.1 pad.18.clone
  32.8 0.9 constant_dynamic-slice_fusion
  33.7 0.1 maximum_maximum_fusion
  33.8 62.4 %all-gather = bf16[1664,256]{1,0:T(8,128)(2,1)S(1)} all-gather(bf16[416,256]{1,0:T(8,128)(2,1)S(1)} %maximum_maximum_fusion), channel_id=2, replica_groups=mesh['y'=4,'zq'=2,'zp'=4,'c'=2,'x'=4,'zh'=4] {'zh'}, dimensions={0}, use_global_device_ids=true | all-gather | bytes 1064960 | tf_op jit(solution)/shard_map/all_gather | solution.py:75
  96.2 0.0 collective-permute-done.1
  96.2 0.0 collective-permute-done
  96.2 0.1 fusion.64
  96.3 2.2 all_gather.32
  98.5 0.2 copy.24
  98.7 2.2 all_gather.33
  100.8 2.2 all_gather.34
  103.0 3.5 collective-permute-start.2
  106.5 2.4 collective-permute-start.3
  108.9 0.1 pad_maximum_fusion.2
  109.0 0.0 copy-start
  109.0 1.1 pad_maximum_fusion
  110.1 42.1 %all_gather.35 = bf16[320,1024]{0,1:T(8,128)(2,1)S(1)} all-gather(bf16[320,256]{0,1:T(8,128)(2,1)S(1)} %pad_maximum_fusion.2), channel_id=1, replica_groups=mesh['y'=4,'zq'=2,'zp'=4,'c'=2,'x'=4,'zh'=4] {'zp'}, dimensions={1}, use_global_device_ids=true | all-gather | bytes 819200 | tf_op jit(solution)/shard_map/all_gather | solution.py:92
  152.2 0.0 collective-permute-done.2
  152.2 0.0 collective-permute-done.3
  152.2 0.0 all-gather.4.cloned.1.call-update
  152.3 0.7 fusion.66
  152.9 5.2 %collective-permute-start.4 = (bf16[1024,256]{0,1:T(8,128)(2,1)S(1)}, bf16[1024,256]{0,1:T(8,128)(2,1)}, u32[]{:S(2)}, u32[]{:S(2)}) collective-permute-start(bf16[1024,256]{0,1:T(8,128)(2,1)S(1)} %copy.24), channel_id=1, source_target_pairs={{0,512},{256,768},{512,0},{768,256},{1,513},{257,769},{513,1},{769... | collective-permute-start | bytes 1572872 | tf_op jit(solution)/shard_map/ppermute | solution.py:43
  158.3 0.2 fusion.10
  158.5 10.5 %psum.21 = f32[320]{0:T(512)S(1)} all-reduce(f32[320]{0:T(512)S(1)} %fusion.10), channel_id=1, replica_groups=mesh['y'=4,'zq'=2,'zp'=4,'c'=2,'x'=4,'zh'=4] {'x'}, use_global_device_ids=true, to_apply=%region_1.2 | all-reduce | flops 320 | bytes 2560 | tf_op jit(solution)/shard_map/psum | solution.py:97
  169.0 0.0 collective-permute-done.4
  169.0 0.2 fusion.50
  169.2 5.7 %fusion.18 = bf16[4,256,256]{1,2,0:T(8,128)(2,1)S(1)} fusion(bf16[1,1024,256]{1,2,0:T(8,128)(2,1)} %bitcast.14, bf16[1,1024,256]{1,2,0:T(8,128)(2,1)} %bitcast.13, bf16[1,1024,256]{1,2,0:T(8,128)(2,1)S(1)} %bitcast.98, bf16[1,1024,256]{1,2,0:T(8,128)(2,1)S(1)} %bitcast.80, f32[320,1024]{0,1:T(8,128)S(1)} %get-tuple-element.51, ...), kind=kOutput, calls=%fused_computation.25 | convolution fusion | flops 544735232 | bytes 5783568 | tf_op jit(solution)/shard_map/tk,xkn->xtn/dot_general | solution.py:109
  174.9 0.6 gather_fusion
  175.5 10.5 %all_to_all.15 = bf16[4,256,256]{1,2,0:T(8,128)(2,1)S(1)} all-to-all(bf16[4,256,256]{1,2,0:T(8,128)(2,1)S(1)} %gather_fusion), channel_id=1, replica_groups=mesh['y'=4,'zq'=2,'zp'=4,'c'=2,'x'=4,'zh'=4] {'x'}, dimensions={0} | all-to-all | bytes 1048576 | tf_op jit(solution)/shard_map/all_to_all | solution.py:116
  186.0 0.1 convert_reduce_fusion.2
  186.1 0.1 slice.164
  186.2 1.9 collective-permute-start.5
  188.1 7.6 %collective-permute-done.5 = bf16[64,256]{0,1:T(8,128)(2,1)S(1)} collective-permute-done((bf16[64,256]{0,1:T(8,128)(2,1)S(1)}, bf16[64,256]{0,1:T(8,128)(2,1)S(1)}, u32[]{:S(2)}, u32[]{:S(2)}) %collective-permute-start.5) | collective-permute-done | bytes 32800 | tf_op jit(solution)/shard_map/ppermute | solution.py:91
  195.7 1.9 collective-permute-start.6
  197.6 0.1 pad_maximum_fusion.3
  197.7 29.3 %all_gather.38 = bf16[320,1024]{0,1:T(8,128)(2,1)S(1)} all-gather(bf16[320,256]{0,1:T(8,128)(2,1)S(1)} %pad_maximum_fusion.3), channel_id=1, replica_groups=mesh['y'=4,'zq'=2,'zp'=4,'c'=2,'x'=4,'zh'=4] {'zp'}, dimensions={1}, use_global_device_ids=true | all-gather | bytes 819200 | tf_op jit(solution)/shard_map/all_gather | solution.py:92
  227.1 0.2 fusion.11
  227.3 8.9 %psum.22 = f32[320]{0:T(512)S(1)} all-reduce(f32[320]{0:T(512)S(1)} %fusion.11), channel_id=1, replica_groups=mesh['y'=4,'zq'=2,'zp'=4,'c'=2,'x'=4,'zh'=4] {'x'}, use_global_device_ids=true, to_apply=%region_4.5 | all-reduce | flops 320 | bytes 2560 | tf_op jit(solution)/shard_map/psum | solution.py:97
  236.2 0.2 fusion.51
  236.4 0.0 all-gather.4.cloned.1.call-done
  236.4 6.4 %fusion.22 = bf16[4,256,256]{1,2,0:T(8,128)(2,1)S(1)} fusion(bf16[4,2,1024,256]{3,2,1,0:T(8,128)(2,1)} %bitcast.96, f32[320,1024]{0,1:T(8,128)S(1)} %get-tuple-element.49, bf16[320,1024]{0,1:T(8,128)(2,1)S(1)} %get-tuple-element.48, u32[]{:T(128)} %bitcast.32, f32[1024]{0:T(1024)S(1)} %bitcast.88, u32[]{:T(128)} %bitcast.30, f32[1024]{0:T(1024)S(1)} %bitcast.89, ...), kind=kOutput, calls=%fused_computation.27 | convolution fusion | flops 541589504 | bytes 5785600 | tf_op jit(solution)/shard_map/tk,xkn->xtn/dot_general | solution.py:109
  242.8 10.5 %all_to_all.16 = bf16[4,256,256]{1,2,0:T(8,128)(2,1)S(1)} all-to-all(bf16[4,256,256]{1,2,0:T(8,128)(2,1)S(1)} %fusion.22), channel_id=1, replica_groups=mesh['y'=4,'zq'=2,'zp'=4,'c'=2,'x'=4,'zh'=4] {'x'}, dimensions={0} | all-to-all | bytes 1048576 | tf_op jit(solution)/shard_map/all_to_all | solution.py:116
  253.3 0.1 convert_reduce_fusion.1
  253.4 0.1 slice.171
  253.5 1.9 collective-permute-start.7
  255.4 7.6 %collective-permute-done.7 = bf16[64,256]{0,1:T(8,128)(2,1)S(1)} collective-permute-done((bf16[64,256]{0,1:T(8,128)(2,1)S(1)}, bf16[64,256]{0,1:T(8,128)(2,1)S(1)}, u32[]{:S(2)}, u32[]{:S(2)}) %collective-permute-start.7) | collective-permute-done | bytes 32800 | tf_op jit(solution)/shard_map/ppermute | solution.py:91
  263.1 1.9 collective-permute-start.8
  265.0 0.1 pad_maximum_fusion.4
  265.1 33.3 %all_gather.39 = bf16[320,1024]{0,1:T(8,128)(2,1)S(1)} all-gather(bf16[320,256]{0,1:T(8,128)(2,1)S(1)} %pad_maximum_fusion.4), channel_id=1, replica_groups=mesh['y'=4,'zq'=2,'zp'=4,'c'=2,'x'=4,'zh'=4] {'zp'}, dimensions={1}, use_global_device_ids=true | all-gather | bytes 819200 | tf_op jit(solution)/shard_map/all_gather | solution.py:92
  298.4 0.2 fusion.12
  298.6 8.9 %psum.23 = f32[320]{0:T(512)S(1)} all-reduce(f32[320]{0:T(512)S(1)} %fusion.12), channel_id=1, replica_groups=mesh['y'=4,'zq'=2,'zp'=4,'c'=2,'x'=4,'zh'=4] {'x'}, use_global_device_ids=true, to_apply=%region_7.8 | all-reduce | flops 320 | bytes 2560 | tf_op jit(solution)/shard_map/psum | solution.py:97
  307.5 0.2 fusion.52
  307.7 6.4 %fusion.21 = bf16[4,256,256]{1,2,0:T(8,128)(2,1)S(1)} fusion(bf16[4,2,1024,256]{3,2,1,0:T(8,128)(2,1)} %bitcast.97, f32[320,1024]{0,1:T(8,128)S(1)} %get-tuple-element.47, bf16[320,1024]{0,1:T(8,128)(2,1)S(1)} %get-tuple-element.46, u32[]{:T(128)} %bitcast.44, f32[1024]{0:T(1024)S(1)} %bitcast.85, u32[]{:T(128)} %bitcast.42, f32[1024]{0:T(1024)S(1)} %bitcast.86, ...), kind=kOutput, calls=%fused_computation.26 | convolution fusion | flops 541589504 | bytes 5785600 | tf_op jit(solution)/shard_map/tk,xkn->xtn/dot_general | solution.py:109
  314.2 0.0 collective-permute-done.8
  314.2 10.5 %all_to_all.17 = bf16[4,256,256]{1,2,0:T(8,128)(2,1)S(1)} all-to-all(bf16[4,256,256]{1,2,0:T(8,128)(2,1)S(1)} %fusion.21), channel_id=1, replica_groups=mesh['y'=4,'zq'=2,'zp'=4,'c'=2,'x'=4,'zh'=4] {'x'}, dimensions={0} | all-to-all | bytes 1048576 | tf_op jit(solution)/shard_map/all_to_all | solution.py:116
  324.7 0.1 convert_reduce_fusion
  324.8 1.9 collective-permute-start.9
  326.7 25.0 %collective-permute-done.9 = bf16[256,256]{0,1:T(8,128)(2,1)S(1)} collective-permute-done((bf16[256,256]{0,1:T(8,128)(2,1)S(1)}, bf16[256,256]{0,1:T(8,128)(2,1)S(1)}, u32[]{:S(2)}, u32[]{:S(2)}) %collective-permute-start.9) | collective-permute-done | bytes 131104 | tf_op jit(solution)/shard_map/ppermute | solution.py:119
  351.8 0.9 copy.20
  (21 shorter events, 0.4 us)
Async XLA Ops:
  6.5 229.9 %all-gather.4.cloned.1.call-start = ((), (), s32[]{:S(2)}) async-start(), calls=%async_computation.3 | async-start | bytes 5242880 | tf_op jit(solution)/shard_map/all_gather | solution.py:95
  7.5 88.7 %collective-permute-start = (bf16[256,256]{0,1:T(8,128)(2,1)S(1)}, bf16[256,256]{0,1:T(8,128)(2,1)S(1)}, u32[]{:S(2)}, u32[]{:S(2)}) collective-permute-start(bf16[256,256]{0,1:T(8,128)(2,1)S(1)} %copy.11), channel_id=1, source_target_pairs={{0,0},{1,32},{2,64},{3,96},{32,128},{33,160},{34,192},{35,224},{64... | collective-permute-start | bytes 393224 | tf_op jit(solution)/shard_map/ppermute | solution.py:57
  30.0 66.2 %collective-permute-start.1 = (bf16[64,256]{0,1:T(8,128)(2,1)S(1)}, bf16[64,256]{0,1:T(8,128)(2,1)S(1)}, u32[]{:S(2)}, u32[]{:S(2)}) collective-permute-start(bf16[64,256]{0,1:T(8,128)(2,1)S(1)} %slice.154), channel_id=1, source_target_pairs={{0,16},{1,48},{2,80},{3,112},{16,128},{17,160},{18,192},{19,224},{... | collective-permute-start | bytes 98312 | tf_op jit(solution)/shard_map/ppermute | solution.py:58
  103.0 49.2 %collective-permute-start.2 = (bf16[1024,256]{0,1:T(8,128)(2,1)S(1)}, bf16[1024,256]{0,1:T(8,128)(2,1)S(1)}, u32[]{:S(2)}, u32[]{:S(2)}) collective-permute-start(bf16[1024,256]{0,1:T(8,128)(2,1)S(1)} %copy.24), channel_id=1, source_target_pairs={{0,256},{256,512},{512,768},{768,0},{1,257},{257,513},{513,769},{7... | collective-permute-start | bytes 1572872 | tf_op jit(solution)/shard_map/ppermute | solution.py:43
  106.5 45.7 %collective-permute-start.3 = (bf16[1024,256]{0,1:T(8,128)(2,1)S(1)}, bf16[1024,256]{0,1:T(8,128)(2,1)}, u32[]{:S(2)}, u32[]{:S(2)}) collective-permute-start(bf16[1024,256]{0,1:T(8,128)(2,1)S(1)} %copy.24), channel_id=1, source_target_pairs={{0,768},{256,0},{512,256},{768,512},{1,769},{257,1},{513,257},{769... | collective-permute-start | bytes 1572872 | tf_op jit(solution)/shard_map/ppermute | solution.py:43
  109.0 43.2 %copy-start = (s32[3,4]{1,0:T(4,128)S(1)}, s32[3,4]{1,0:T(4,128)}, u32[]{:S(2)}) copy-start(s32[3,4]{1,0:T(4,128)} %param.7) | copy-start | bytes 148
  152.9 16.1 %collective-permute-start.4 = (bf16[1024,256]{0,1:T(8,128)(2,1)S(1)}, bf16[1024,256]{0,1:T(8,128)(2,1)}, u32[]{:S(2)}, u32[]{:S(2)}) collective-permute-start(bf16[1024,256]{0,1:T(8,128)(2,1)S(1)} %copy.24), channel_id=1, source_target_pairs={{0,512},{256,768},{512,0},{768,256},{1,513},{257,769},{513,1},{769... | collective-permute-start | bytes 1572872 | tf_op jit(solution)/shard_map/ppermute | solution.py:43
  186.2 9.5 %collective-permute-start.5 = (bf16[64,256]{0,1:T(8,128)(2,1)S(1)}, bf16[64,256]{0,1:T(8,128)(2,1)S(1)}, u32[]{:S(2)}, u32[]{:S(2)}) collective-permute-start(bf16[64,256]{0,1:T(8,128)(2,1)S(1)} %slice.164), channel_id=1, source_target_pairs={{0,16},{16,128},{128,144},{144,1},{1,17},{17,129},{129,145},{145,2... | collective-permute-start | bytes 98312 | tf_op jit(solution)/shard_map/ppermute | solution.py:91
  195.7 47.1 %collective-permute-start.6 = (bf16[256,256]{0,1:T(8,128)(2,1)S(1)}, bf16[256,256]{0,1:T(8,128)(2,1)S(1)}, u32[]{:S(2)}, u32[]{:S(2)}) collective-permute-start(bf16[256,256]{0,1:T(8,128)(2,1)S(1)} %add_convert_fusion.2), channel_id=1, source_target_pairs={{0,0},{32,1},{64,2},{96,3},{128,32},{160,33},{192,34},{224,35},{1,... | collective-permute-start | bytes 393224 | tf_op jit(solution)/shard_map/ppermute | solution.py:114
  253.5 9.5 %collective-permute-start.7 = (bf16[64,256]{0,1:T(8,128)(2,1)S(1)}, bf16[64,256]{0,1:T(8,128)(2,1)S(1)}, u32[]{:S(2)}, u32[]{:S(2)}) collective-permute-start(bf16[64,256]{0,1:T(8,128)(2,1)S(1)} %slice.171), channel_id=1, source_target_pairs={{0,16},{16,128},{128,144},{144,1},{1,17},{17,129},{129,145},{145,2... | collective-permute-start | bytes 98312 | tf_op jit(solution)/shard_map/ppermute | solution.py:91
  263.1 51.1 %collective-permute-start.8 = (bf16[256,256]{0,1:T(8,128)(2,1)S(1)}, bf16[256,256]{0,1:T(8,128)(2,1)S(1)}, u32[]{:S(2)}, u32[]{:S(2)}) collective-permute-start(bf16[256,256]{0,1:T(8,128)(2,1)S(1)} %add_convert_fusion.1), channel_id=1, source_target_pairs={{0,0},{32,1},{64,2},{96,3},{128,32},{160,33},{192,34},{224,35},{1,... | collective-permute-start | bytes 393224 | tf_op jit(solution)/shard_map/ppermute | solution.py:114
  324.8 26.9 %collective-permute-start.9 = (bf16[256,256]{0,1:T(8,128)(2,1)S(1)}, bf16[256,256]{0,1:T(8,128)(2,1)S(1)}, u32[]{:S(2)}, u32[]{:S(2)}) collective-permute-start(bf16[256,256]{0,1:T(8,128)(2,1)S(1)} %add_convert_fusion), channel_id=1, source_target_pairs={{0,0},{32,1},{64,2},{96,3},{128,32},{160,33},{192,34},{224,35},{1,... | collective-permute-start | bytes 393224 | tf_op jit(solution)/shard_map/ppermute | solution.py:119
Sparse Core Ops, SparseCore 0:
  152.3 57.2 all-gather.3

commit v8 on v7

--- a/solution.py
+++ b/solution.py
@@ -99,18 +99,18 @@
             squares, turned[2] = lax.optimization_barrier((squares, turned[2]))
             first = jnp.stack(turned)
         normed = values * lax.rsqrt(squares / total_channels + 1e-06)[:, None]
-        stored = normed.astype(jnp.bfloat16)
+        stored = lax.optimization_barrier(normed.astype(jnp.bfloat16))
         conv = jnp.zeros((row_count, values.shape[1]), jnp.float32)
         for k in range(n_taps):
             window = lax.dynamic_slice(stored, (starts[layer, k], jnp.uint32(0)), (row_count, stored.shape[1]))
             conv = conv + coeffs[layer, k] * window.astype(jnp.float32)
-        gated = (conv * jax.nn.silu(normed[REACH:])).astype(jnp.bfloat16)
+        gated = lax.optimization_barrier((conv * jax.nn.silu(normed[REACH:])).astype(jnp.bfloat16))
         tile = first if layer == 0 else later[:, layer - 1]
         partial = jnp.einsum("tk,xkn->xtn", gated, tile, preferred_element_type=jnp.float32).astype(jnp.bfloat16)
         if layer == 0:
             partial = partial[entry_of]
         else:
-            ready, _ = lax.optimization_barrier((hidden, before))
+            ready, _ = lax.optimization_barrier((hidden, wide))
             partial, home = lax.optimization_barrier((partial, lax.ppermute(ready, MOVED, back)))
             returned.append(home)
         terms = lax.all_to_all(partial, "x", split_axis=0, concat_axis=0)

time: 360 us -> 349 us (0.969)
  the two profiles are of different devices: /device:TPU:136 before, /device:TPU:160 now
where the time goes in v8:
time: 349 us
  blocking collectives  204 us (58%)
  waiting for transfers between devices  56.6 us (16%)
  starting transfers between devices  46.8 us (13%)
  other arithmetic  17.4 us (5%)
  between operations  13.8 us (4%)
  matrix products  5.12 us (1%)
  local copies, waits for them, and re-layouts  4.87 us (1%)
    all_gather x3, blocking collectives, body(): lax.all_gather(jnp.concatenate([before, hidden], axis=0), 'zp', axis=1, t...  71 us
    all_gather x1, blocking collectives, body(): got = lax.all_gather(sent, 'zh', axis=0)  63.7 us
    all_to_all x3, blocking collectives, body(): terms = lax.all_to_all(partial, 'x', split_axis=0, concat_axis=0)  33.8 us
    psum x3, blocking collectives, body(): squares = lax.psum(jnp.sum(values * values, axis=-1), 'x')  28.9 us
    ppermute x1, waiting for transfers between devices, body(): returned.append(lax.ppermute(hidden, MOVED, back))  23.5 us
    ppermute x1, starting transfers between devices, body(): hidden = lax.ppermute(signal, MOVED, there)  22.8 us
    ppermute x2, waiting for transfers between devices, body(): before = lax.ppermute(hidden[row_count - REACH:], PLACE, forward)  15.9 us
    ppermute x2, waiting for transfers between devices, body(): lax.ppermute(ready, MOVED, back)  15.8 us
  transfers between devices with their start and end apart: 11, of which 6 were waited for; matrix products, arithmetic and copies ran while one was open for 7% of the time, Pallas kernels for 0%

profile of v8, /device:TPU:160, one launch (start us, length us, event | category | flops | bytes accessed | tf_op | source)
XLA Modules:
  0.0 348.6 jit_solution(8506412756021290459)
XLA Ops:
  6.5 1.0 copy.11
  7.5 22.8 %collective-permute-start = (bf16[256,256]{0,1:T(8,128)(2,1)S(1)}, bf16[256,256]{0,1:T(8,128)(2,1)S(1)}, u32[]{:S(2)}, u32[]{:S(2)}) collective-permute-start(bf16[256,256]{0,1:T(8,128)(2,1)S(1)} %copy.11), channel_id=1, source_target_pairs={{0,0},{1,32},{2,64},{3,96},{32,128},{33,160},{34,192},{35,224},{64... | collective-permute-start | bytes 393224 | tf_op jit(solution)/shard_map/ppermute | solution.py:57
  30.4 0.1 slice.154
  30.5 3.7 %collective-permute-start.1 = (bf16[64,256]{0,1:T(8,128)(2,1)S(1)}, bf16[64,256]{0,1:T(8,128)(2,1)S(1)}, u32[]{:S(2)}, u32[]{:S(2)}) collective-permute-start(bf16[64,256]{0,1:T(8,128)(2,1)S(1)} %slice.154), channel_id=1, source_target_pairs={{0,16},{1,48},{2,80},{3,112},{16,128},{17,160},{18,192},{19,224},{... | collective-permute-start | bytes 98312 | tf_op jit(solution)/shard_map/ppermute | solution.py:58
  34.2 0.7 reduce-precision_convert_fusion
  35.0 0.1 pad.18.clone
  35.0 0.9 constant_dynamic-slice_fusion
  36.0 0.1 maximum_maximum_fusion
  36.1 63.7 %all-gather = bf16[1664,256]{1,0:T(8,128)(2,1)S(1)} all-gather(bf16[416,256]{1,0:T(8,128)(2,1)S(1)} %maximum_maximum_fusion), channel_id=2, replica_groups=mesh['y'=4,'zq'=2,'zp'=4,'c'=2,'x'=4,'zh'=4] {'zh'}, dimensions={0}, use_global_device_ids=true | all-gather | bytes 1064960 | tf_op jit(solution)/shard_map/all_gather | solution.py:75
  99.8 0.1 fusion.34
  99.9 2.2 all_gather.32
  102.1 0.2 copy.24
  102.3 2.2 all_gather.33
  104.5 2.2 all_gather.34
  106.6 3.5 collective-permute-start.2
  110.1 3.6 %collective-permute-start.3 = (bf16[1024,256]{0,1:T(8,128)(2,1)S(1)}, bf16[1024,256]{0,1:T(8,128)(2,1)}, u32[]{:S(2)}, u32[]{:S(2)}) collective-permute-start(bf16[1024,256]{0,1:T(8,128)(2,1)S(1)} %copy.24), channel_id=1, source_target_pairs={{0,768},{256,0},{512,256},{768,512},{1,769},{257,1},{513,257},{769... | collective-permute-start | bytes 1572872 | tf_op jit(solution)/shard_map/ppermute | solution.py:43
  113.7 0.1 pad_maximum_fusion.2
  113.8 0.0 copy-start
  113.8 1.1 pad_maximum_fusion
  114.9 36.9 %all_gather.35 = bf16[320,1024]{0,1:T(8,128)(2,1)S(1)} all-gather(bf16[320,256]{0,1:T(8,128)(2,1)S(1)} %pad_maximum_fusion.2), channel_id=1, replica_groups=mesh['y'=4,'zq'=2,'zp'=4,'c'=2,'x'=4,'zh'=4] {'zp'}, dimensions={1}, use_global_device_ids=true | all-gather | bytes 819200 | tf_op jit(solution)/shard_map/all_gather | solution.py:92
  151.8 0.0 all-gather.4.cloned.1.call-update
  151.9 0.7 fusion.36
  152.6 3.4 collective-permute-start.4
  156.1 0.2 fusion.10
  156.4 10.5 %psum.21 = f32[320]{0:T(512)S(1)} all-reduce(f32[320]{0:T(512)S(1)} %fusion.10), channel_id=1, replica_groups=mesh['y'=4,'zq'=2,'zp'=4,'c'=2,'x'=4,'zh'=4] {'x'}, use_global_device_ids=true, to_apply=%region_1.2 | all-reduce | flops 320 | bytes 2560 | tf_op jit(solution)/shard_map/psum | solution.py:97
  166.9 1.4 collective-permute-done.4
  168.2 0.2 fusion.26
  168.4 4.3 %multiply_convert_fusion.2 = bf16[256,1024]{0,1:T(8,128)(2,1)S(1)} fusion(f32[320,1024]{0,1:T(8,128)S(1)} %get-tuple-element.51, bf16[320,1024]{0,1:T(8,128)(2,1)S(1)} %get-tuple-element.50, u32[]{:T(128)} %bitcast.22, f32[1024]{0:T(1024)S(1)} %bitcast.92, u32[]{:T(128)} %bitcast.20, f32[1024]{0:T(1024)S(1)} %bitcast.93, u32[]{:T(128)} %bitcast.18, ...), kind=kLoop, calls=%fused_computation.34 | loop fusion | flops 4456448 | bytes 3686416 | tf_op jit(solution)/shard_map/convert_element_type | solution.py:107
  172.7 2.0 fusion.18
  174.8 0.6 gather_fusion
  175.4 12.2 %all_to_all.15 = bf16[4,256,256]{1,2,0:T(8,128)(2,1)S(1)} all-to-all(bf16[4,256,256]{1,2,0:T(8,128)(2,1)S(1)} %gather_fusion), channel_id=1, replica_groups=mesh['y'=4,'zq'=2,'zp'=4,'c'=2,'x'=4,'zh'=4] {'x'}, dimensions={0} | all-to-all | bytes 1048576 | tf_op jit(solution)/shard_map/all_to_all | solution.py:116
  187.5 0.1 convert_reduce_fusion.2
  187.6 0.1 slice.164
  187.7 1.9 collective-permute-start.5
  189.7 7.7 %collective-permute-done.5 = bf16[64,256]{0,1:T(8,128)(2,1)S(1)} collective-permute-done((bf16[64,256]{0,1:T(8,128)(2,1)S(1)}, bf16[64,256]{0,1:T(8,128)(2,1)S(1)}, u32[]{:S(2)}, u32[]{:S(2)}) %collective-permute-start.5) | collective-permute-done | bytes 32800 | tf_op jit(solution)/shard_map/ppermute | solution.py:91
  197.3 0.1 pad_maximum_fusion.3
  197.4 18.8 %all_gather.38 = bf16[320,1024]{0,1:T(8,128)(2,1)S(1)} all-gather(bf16[320,256]{0,1:T(8,128)(2,1)S(1)} %pad_maximum_fusion.3), channel_id=1, replica_groups=mesh['y'=4,'zq'=2,'zp'=4,'c'=2,'x'=4,'zh'=4] {'zp'}, dimensions={1}, use_global_device_ids=true | all-gather | bytes 819200 | tf_op jit(solution)/shard_map/all_gather | solution.py:92
  216.2 1.9 collective-permute-start.6
  218.1 0.2 fusion.11
  218.3 9.6 %psum.22 = f32[320]{0:T(512)S(1)} all-reduce(f32[320]{0:T(512)S(1)} %fusion.11), channel_id=1, replica_groups=mesh['y'=4,'zq'=2,'zp'=4,'c'=2,'x'=4,'zh'=4] {'x'}, use_global_device_ids=true, to_apply=%region_4.5 | all-reduce | flops 320 | bytes 2560 | tf_op jit(solution)/shard_map/psum | solution.py:97
  227.9 0.2 fusion.27
  228.1 4.4 %multiply_convert_fusion.1 = bf16[256,1024]{0,1:T(8,128)(2,1)S(1)} fusion(f32[320,1024]{0,1:T(8,128)S(1)} %get-tuple-element.49, bf16[320,1024]{0,1:T(8,128)(2,1)S(1)} %get-tuple-element.48, u32[]{:T(128)} %bitcast.32, f32[1024]{0:T(1024)S(1)} %bitcast.88, u32[]{:T(128)} %bitcast.30, f32[1024]{0:T(1024)S(1)} %bitcast.89, u32[]{:T(128)} %bitcast.28, ...), kind=kLoop, calls=%fused_computation.32 | loop fusion | flops 4456448 | bytes 3686416 | tf_op jit(solution)/shard_map/convert_element_type | solution.py:107
  232.5 0.0 all-gather.4.cloned.1.call-done
  232.6 2.3 fusion.22
  234.9 5.7 %collective-permute-done.6 = bf16[256,256]{0,1:T(8,128)(2,1)S(1)} collective-permute-done((bf16[256,256]{0,1:T(8,128)(2,1)S(1)}, bf16[256,256]{0,1:T(8,128)(2,1)S(1)}, u32[]{:S(2)}, u32[]{:S(2)}) %collective-permute-start.6) | collective-permute-done | bytes 131104 | tf_op jit(solution)/shard_map/ppermute | solution.py:114
  240.6 11.1 %all_to_all.16 = bf16[4,256,256]{1,2,0:T(8,128)(2,1)S(1)} all-to-all(bf16[4,256,256]{1,2,0:T(8,128)(2,1)S(1)} %fusion.22), channel_id=1, replica_groups=mesh['y'=4,'zq'=2,'zp'=4,'c'=2,'x'=4,'zh'=4] {'x'}, dimensions={0} | all-to-all | bytes 1048576 | tf_op jit(solution)/shard_map/all_to_all | solution.py:116
  251.7 0.1 convert_reduce_fusion.1
  251.8 0.1 slice.171
  251.9 1.9 collective-permute-start.7
  253.8 8.2 %collective-permute-done.7 = bf16[64,256]{0,1:T(8,128)(2,1)S(1)} collective-permute-done((bf16[64,256]{0,1:T(8,128)(2,1)S(1)}, bf16[64,256]{0,1:T(8,128)(2,1)S(1)}, u32[]{:S(2)}, u32[]{:S(2)}) %collective-permute-start.7) | collective-permute-done | bytes 32800 | tf_op jit(solution)/shard_map/ppermute | solution.py:91
  262.1 0.1 pad_maximum_fusion.4
  262.2 15.4 %all_gather.39 = bf16[320,1024]{0,1:T(8,128)(2,1)S(1)} all-gather(bf16[320,256]{0,1:T(8,128)(2,1)S(1)} %pad_maximum_fusion.4), channel_id=1, replica_groups=mesh['y'=4,'zq'=2,'zp'=4,'c'=2,'x'=4,'zh'=4] {'zp'}, dimensions={1}, use_global_device_ids=true | all-gather | bytes 819200 | tf_op jit(solution)/shard_map/all_gather | solution.py:92
  277.6 0.2 fusion.12
  277.8 2.2 collective-permute-start.8
  280.0 8.9 %psum.23 = f32[320]{0:T(512)S(1)} all-reduce(f32[320]{0:T(512)S(1)} %fusion.12), channel_id=1, replica_groups=mesh['y'=4,'zq'=2,'zp'=4,'c'=2,'x'=4,'zh'=4] {'x'}, use_global_device_ids=true, to_apply=%region_7.8 | all-reduce | flops 320 | bytes 2560 | tf_op jit(solution)/shard_map/psum | solution.py:97
  288.9 0.2 fusion.28
  289.1 4.8 %multiply_convert_fusion = bf16[256,1024]{0,1:T(8,128)(2,1)S(1)} fusion(f32[320,1024]{0,1:T(8,128)S(1)} %get-tuple-element.47, bf16[320,1024]{0,1:T(8,128)(2,1)S(1)} %get-tuple-element.46, u32[]{:T(128)} %bitcast.44, f32[1024]{0:T(1024)S(1)} %bitcast.85, u32[]{:T(128)} %bitcast.42, f32[1024]{0:T(1024)S(1)} %bitcast.86, u32[]{:T(128)} %bitcast.40, ...), kind=kLoop, calls=%fused_computation.30 | loop fusion | flops 4456448 | bytes 3686416 | tf_op jit(solution)/shard_map/convert_element_type | solution.py:107
  293.9 0.8 fusion.21
  294.6 10.1 %collective-permute-done.8 = bf16[256,256]{0,1:T(8,128)(2,1)S(1)} collective-permute-done((bf16[256,256]{0,1:T(8,128)(2,1)S(1)}, bf16[256,256]{0,1:T(8,128)(2,1)S(1)}, u32[]{:S(2)}, u32[]{:S(2)}) %collective-permute-start.8) | collective-permute-done | bytes 131104 | tf_op jit(solution)/shard_map/ppermute | solution.py:114
  304.7 10.5 %all_to_all.17 = bf16[4,256,256]{1,2,0:T(8,128)(2,1)S(1)} all-to-all(bf16[4,256,256]{1,2,0:T(8,128)(2,1)S(1)} %fusion.21), channel_id=1, replica_groups=mesh['y'=4,'zq'=2,'zp'=4,'c'=2,'x'=4,'zh'=4] {'x'}, dimensions={0} | all-to-all | bytes 1048576 | tf_op jit(solution)/shard_map/all_to_all | solution.py:116
  315.2 0.1 convert_reduce_fusion
  315.3 1.9 collective-permute-start.9
  317.2 23.5 %collective-permute-done.9 = bf16[256,256]{0,1:T(8,128)(2,1)S(1)} collective-permute-done((bf16[256,256]{0,1:T(8,128)(2,1)S(1)}, bf16[256,256]{0,1:T(8,128)(2,1)S(1)}, u32[]{:S(2)}, u32[]{:S(2)}) %collective-permute-start.9) | collective-permute-done | bytes 131104 | tf_op jit(solution)/shard_map/ppermute | solution.py:119
  340.8 0.9 copy.20
  (26 shorter events, 0.4 us)
Async XLA Ops:
  6.5 226.0 %all-gather.4.cloned.1.call-start = ((), (), s32[]{:S(2)}) async-start(), calls=%async_computation.3 | async-start | bytes 5242880 | tf_op jit(solution)/shard_map/all_gather | solution.py:95
  7.5 92.3 %collective-permute-start = (bf16[256,256]{0,1:T(8,128)(2,1)S(1)}, bf16[256,256]{0,1:T(8,128)(2,1)S(1)}, u32[]{:S(2)}, u32[]{:S(2)}) collective-permute-start(bf16[256,256]{0,1:T(8,128)(2,1)S(1)} %copy.11), channel_id=1, source_target_pairs={{0,0},{1,32},{2,64},{3,96},{32,128},{33,160},{34,192},{35,224},{64... | collective-permute-start | bytes 393224 | tf_op jit(solution)/shard_map/ppermute | solution.py:57
  30.5 69.4 %collective-permute-start.1 = (bf16[64,256]{0,1:T(8,128)(2,1)S(1)}, bf16[64,256]{0,1:T(8,128)(2,1)S(1)}, u32[]{:S(2)}, u32[]{:S(2)}) collective-permute-start(bf16[64,256]{0,1:T(8,128)(2,1)S(1)} %slice.154), channel_id=1, source_target_pairs={{0,16},{1,48},{2,80},{3,112},{16,128},{17,160},{18,192},{19,224},{... | collective-permute-start | bytes 98312 | tf_op jit(solution)/shard_map/ppermute | solution.py:58
  106.6 45.2 %collective-permute-start.2 = (bf16[1024,256]{0,1:T(8,128)(2,1)S(1)}, bf16[1024,256]{0,1:T(8,128)(2,1)S(1)}, u32[]{:S(2)}, u32[]{:S(2)}) collective-permute-start(bf16[1024,256]{0,1:T(8,128)(2,1)S(1)} %copy.24), channel_id=1, source_target_pairs={{0,256},{256,512},{512,768},{768,0},{1,257},{257,513},{513,769},{7... | collective-permute-start | bytes 1572872 | tf_op jit(solution)/shard_map/ppermute | solution.py:43
  110.1 41.7 %collective-permute-start.3 = (bf16[1024,256]{0,1:T(8,128)(2,1)S(1)}, bf16[1024,256]{0,1:T(8,128)(2,1)}, u32[]{:S(2)}, u32[]{:S(2)}) collective-permute-start(bf16[1024,256]{0,1:T(8,128)(2,1)S(1)} %copy.24), channel_id=1, source_target_pairs={{0,768},{256,0},{512,256},{768,512},{1,769},{257,1},{513,257},{769... | collective-permute-start | bytes 1572872 | tf_op jit(solution)/shard_map/ppermute | solution.py:43
  113.8 38.0 %copy-start = (s32[3,4]{1,0:T(4,128)S(1)}, s32[3,4]{1,0:T(4,128)}, u32[]{:S(2)}) copy-start(s32[3,4]{1,0:T(4,128)} %param.7) | copy-start | bytes 148
  152.6 15.6 %collective-permute-start.4 = (bf16[1024,256]{0,1:T(8,128)(2,1)S(1)}, bf16[1024,256]{0,1:T(8,128)(2,1)}, u32[]{:S(2)}, u32[]{:S(2)}) collective-permute-start(bf16[1024,256]{0,1:T(8,128)(2,1)S(1)} %copy.24), channel_id=1, source_target_pairs={{0,512},{256,768},{512,0},{768,256},{1,513},{257,769},{513,1},{769... | collective-permute-start | bytes 1572872 | tf_op jit(solution)/shard_map/ppermute | solution.py:43
  187.7 9.6 %collective-permute-start.5 = (bf16[64,256]{0,1:T(8,128)(2,1)S(1)}, bf16[64,256]{0,1:T(8,128)(2,1)S(1)}, u32[]{:S(2)}, u32[]{:S(2)}) collective-permute-start(bf16[64,256]{0,1:T(8,128)(2,1)S(1)} %slice.164), channel_id=1, source_target_pairs={{0,16},{16,128},{128,144},{144,1},{1,17},{17,129},{129,145},{145,2... | collective-permute-start | bytes 98312 | tf_op jit(solution)/shard_map/ppermute | solution.py:91
  216.2 24.4 %collective-permute-start.6 = (bf16[256,256]{0,1:T(8,128)(2,1)S(1)}, bf16[256,256]{0,1:T(8,128)(2,1)S(1)}, u32[]{:S(2)}, u32[]{:S(2)}) collective-permute-start(bf16[256,256]{0,1:T(8,128)(2,1)S(1)} %add_convert_fusion.2), channel_id=1, source_target_pairs={{0,0},{32,1},{64,2},{96,3},{128,32},{160,33},{192,34},{224,35},{1,... | collective-permute-start | bytes 393224 | tf_op jit(solution)/shard_map/ppermute | solution.py:114
  251.9 10.2 %collective-permute-start.7 = (bf16[64,256]{0,1:T(8,128)(2,1)S(1)}, bf16[64,256]{0,1:T(8,128)(2,1)S(1)}, u32[]{:S(2)}, u32[]{:S(2)}) collective-permute-start(bf16[64,256]{0,1:T(8,128)(2,1)S(1)} %slice.171), channel_id=1, source_target_pairs={{0,16},{16,128},{128,144},{144,1},{1,17},{17,129},{129,145},{145,2... | collective-permute-start | bytes 98312 | tf_op jit(solution)/shard_map/ppermute | solution.py:91
  277.8 26.9 %collective-permute-start.8 = (bf16[256,256]{0,1:T(8,128)(2,1)S(1)}, bf16[256,256]{0,1:T(8,128)(2,1)S(1)}, u32[]{:S(2)}, u32[]{:S(2)}) collective-permute-start(bf16[256,256]{0,1:T(8,128)(2,1)S(1)} %add_convert_fusion.1), channel_id=1, source_target_pairs={{0,0},{32,1},{64,2},{96,3},{128,32},{160,33},{192,34},{224,35},{1,... | collective-permute-start | bytes 393224 | tf_op jit(solution)/shard_map/ppermute | solution.py:114
  288.9 5.0 %copy-start.1 = (bf16[8,1024,256]{2,1,0:T(8,128)(2,1)S(1)}, bf16[8,1024,256]{2,1,0:T(8,128)(2,1)}, u32[]{:S(2)}) copy-start(bf16[8,1024,256]{2,1,0:T(8,128)(2,1)} %all-gather.4.cloned.1.call-done) | copy-start | bytes 12582916
  315.3 25.5 %collective-permute-start.9 = (bf16[256,256]{0,1:T(8,128)(2,1)S(1)}, bf16[256,256]{0,1:T(8,128)(2,1)S(1)}, u32[]{:S(2)}, u32[]{:S(2)}) collective-permute-start(bf16[256,256]{0,1:T(8,128)(2,1)S(1)} %add_convert_fusion), channel_id=1, source_target_pairs={{0,0},{32,1},{64,2},{96,3},{128,32},{160,33},{192,34},{224,35},{1,... | collective-permute-start | bytes 393224 | tf_op jit(solution)/shard_map/ppermute | solution.py:119
Sparse Core Ops, SparseCore 0:
  152.0 57.9 all-gather.3

commit v9 on v8

--- a/solution.py
+++ b/solution.py
@@ -13,7 +13,7 @@
     pairs = []
     for zl in range(n_zl):
         for zh in range(n_zh):
-            pairs.append((zl * n_zh + zh, (zl % 2 * n_zh + zh) * n_zh + zl // 2))
+            pairs.append((zl * n_zh + zh, (zl % 2 * n_zh + n_zh - 1 - zh) * n_zh + zl // 2))
     return pairs
 
 
@@ -33,7 +33,7 @@
         zl, c = (section + 1) // n_c % n_zl, (section + 1) % n_c
         y = (section + 1) // (n_c * n_zl)
         for zh in range(n_zh):
-            target = (((y * 2 + zl % 2) * n_zp + zh) * n_c + c) * n_zh + zl // 2
+            target = (((y * 2 + zl % 2) * n_zp + n_zh - 1 - zh) * n_c + c) * n_zh + zl // 2
             pairs.append((section * n_zh + zh, target))
     return pairs
 
@@ -56,10 +56,10 @@
 
     hidden = lax.ppermute(signal, MOVED, there)
     before = lax.ppermute(signal[row_count - REACH :], SECTION + ("zh",), first_halo_pairs(n_y, n_zl, n_c, n_zh))
-    starts = (REACH - offsets).astype(jnp.uint32)
+    starts = REACH - offsets
 
     half = width // n_c
-    share = lax.dynamic_slice(mixing, (0, c * half, (y * n_zh + zp) * width), (layers, half, width))
+    share = lax.dynamic_slice(mixing, (0, c * half, (y * n_zh + n_zh - 1 - zp) * width), (layers, half, width))
     high = lax.reduce_precision(taps, 8, 7)
     low = (taps - high).astype(jnp.bfloat16)
     n_tap_rows = layers * n_taps
@@ -74,6 +74,7 @@
     )
     got = lax.all_gather(sent, "zh", axis=0)
     hidden, before, got = lax.optimization_barrier((hidden, before, got))
+    got = got[::-1]
     coeffs = got[:, layers * half :].astype(jnp.float32)
     coeffs = coeffs[:, :n_tap_rows] + coeffs[:, n_tap_rows : 2 * n_tap_rows]
     coeffs = coeffs.transpose(1, 0, 2).reshape(layers, n_taps, n_zh * width)
@@ -102,7 +103,9 @@
         stored = lax.optimization_barrier(normed.astype(jnp.bfloat16))
         conv = jnp.zeros((row_count, values.shape[1]), jnp.float32)
         for k in range(n_taps):
-            window = lax.dynamic_slice(stored, (starts[layer, k], jnp.uint32(0)), (row_count, stored.shape[1]))
+            window = lax.dynamic_slice(
+                stored, (starts[layer, k], 0), (row_count, stored.shape[1]), allow_negative_indices=False
+            )
             conv = conv + coeffs[layer, k] * window.astype(jnp.float32)
         gated = lax.optimization_barrier((conv * jax.nn.silu(normed[REACH:])).astype(jnp.bfloat16))
         tile = first if layer == 0 else later[:, layer - 1]

time: 349 us -> 347 us (level)
  the two profiles are of different devices: /device:TPU:160 before, /device:TPU:97 now
where the time goes in v9:
time: 347 us; the launch traced here: 346 us
  blocking collectives  190 us (55%)
  starting transfers between devices  64.6 us (19%)
  waiting for transfers between devices  50.3 us (14%)
  other arithmetic  17.4 us (5%)
  between operations  13.8 us (4%)
  matrix products  5.04 us (1%)
  local copies, waits for them, and re-layouts  4.94 us (1%)
    all_gather x1, blocking collectives, body(): got = lax.all_gather(sent, 'zh', axis=0)  62.6 us
    all_gather x3, blocking collectives, body(): lax.all_gather(jnp.concatenate([before, hidden], axis=0), 'zp', axis=1, t...  61.1 us
    all_to_all x3, blocking collectives, body(): terms = lax.all_to_all(partial, 'x', split_axis=0, concat_axis=0)  35.3 us
    ppermute x2, waiting for transfers between devices, body(): lax.ppermute(ready, MOVED, back)  23.9 us
    psum x3, blocking collectives, body(): squares = lax.psum(jnp.sum(values * values, axis=-1), 'x')  22.8 us
    ppermute x1, starting transfers between devices, body(): hidden = lax.ppermute(signal, MOVED, there)  22.1 us
    ppermute x1, waiting for transfers between devices, body(): returned.append(lax.ppermute(hidden, MOVED, back))  21.8 us
    ppermute x2, starting transfers between devices, body(): before = lax.ppermute(hidden[row_count - REACH:], PLACE, forward)  14.3 us
  transfers between devices with their start and end apart: 11, of which 6 were waited for; matrix products, arithmetic and copies ran while one was open for 7% of the time, Pallas kernels for 0%

profile of v9, /device:TPU:97, one launch (start us, length us, event | category | flops | bytes accessed | tf_op | source)
XLA Modules:
  0.0 346.4 jit_solution(17132980585622607623)
XLA Ops:
  6.5 1.0 copy.11
  7.5 22.1 %collective-permute-start = (bf16[256,256]{0,1:T(8,128)(2,1)S(1)}, bf16[256,256]{0,1:T(8,128)(2,1)S(1)}, u32[]{:S(2)}, u32[]{:S(2)}) collective-permute-start(bf16[256,256]{0,1:T(8,128)(2,1)S(1)} %copy.11), channel_id=1, source_target_pairs={{0,96},{1,64},{2,32},{3,0},{32,224},{33,192},{34,160},{35,128},{64... | collective-permute-start | bytes 393224 | tf_op jit(solution)/shard_map/ppermute | solution.py:57
  29.6 0.1 slice.170
  29.7 6.9 %collective-permute-start.1 = (bf16[64,256]{0,1:T(8,128)(2,1)S(1)}, bf16[64,256]{0,1:T(8,128)(2,1)S(1)}, u32[]{:S(2)}, u32[]{:S(2)}) collective-permute-start(bf16[64,256]{0,1:T(8,128)(2,1)S(1)} %slice.170), channel_id=1, source_target_pairs={{0,112},{1,80},{2,48},{3,16},{16,224},{17,192},{18,160},{19,128},{... | collective-permute-start | bytes 98312 | tf_op jit(solution)/shard_map/ppermute | solution.py:58
  36.7 0.7 reduce-precision_convert_fusion
  37.4 0.1 pad.18.clone
  37.5 0.9 constant_dynamic-slice_fusion
  38.4 0.1 maximum_maximum_fusion
  38.6 62.6 %all-gather = bf16[1664,256]{1,0:T(8,128)(2,1)S(1)} all-gather(bf16[416,256]{1,0:T(8,128)(2,1)S(1)} %maximum_maximum_fusion), channel_id=2, replica_groups=mesh['y'=4,'zq'=2,'zp'=4,'c'=2,'x'=4,'zh'=4] {'zh'}, dimensions={0}, use_global_device_ids=true | all-gather | bytes 1064960 | tf_op jit(solution)/shard_map/all_gather | solution.py:75
  101.1 0.1 fusion.34
  101.2 4.2 %all_gather.32 = bf16[4,256,256]{2,1,0:T(8,128)(2,1)S(1)} all-gather(bf16[4,128,256]{2,1,0:T(8,128)(2,1)S(1)} %slice.128), channel_id=1, replica_groups=mesh['y'=4,'zq'=2,'zp'=4,'c'=2,'x'=4,'zh'=4] {'c'}, dimensions={1}, use_global_device_ids=true | all-gather | bytes 786432 | tf_op jit(solution)/shard_map/all_gather | solution.py:82
  105.4 0.2 copy.24
  105.6 2.2 all_gather.33
  107.8 2.2 all_gather.34
  110.0 1.9 collective-permute-start.2
  111.9 8.1 %collective-permute-start.3 = (bf16[1024,256]{0,1:T(8,128)(2,1)S(1)}, bf16[1024,256]{0,1:T(8,128)(2,1)}, u32[]{:S(2)}, u32[]{:S(2)}) collective-permute-start(bf16[1024,256]{0,1:T(8,128)(2,1)S(1)} %copy.24), channel_id=1, source_target_pairs={{0,768},{256,0},{512,256},{768,512},{1,769},{257,1},{513,257},{769... | collective-permute-start | bytes 1572872 | tf_op jit(solution)/shard_map/ppermute | solution.py:43
  120.0 0.1 pad_maximum_fusion.2
  120.2 0.0 copy-start
  120.2 1.1 pad_maximum_fusion
  121.2 23.8 %all_gather.35 = bf16[320,1024]{0,1:T(8,128)(2,1)S(1)} all-gather(bf16[320,256]{0,1:T(8,128)(2,1)S(1)} %pad_maximum_fusion.2), channel_id=1, replica_groups=mesh['y'=4,'zq'=2,'zp'=4,'c'=2,'x'=4,'zh'=4] {'zp'}, dimensions={1}, use_global_device_ids=true | all-gather | bytes 819200 | tf_op jit(solution)/shard_map/all_gather | solution.py:93
  145.0 0.0 all-gather.4.cloned.1.call-update
  145.1 0.7 fusion.36
  145.8 3.7 %collective-permute-start.4 = (bf16[1024,256]{0,1:T(8,128)(2,1)S(1)}, bf16[1024,256]{0,1:T(8,128)(2,1)}, u32[]{:S(2)}, u32[]{:S(2)}) collective-permute-start(bf16[1024,256]{0,1:T(8,128)(2,1)S(1)} %copy.24), channel_id=1, source_target_pairs={{0,512},{256,768},{512,0},{768,256},{1,513},{257,769},{513,1},{769... | collective-permute-start | bytes 1572872 | tf_op jit(solution)/shard_map/ppermute | solution.py:43
  149.7 0.2 fusion.10
  149.9 8.9 %psum.21 = f32[320]{0:T(512)S(1)} all-reduce(f32[320]{0:T(512)S(1)} %fusion.10), channel_id=1, replica_groups=mesh['y'=4,'zq'=2,'zp'=4,'c'=2,'x'=4,'zh'=4] {'x'}, use_global_device_ids=true, to_apply=%region_1.2 | all-reduce | flops 320 | bytes 2560 | tf_op jit(solution)/shard_map/psum | solution.py:98
  158.8 0.7 collective-permute-done.4
  159.5 0.2 fusion.26
  159.7 4.3 %multiply_convert_fusion.2 = bf16[256,1024]{0,1:T(8,128)(2,1)S(1)} fusion(f32[320,1024]{0,1:T(8,128)S(1)} %get-tuple-element.51, bf16[320,1024]{0,1:T(8,128)(2,1)S(1)} %get-tuple-element.50, s32[]{:T(128)} %bitcast.22, f32[1024]{0:T(1024)S(1)} %bitcast.92, s32[]{:T(128)} %bitcast.20, f32[1024]{0:T(1024)S(1)} %bitcast.93, s32[]{:T(128)} %bitcast.18, ...), kind=kLoop, calls=%fused_computation.34 | loop fusion | flops 4456448 | bytes 3686416 | tf_op jit(solution)/shard_map/convert_element_type | solution.py:110
  164.0 1.9 fusion.18
  166.0 0.6 gather_fusion
  166.5 12.1 %all_to_all.15 = bf16[4,256,256]{1,2,0:T(8,128)(2,1)S(1)} all-to-all(bf16[4,256,256]{1,2,0:T(8,128)(2,1)S(1)} %gather_fusion), channel_id=1, replica_groups=mesh['y'=4,'zq'=2,'zp'=4,'c'=2,'x'=4,'zh'=4] {'x'}, dimensions={0} | all-to-all | bytes 1048576 | tf_op jit(solution)/shard_map/all_to_all | solution.py:119
  178.6 0.1 convert_reduce_fusion.2
  178.7 0.1 slice.180
  178.8 12.3 %collective-permute-start.5 = (bf16[64,256]{0,1:T(8,128)(2,1)S(1)}, bf16[64,256]{0,1:T(8,128)(2,1)S(1)}, u32[]{:S(2)}, u32[]{:S(2)}) collective-permute-start(bf16[64,256]{0,1:T(8,128)(2,1)S(1)} %slice.180), channel_id=1, source_target_pairs={{0,16},{16,128},{128,144},{144,1},{1,17},{17,129},{129,145},{145,2... | collective-permute-start | bytes 98312 | tf_op jit(solution)/shard_map/ppermute | solution.py:92
  191.2 2.6 collective-permute-done.5
  193.8 0.1 pad_maximum_fusion.3
  193.9 15.7 %all_gather.38 = bf16[320,1024]{0,1:T(8,128)(2,1)S(1)} all-gather(bf16[320,256]{0,1:T(8,128)(2,1)S(1)} %pad_maximum_fusion.3), channel_id=1, replica_groups=mesh['y'=4,'zq'=2,'zp'=4,'c'=2,'x'=4,'zh'=4] {'zp'}, dimensions={1}, use_global_device_ids=true | all-gather | bytes 819200 | tf_op jit(solution)/shard_map/all_gather | solution.py:93
  209.6 3.0 collective-permute-start.6
  212.6 0.2 fusion.11
  212.9 6.9 %psum.22 = f32[320]{0:T(512)S(1)} all-reduce(f32[320]{0:T(512)S(1)} %fusion.11), channel_id=1, replica_groups=mesh['y'=4,'zq'=2,'zp'=4,'c'=2,'x'=4,'zh'=4] {'x'}, use_global_device_ids=true, to_apply=%region_4.5 | all-reduce | flops 320 | bytes 2560 | tf_op jit(solution)/shard_map/psum | solution.py:98
  219.7 0.2 fusion.27
  219.9 4.4 %multiply_convert_fusion.1 = bf16[256,1024]{0,1:T(8,128)(2,1)S(1)} fusion(f32[320,1024]{0,1:T(8,128)S(1)} %get-tuple-element.49, bf16[320,1024]{0,1:T(8,128)(2,1)S(1)} %get-tuple-element.48, s32[]{:T(128)} %bitcast.32, f32[1024]{0:T(1024)S(1)} %bitcast.88, s32[]{:T(128)} %bitcast.30, f32[1024]{0:T(1024)S(1)} %bitcast.89, s32[]{:T(128)} %bitcast.28, ...), kind=kLoop, calls=%fused_computation.32 | loop fusion | flops 4456448 | bytes 3686416 | tf_op jit(solution)/shard_map/convert_element_type | solution.py:110
  224.4 0.0 all-gather.4.cloned.1.call-done
  224.4 2.4 fusion.22
  226.7 8.5 %collective-permute-done.6 = bf16[256,256]{0,1:T(8,128)(2,1)S(1)} collective-permute-done((bf16[256,256]{0,1:T(8,128)(2,1)S(1)}, bf16[256,256]{0,1:T(8,128)(2,1)S(1)}, u32[]{:S(2)}, u32[]{:S(2)}) %collective-permute-start.6) | collective-permute-done | bytes 131104 | tf_op jit(solution)/shard_map/ppermute | solution.py:117
  235.2 11.6 %all_to_all.16 = bf16[4,256,256]{1,2,0:T(8,128)(2,1)S(1)} all-to-all(bf16[4,256,256]{1,2,0:T(8,128)(2,1)S(1)} %fusion.22), channel_id=1, replica_groups=mesh['y'=4,'zq'=2,'zp'=4,'c'=2,'x'=4,'zh'=4] {'x'}, dimensions={0} | all-to-all | bytes 1048576 | tf_op jit(solution)/shard_map/all_to_all | solution.py:119
  246.8 0.1 convert_reduce_fusion.1
  246.9 0.1 slice.187
  247.0 1.9 collective-permute-start.7
  248.9 1.3 collective-permute-done.7
  250.2 0.1 pad_maximum_fusion.4
  250.4 21.7 %all_gather.39 = bf16[320,1024]{0,1:T(8,128)(2,1)S(1)} all-gather(bf16[320,256]{0,1:T(8,128)(2,1)S(1)} %pad_maximum_fusion.4), channel_id=1, replica_groups=mesh['y'=4,'zq'=2,'zp'=4,'c'=2,'x'=4,'zh'=4] {'zp'}, dimensions={1}, use_global_device_ids=true | all-gather | bytes 819200 | tf_op jit(solution)/shard_map/all_gather | solution.py:93
  272.0 0.2 fusion.12
  272.3 2.7 collective-permute-start.8
  274.9 7.1 %psum.23 = f32[320]{0:T(512)S(1)} all-reduce(f32[320]{0:T(512)S(1)} %fusion.12), channel_id=1, replica_groups=mesh['y'=4,'zq'=2,'zp'=4,'c'=2,'x'=4,'zh'=4] {'x'}, use_global_device_ids=true, to_apply=%region_7.8 | all-reduce | flops 320 | bytes 2560 | tf_op jit(solution)/shard_map/psum | solution.py:98
  282.0 0.2 fusion.28
  282.2 4.8 %multiply_convert_fusion = bf16[256,1024]{0,1:T(8,128)(2,1)S(1)} fusion(f32[320,1024]{0,1:T(8,128)S(1)} %get-tuple-element.47, bf16[320,1024]{0,1:T(8,128)(2,1)S(1)} %get-tuple-element.46, s32[]{:T(128)} %bitcast.44, f32[1024]{0:T(1024)S(1)} %bitcast.85, s32[]{:T(128)} %bitcast.42, f32[1024]{0:T(1024)S(1)} %bitcast.86, s32[]{:T(128)} %bitcast.40, ...), kind=kLoop, calls=%fused_computation.30 | loop fusion | flops 4456448 | bytes 3686416 | tf_op jit(solution)/shard_map/convert_element_type | solution.py:110
  287.0 0.8 fusion.21
  287.8 15.4 %collective-permute-done.8 = bf16[256,256]{0,1:T(8,128)(2,1)S(1)} collective-permute-done((bf16[256,256]{0,1:T(8,128)(2,1)S(1)}, bf16[256,256]{0,1:T(8,128)(2,1)S(1)}, u32[]{:S(2)}, u32[]{:S(2)}) %collective-permute-start.8) | collective-permute-done | bytes 131104 | tf_op jit(solution)/shard_map/ppermute | solution.py:117
  303.2 11.6 %all_to_all.17 = bf16[4,256,256]{1,2,0:T(8,128)(2,1)S(1)} all-to-all(bf16[4,256,256]{1,2,0:T(8,128)(2,1)S(1)} %fusion.21), channel_id=1, replica_groups=mesh['y'=4,'zq'=2,'zp'=4,'c'=2,'x'=4,'zh'=4] {'x'}, dimensions={0} | all-to-all | bytes 1048576 | tf_op jit(solution)/shard_map/all_to_all | solution.py:119
  314.8 0.1 convert_reduce_fusion
  314.9 1.9 collective-permute-start.9
  316.8 21.8 %collective-permute-done.9 = bf16[256,256]{0,1:T(8,128)(2,1)S(1)} collective-permute-done((bf16[256,256]{0,1:T(8,128)(2,1)S(1)}, bf16[256,256]{0,1:T(8,128)(2,1)S(1)}, u32[]{:S(2)}, u32[]{:S(2)}) %collective-permute-start.9) | collective-permute-done | bytes 131104 | tf_op jit(solution)/shard_map/ppermute | solution.py:122
  338.6 0.9 copy.20
  (30 shorter events, 0.4 us)
Async XLA Ops:
  6.5 217.8 %all-gather.4.cloned.1.call-start = ((), (), s32[]{:S(2)}) async-start(), calls=%async_computation.3 | async-start | bytes 5242880 | tf_op jit(solution)/shard_map/all_gather | solution.py:96
  7.5 93.6 %collective-permute-start = (bf16[256,256]{0,1:T(8,128)(2,1)S(1)}, bf16[256,256]{0,1:T(8,128)(2,1)S(1)}, u32[]{:S(2)}, u32[]{:S(2)}) collective-permute-start(bf16[256,256]{0,1:T(8,128)(2,1)S(1)} %copy.11), channel_id=1, source_target_pairs={{0,96},{1,64},{2,32},{3,0},{32,224},{33,192},{34,160},{35,128},{64... | collective-permute-start | bytes 393224 | tf_op jit(solution)/shard_map/ppermute | solution.py:57
  29.7 71.4 %collective-permute-start.1 = (bf16[64,256]{0,1:T(8,128)(2,1)S(1)}, bf16[64,256]{0,1:T(8,128)(2,1)S(1)}, u32[]{:S(2)}, u32[]{:S(2)}) collective-permute-start(bf16[64,256]{0,1:T(8,128)(2,1)S(1)} %slice.170), channel_id=1, source_target_pairs={{0,112},{1,80},{2,48},{3,16},{16,224},{17,192},{18,160},{19,128},{... | collective-permute-start | bytes 98312 | tf_op jit(solution)/shard_map/ppermute | solution.py:58
  110.0 35.0 %collective-permute-start.2 = (bf16[1024,256]{0,1:T(8,128)(2,1)S(1)}, bf16[1024,256]{0,1:T(8,128)(2,1)S(1)}, u32[]{:S(2)}, u32[]{:S(2)}) collective-permute-start(bf16[1024,256]{0,1:T(8,128)(2,1)S(1)} %copy.24), channel_id=1, source_target_pairs={{0,256},{256,512},{512,768},{768,0},{1,257},{257,513},{513,769},{7... | collective-permute-start | bytes 1572872 | tf_op jit(solution)/shard_map/ppermute | solution.py:43
  111.9 33.1 %collective-permute-start.3 = (bf16[1024,256]{0,1:T(8,128)(2,1)S(1)}, bf16[1024,256]{0,1:T(8,128)(2,1)}, u32[]{:S(2)}, u32[]{:S(2)}) collective-permute-start(bf16[1024,256]{0,1:T(8,128)(2,1)S(1)} %copy.24), channel_id=1, source_target_pairs={{0,768},{256,0},{512,256},{768,512},{1,769},{257,1},{513,257},{769... | collective-permute-start | bytes 1572872 | tf_op jit(solution)/shard_map/ppermute | solution.py:43
  120.2 24.9 %copy-start = (s32[3,4]{1,0:T(4,128)S(1)}, s32[3,4]{1,0:T(4,128)}, u32[]{:S(2)}) copy-start(s32[3,4]{1,0:T(4,128)} %param.7) | copy-start | bytes 148
  145.8 13.7 %collective-permute-start.4 = (bf16[1024,256]{0,1:T(8,128)(2,1)S(1)}, bf16[1024,256]{0,1:T(8,128)(2,1)}, u32[]{:S(2)}, u32[]{:S(2)}) collective-permute-start(bf16[1024,256]{0,1:T(8,128)(2,1)S(1)} %copy.24), channel_id=1, source_target_pairs={{0,512},{256,768},{512,0},{768,256},{1,513},{257,769},{513,1},{769... | collective-permute-start | bytes 1572872 | tf_op jit(solution)/shard_map/ppermute | solution.py:43
  178.8 14.9 %collective-permute-start.5 = (bf16[64,256]{0,1:T(8,128)(2,1)S(1)}, bf16[64,256]{0,1:T(8,128)(2,1)S(1)}, u32[]{:S(2)}, u32[]{:S(2)}) collective-permute-start(bf16[64,256]{0,1:T(8,128)(2,1)S(1)} %slice.180), channel_id=1, source_target_pairs={{0,16},{16,128},{128,144},{144,1},{1,17},{17,129},{129,145},{145,2... | collective-permute-start | bytes 98312 | tf_op jit(solution)/shard_map/ppermute | solution.py:92
  209.6 25.6 %collective-permute-start.6 = (bf16[256,256]{0,1:T(8,128)(2,1)S(1)}, bf16[256,256]{0,1:T(8,128)(2,1)S(1)}, u32[]{:S(2)}, u32[]{:S(2)}) collective-permute-start(bf16[256,256]{0,1:T(8,128)(2,1)S(1)} %add_convert_fusion.2), channel_id=1, source_target_pairs={{96,0},{64,1},{32,2},{0,3},{224,32},{192,33},{160,34},{128,35},{97... | collective-permute-start | bytes 393224 | tf_op jit(solution)/shard_map/ppermute | solution.py:117
  247.0 3.3 collective-permute-start.7
  272.3 30.9 %collective-permute-start.8 = (bf16[256,256]{0,1:T(8,128)(2,1)S(1)}, bf16[256,256]{0,1:T(8,128)(2,1)S(1)}, u32[]{:S(2)}, u32[]{:S(2)}) collective-permute-start(bf16[256,256]{0,1:T(8,128)(2,1)S(1)} %add_convert_fusion.1), channel_id=1, source_target_pairs={{96,0},{64,1},{32,2},{0,3},{224,32},{192,33},{160,34},{128,35},{97... | collective-permute-start | bytes 393224 | tf_op jit(solution)/shard_map/ppermute | solution.py:117
  282.0 5.0 %copy-start.1 = (bf16[8,1024,256]{2,1,0:T(8,128)(2,1)S(1)}, bf16[8,1024,256]{2,1,0:T(8,128)(2,1)}, u32[]{:S(2)}) copy-start(bf16[8,1024,256]{2,1,0:T(8,128)(2,1)} %all-gather.4.cloned.1.call-done) | copy-start | bytes 12582916
  314.9 23.7 %collective-permute-start.9 = (bf16[256,256]{0,1:T(8,128)(2,1)S(1)}, bf16[256,256]{0,1:T(8,128)(2,1)S(1)}, u32[]{:S(2)}, u32[]{:S(2)}) collective-permute-start(bf16[256,256]{0,1:T(8,128)(2,1)S(1)} %add_convert_fusion), channel_id=1, source_target_pairs={{96,0},{64,1},{32,2},{0,3},{224,32},{192,33},{160,34},{128,35},{97... | collective-permute-start | bytes 393224 | tf_op jit(solution)/shard_map/ppermute | solution.py:122
Sparse Core Ops, SparseCore 0:
  145.2 60.7 all-gather.3

commit v10 on v9

--- a/solution.py
+++ b/solution.py
@@ -54,8 +54,6 @@
     back = [(target, source) for source, target in there]
     forward = halo_pairs(n_y, n_zl, n_c, n_zh)
 
-    hidden = lax.ppermute(signal, MOVED, there)
-    before = lax.ppermute(signal[row_count - REACH :], SECTION + ("zh",), first_halo_pairs(n_y, n_zl, n_c, n_zh))
     starts = REACH - offsets
 
     half = width // n_c
@@ -73,7 +71,9 @@
         axis=0,
     )
     got = lax.all_gather(sent, "zh", axis=0)
-    hidden, before, got = lax.optimization_barrier((hidden, before, got))
+    signal, got = lax.optimization_barrier((signal, got))
+    hidden = lax.ppermute(signal, MOVED, there)
+    before = lax.ppermute(signal[row_count - REACH :], SECTION + ("zh",), first_halo_pairs(n_y, n_zl, n_c, n_zh))
     got = got[::-1]
     coeffs = got[:, layers * half :].astype(jnp.float32)
     coeffs = coeffs[:, :n_tap_rows] + coeffs[:, n_tap_rows : 2 * n_tap_rows]
@@ -82,9 +82,9 @@
         lax.all_gather(got[:, layer * half : (layer + 1) * half], "c", axis=1, tiled=True).reshape(n_zh * width, width)
         for layer in range(layers)
     ]
-    hidden, whole = lax.optimization_barrier((hidden, whole))
+    hidden, before, whole = lax.optimization_barrier((hidden, before, whole))
     turned = [whole[0]] + [rotated(whole[0], "y", k) for k in range(1, n_y)]
-    rest = jnp.stack(whole[1:])
+    hidden, before, rest = lax.optimization_barrier((hidden, before, jnp.stack(whole[1:])))
     entry_of = (y - jnp.arange(n_x)) % n_y
     returned = []
     for layer in range(layers):
@@ -100,7 +100,7 @@
             squares, turned[2] = lax.optimization_barrier((squares, turned[2]))
             first = jnp.stack(turned)
         normed = values * lax.rsqrt(squares / total_channels + 1e-06)[:, None]
-        stored = lax.optimization_barrier(normed.astype(jnp.bfloat16))
+        stored, normed = lax.optimization_barrier((normed.astype(jnp.bfloat16), normed))
         conv = jnp.zeros((row_count, values.shape[1]), jnp.float32)
         for k in range(n_taps):
             window = lax.dynamic_slice(

time: 347 us -> 348 us (level)
  blocking collectives: 190 us -> 196 us
  starting transfers between devices: 64.6 us -> 60.5 us
    all_gather x1, blocking collectives: 62.6 us -> 75.3 us  [body(): got = lax.all_gather(sent, 'zh', axis=0)]
    ppermute x1, starting transfers between devices: 6.93 us -> 16 us  [body(): lax.ppermute(signal[row_count - REACH:], SECTION + ('zh',), first_halo_pa...]
    ppermute x1, starting transfers between devices: 22.1 us -> 13.2 us  [body(): hidden = lax.ppermute(signal, MOVED, there)]
    ppermute x2, waiting for transfers between devices: 23.9 us -> 18 us  [body(): lax.ppermute(ready, MOVED, back)]
    ppermute x1, waiting for transfers between devices: 21.8 us -> 25.9 us  [body(): returned.append(lax.ppermute(hidden, MOVED, back))]
    ppermute x3, starting transfers between devices: 13.7 us -> 10.2 us  [rotated(): lax.ppermute(value, axis, [(source, (source + steps) % count) for source...]
  transfers between devices with their start and end apart: 11 -> 11, of which waited for: 6 -> 5; matrix products, arithmetic and copies ran while one was open for 7% -> 7% of each run, Pallas kernels for 0% -> 0%
where the time goes in v10:
time: 348 us; the launch traced here: 347 us
  blocking collectives  196 us (56%)
  starting transfers between devices  60.5 us (17%)
  waiting for transfers between devices  48.3 us (14%)
  other arithmetic  18.4 us (5%)
  between operations  13.8 us (4%)
  matrix products  4.86 us (1%)
  local copies, waits for them, and re-layouts  4.85 us (1%)
    all_gather x1, blocking collectives, body(): got = lax.all_gather(sent, 'zh', axis=0)  75.3 us
    all_gather x3, blocking collectives, body(): lax.all_gather(jnp.concatenate([before, hidden], axis=0), 'zp', axis=1, t...  60 us
    all_to_all x3, blocking collectives, body(): terms = lax.all_to_all(partial, 'x', split_axis=0, concat_axis=0)  31.8 us
    ppermute x1, waiting for transfers between devices, body(): returned.append(lax.ppermute(hidden, MOVED, back))  25.9 us
    psum x3, blocking collectives, body(): squares = lax.psum(jnp.sum(values * values, axis=-1), 'x')  22.5 us
    ppermute x2, waiting for transfers between devices, body(): lax.ppermute(ready, MOVED, back)  18 us
    ppermute x1, starting transfers between devices, body(): lax.ppermute(signal[row_count - REACH:], SECTION + ('zh',), first_halo_pa...  16 us
    ppermute x2, starting transfers between devices, body(): before = lax.ppermute(hidden[row_count - REACH:], PLACE, forward)  13.8 us
  transfers between devices with their start and end apart: 11, of which 5 were waited for; matrix products, arithmetic and copies ran while one was open for 7% of the time, Pallas kernels for 0%

profile of v10, /device:TPU:97, one launch (start us, length us, event | category | flops | bytes accessed | tf_op | source)
XLA Modules:
  0.0 346.8 jit_solution(15877167033643701610)
XLA Ops:
  6.5 0.7 reduce-precision_convert_fusion
  7.3 0.1 pad.18.clone
  7.4 0.9 constant_dynamic-slice_fusion
  8.3 0.1 maximum_maximum_fusion
  8.5 75.3 %all-gather = bf16[1664,256]{1,0:T(8,128)(2,1)S(1)} all-gather(bf16[416,256]{1,0:T(8,128)(2,1)S(1)} %maximum_maximum_fusion), channel_id=2, replica_groups=mesh['y'=4,'zq'=2,'zp'=4,'c'=2,'x'=4,'zh'=4] {'zh'}, dimensions={0}, use_global_device_ids=true | all-gather | bytes 1064960 | tf_op jit(solution)/shard_map/all_gather | solution.py:73
  83.7 0.1 copy.11
  83.8 13.2 %collective-permute-start = (bf16[256,256]{0,1:T(8,128)(2,1)S(1)}, bf16[256,256]{0,1:T(8,128)(2,1)S(1)}, u32[]{:S(2)}, u32[]{:S(2)}) collective-permute-start(bf16[256,256]{0,1:T(8,128)(2,1)S(1)} %copy.11), channel_id=1, source_target_pairs={{0,96},{1,64},{2,32},{3,0},{32,224},{33,192},{34,160},{35,128},{64... | collective-permute-start | bytes 393224 | tf_op jit(solution)/shard_map/ppermute | solution.py:75
  97.1 0.1 slice.170
  97.2 16.0 %collective-permute-start.1 = (bf16[64,256]{0,1:T(8,128)(2,1)S(1)}, bf16[64,256]{0,1:T(8,128)(2,1)}, u32[]{:S(2)}, u32[]{:S(2)}) collective-permute-start(bf16[64,256]{0,1:T(8,128)(2,1)S(1)} %slice.170), channel_id=1, source_target_pairs={{0,112},{1,80},{2,48},{3,16},{16,224},{17,192},{18,160},{19,128},{... | collective-permute-start | bytes 98312 | tf_op jit(solution)/shard_map/ppermute | solution.py:76
  113.2 0.1 fusion.34
  113.2 2.2 all_gather.32
  115.4 2.2 all_gather.33
  117.6 2.2 all_gather.34
  119.8 0.2 copy.24
  120.0 0.0 collective-permute-done.1
  120.1 3.2 collective-permute-start.2
  123.3 3.4 collective-permute-start.3
  126.6 1.1 pad_maximum_fusion
  127.7 1.0 pad_maximum_fusion.2
  128.7 17.1 %all_gather.35 = bf16[320,1024]{0,1:T(8,128)(2,1)S(1)} all-gather(bf16[320,256]{0,1:T(8,128)(2,1)S(1)} %pad_maximum_fusion.2), channel_id=1, replica_groups=mesh['y'=4,'zq'=2,'zp'=4,'c'=2,'x'=4,'zh'=4] {'zp'}, dimensions={1}, use_global_device_ids=true | all-gather | bytes 819200 | tf_op jit(solution)/shard_map/all_gather | solution.py:93
  145.8 0.0 all-gather.4.cloned.1.call-update
  146.0 3.6 %collective-permute-start.4 = (bf16[1024,256]{0,1:T(8,128)(2,1)S(1)}, bf16[1024,256]{0,1:T(8,128)(2,1)S(1)}, u32[]{:S(2)}, u32[]{:S(2)}) collective-permute-start(bf16[1024,256]{0,1:T(8,128)(2,1)S(1)} %copy.24), channel_id=1, source_target_pairs={{0,512},{256,768},{512,0},{768,256},{1,513},{257,769},{513,1},{769... | collective-permute-start | bytes 1572872 | tf_op jit(solution)/shard_map/ppermute | solution.py:43
  149.7 0.7 fusion.36
  150.4 0.2 fusion.10
  150.6 8.8 %psum.21 = f32[320]{0:T(512)S(1)} all-reduce(f32[320]{0:T(512)S(1)} %fusion.10), channel_id=1, replica_groups=mesh['y'=4,'zq'=2,'zp'=4,'c'=2,'x'=4,'zh'=4] {'x'}, use_global_device_ids=true, to_apply=%region_1.2 | all-reduce | flops 320 | bytes 2560 | tf_op jit(solution)/shard_map/psum | solution.py:98
  159.4 0.8 copy-done.3
  160.2 0.2 convert_multiply_fusion.4
  160.4 4.4 %multiply_convert_fusion.2 = bf16[256,1024]{0,1:T(8,128)(2,1)S(1)} fusion(f32[320,1024]{0,1:T(8,128)S(1)} %get-tuple-element.50, bf16[320,1024]{0,1:T(8,128)(2,1)S(1)} %get-tuple-element.49, s32[]{:T(128)} %bitcast.22, f32[1024]{0:T(1024)S(1)} %bitcast.92, s32[]{:T(128)} %bitcast.20, f32[1024]{0:T(1024)S(1)} %bitcast.93, s32[]{:T(128)} %bitcast.18, ...), kind=kLoop, calls=%fused_computation.34 | loop fusion | flops 4456448 | bytes 3686416 | tf_op jit(solution)/shard_map/convert_element_type | solution.py:110
  164.8 1.8 fusion.18
  166.6 0.6 gather_fusion
  167.2 9.3 %all_to_all.15 = bf16[4,256,256]{1,2,0:T(8,128)(2,1)S(1)} all-to-all(bf16[4,256,256]{1,2,0:T(8,128)(2,1)S(1)} %gather_fusion), channel_id=1, replica_groups=mesh['y'=4,'zq'=2,'zp'=4,'c'=2,'x'=4,'zh'=4] {'x'}, dimensions={0} | all-to-all | bytes 1048576 | tf_op jit(solution)/shard_map/all_to_all | solution.py:119
  176.5 0.1 convert_reduce_fusion.2
  176.6 0.1 slice.179
  176.7 10.3 %collective-permute-start.5 = (bf16[64,256]{0,1:T(8,128)(2,1)S(1)}, bf16[64,256]{0,1:T(8,128)(2,1)S(1)}, u32[]{:S(2)}, u32[]{:S(2)}) collective-permute-start(bf16[64,256]{0,1:T(8,128)(2,1)S(1)} %slice.179), channel_id=1, source_target_pairs={{0,16},{16,128},{128,144},{144,1},{1,17},{17,129},{129,145},{145,2... | collective-permute-start | bytes 98312 | tf_op jit(solution)/shard_map/ppermute | solution.py:92
  187.0 3.0 collective-permute-done.5
  190.1 0.1 pad_maximum_fusion.3
  190.2 17.5 %all_gather.38 = bf16[320,1024]{0,1:T(8,128)(2,1)S(1)} all-gather(bf16[320,256]{0,1:T(8,128)(2,1)S(1)} %pad_maximum_fusion.3), channel_id=1, replica_groups=mesh['y'=4,'zq'=2,'zp'=4,'c'=2,'x'=4,'zh'=4] {'zp'}, dimensions={1}, use_global_device_ids=true | all-gather | bytes 819200 | tf_op jit(solution)/shard_map/all_gather | solution.py:93
  207.7 3.1 collective-permute-start.6
  210.8 0.2 fusion.11
  211.0 6.9 %psum.22 = f32[320]{0:T(512)S(1)} all-reduce(f32[320]{0:T(512)S(1)} %fusion.11), channel_id=1, replica_groups=mesh['y'=4,'zq'=2,'zp'=4,'c'=2,'x'=4,'zh'=4] {'x'}, use_global_device_ids=true, to_apply=%region_4.5 | all-reduce | flops 320 | bytes 2560 | tf_op jit(solution)/shard_map/psum | solution.py:98
  217.9 0.2 convert_multiply_fusion.2
  218.1 4.4 %multiply_convert_fusion.1 = bf16[256,1024]{0,1:T(8,128)(2,1)S(1)} fusion(f32[320,1024]{0,1:T(8,128)S(1)} %get-tuple-element.52, bf16[320,1024]{0,1:T(8,128)(2,1)S(1)} %get-tuple-element.51, s32[]{:T(128)} %bitcast.32, f32[1024]{0:T(1024)S(1)} %bitcast.88, s32[]{:T(128)} %bitcast.30, f32[1024]{0:T(1024)S(1)} %bitcast.89, s32[]{:T(128)} %bitcast.28, ...), kind=kLoop, calls=%fused_computation.32 | loop fusion | flops 4456448 | bytes 3686416 | tf_op jit(solution)/shard_map/convert_element_type | solution.py:110
  222.5 0.0 all-gather.4.cloned.1.call-done
  222.6 2.3 fusion.22
  224.9 5.3 %collective-permute-done.6 = bf16[256,256]{0,1:T(8,128)(2,1)S(1)} collective-permute-done((bf16[256,256]{0,1:T(8,128)(2,1)S(1)}, bf16[256,256]{0,1:T(8,128)(2,1)S(1)}, u32[]{:S(2)}, u32[]{:S(2)}) %collective-permute-start.6) | collective-permute-done | bytes 131104 | tf_op jit(solution)/shard_map/ppermute | solution.py:117
  230.2 11.0 %all_to_all.16 = bf16[4,256,256]{1,2,0:T(8,128)(2,1)S(1)} all-to-all(bf16[4,256,256]{1,2,0:T(8,128)(2,1)S(1)} %fusion.22), channel_id=1, replica_groups=mesh['y'=4,'zq'=2,'zp'=4,'c'=2,'x'=4,'zh'=4] {'x'}, dimensions={0} | all-to-all | bytes 1048576 | tf_op jit(solution)/shard_map/all_to_all | solution.py:119
  241.2 0.1 convert_reduce_fusion.1
  241.3 0.1 slice.185
  241.4 3.5 %collective-permute-start.7 = (bf16[64,256]{0,1:T(8,128)(2,1)S(1)}, bf16[64,256]{0,1:T(8,128)(2,1)S(1)}, u32[]{:S(2)}, u32[]{:S(2)}) collective-permute-start(bf16[64,256]{0,1:T(8,128)(2,1)S(1)} %slice.185), channel_id=1, source_target_pairs={{0,16},{16,128},{128,144},{144,1},{1,17},{17,129},{129,145},{145,2... | collective-permute-start | bytes 98312 | tf_op jit(solution)/shard_map/ppermute | solution.py:92
  244.9 1.3 collective-permute-done.7
  246.2 0.1 pad_maximum_fusion.4
  246.4 25.4 %all_gather.39 = bf16[320,1024]{0,1:T(8,128)(2,1)S(1)} all-gather(bf16[320,256]{0,1:T(8,128)(2,1)S(1)} %pad_maximum_fusion.4), channel_id=1, replica_groups=mesh['y'=4,'zq'=2,'zp'=4,'c'=2,'x'=4,'zh'=4] {'zp'}, dimensions={1}, use_global_device_ids=true | all-gather | bytes 819200 | tf_op jit(solution)/shard_map/all_gather | solution.py:93
  271.7 0.2 fusion.12
  271.9 2.3 collective-permute-start.8
  274.2 6.9 %psum.23 = f32[320]{0:T(512)S(1)} all-reduce(f32[320]{0:T(512)S(1)} %fusion.12), channel_id=1, replica_groups=mesh['y'=4,'zq'=2,'zp'=4,'c'=2,'x'=4,'zh'=4] {'x'}, use_global_device_ids=true, to_apply=%region_7.8 | all-reduce | flops 320 | bytes 2560 | tf_op jit(solution)/shard_map/psum | solution.py:98
  281.1 0.2 convert_multiply_fusion
  281.3 4.8 %multiply_convert_fusion = bf16[256,1024]{0,1:T(8,128)(2,1)S(1)} fusion(f32[320,1024]{0,1:T(8,128)S(1)} %get-tuple-element.57, bf16[320,1024]{0,1:T(8,128)(2,1)S(1)} %get-tuple-element.56, s32[]{:T(128)} %bitcast.44, f32[1024]{0:T(1024)S(1)} %bitcast.85, s32[]{:T(128)} %bitcast.42, f32[1024]{0:T(1024)S(1)} %bitcast.86, s32[]{:T(128)} %bitcast.40, ...), kind=kLoop, calls=%fused_computation.30 | loop fusion | flops 4456448 | bytes 3686416 | tf_op jit(solution)/shard_map/convert_element_type | solution.py:110
  286.1 0.8 fusion.21
  286.9 12.7 %collective-permute-done.8 = bf16[256,256]{0,1:T(8,128)(2,1)S(1)} collective-permute-done((bf16[256,256]{0,1:T(8,128)(2,1)S(1)}, bf16[256,256]{0,1:T(8,128)(2,1)S(1)}, u32[]{:S(2)}, u32[]{:S(2)}) %collective-permute-start.8) | collective-permute-done | bytes 131104 | tf_op jit(solution)/shard_map/ppermute | solution.py:117
  299.6 11.5 %all_to_all.17 = bf16[4,256,256]{1,2,0:T(8,128)(2,1)S(1)} all-to-all(bf16[4,256,256]{1,2,0:T(8,128)(2,1)S(1)} %fusion.21), channel_id=1, replica_groups=mesh['y'=4,'zq'=2,'zp'=4,'c'=2,'x'=4,'zh'=4] {'x'}, dimensions={0} | all-to-all | bytes 1048576 | tf_op jit(solution)/shard_map/all_to_all | solution.py:119
  311.1 0.1 convert_reduce_fusion
  311.2 1.9 collective-permute-start.9
  313.1 25.9 %collective-permute-done.9 = bf16[256,256]{0,1:T(8,128)(2,1)S(1)} collective-permute-done((bf16[256,256]{0,1:T(8,128)(2,1)S(1)}, bf16[256,256]{0,1:T(8,128)(2,1)S(1)}, u32[]{:S(2)}, u32[]{:S(2)}) %collective-permute-start.9) | collective-permute-done | bytes 131104 | tf_op jit(solution)/shard_map/ppermute | solution.py:122
  339.1 0.9 copy.20
  (36 shorter events, 0.4 us)
Async XLA Ops:
  6.5 77.2 %copy-start = (bf16[256,256]{1,0:T(8,128)(2,1)S(1)}, bf16[256,256]{1,0:T(8,128)(2,1)}, u32[]{:S(2)}) copy-start(bf16[256,256]{1,0:T(8,128)(2,1)} %param.4) | copy-start | bytes 393220
  6.5 216.0 %all-gather.4.cloned.1.call-start = ((), (), s32[]{:S(2)}) async-start(), calls=%async_computation.3 | async-start | bytes 5242880 | tf_op jit(solution)/shard_map/all_gather | solution.py:96
  83.8 36.2 %collective-permute-start = (bf16[256,256]{0,1:T(8,128)(2,1)S(1)}, bf16[256,256]{0,1:T(8,128)(2,1)S(1)}, u32[]{:S(2)}, u32[]{:S(2)}) collective-permute-start(bf16[256,256]{0,1:T(8,128)(2,1)S(1)} %copy.11), channel_id=1, source_target_pairs={{0,96},{1,64},{2,32},{3,0},{32,224},{33,192},{34,160},{35,128},{64... | collective-permute-start | bytes 393224 | tf_op jit(solution)/shard_map/ppermute | solution.py:75
  97.2 22.9 %collective-permute-start.1 = (bf16[64,256]{0,1:T(8,128)(2,1)S(1)}, bf16[64,256]{0,1:T(8,128)(2,1)}, u32[]{:S(2)}, u32[]{:S(2)}) collective-permute-start(bf16[64,256]{0,1:T(8,128)(2,1)S(1)} %slice.170), channel_id=1, source_target_pairs={{0,112},{1,80},{2,48},{3,16},{16,224},{17,192},{18,160},{19,128},{... | collective-permute-start | bytes 98312 | tf_op jit(solution)/shard_map/ppermute | solution.py:76
  120.1 25.8 %collective-permute-start.2 = (bf16[1024,256]{0,1:T(8,128)(2,1)S(1)}, bf16[1024,256]{0,1:T(8,128)(2,1)S(1)}, u32[]{:S(2)}, u32[]{:S(2)}) collective-permute-start(bf16[1024,256]{0,1:T(8,128)(2,1)S(1)} %copy.24), channel_id=1, source_target_pairs={{0,256},{256,512},{512,768},{768,0},{1,257},{257,513},{513,769},{7... | collective-permute-start | bytes 1572872 | tf_op jit(solution)/shard_map/ppermute | solution.py:43
  123.3 22.6 %collective-permute-start.3 = (bf16[1024,256]{0,1:T(8,128)(2,1)S(1)}, bf16[1024,256]{0,1:T(8,128)(2,1)}, u32[]{:S(2)}, u32[]{:S(2)}) collective-permute-start(bf16[1024,256]{0,1:T(8,128)(2,1)S(1)} %copy.24), channel_id=1, source_target_pairs={{0,768},{256,0},{512,256},{768,512},{1,769},{257,1},{513,257},{769... | collective-permute-start | bytes 1572872 | tf_op jit(solution)/shard_map/ppermute | solution.py:43
  127.7 18.2 %copy-start.1 = (s32[3,4]{1,0:T(4,128)S(1)}, s32[3,4]{1,0:T(4,128)}, u32[]{:S(2)}) copy-start(s32[3,4]{1,0:T(4,128)} %param.7) | copy-start | bytes 148
  146.0 13.4 %collective-permute-start.4 = (bf16[1024,256]{0,1:T(8,128)(2,1)S(1)}, bf16[1024,256]{0,1:T(8,128)(2,1)S(1)}, u32[]{:S(2)}, u32[]{:S(2)}) collective-permute-start(bf16[1024,256]{0,1:T(8,128)(2,1)S(1)} %copy.24), channel_id=1, source_target_pairs={{0,512},{256,768},{512,0},{768,256},{1,513},{257,769},{513,1},{769... | collective-permute-start | bytes 1572872 | tf_op jit(solution)/shard_map/ppermute | solution.py:43
  159.4 0.8 copy-start.3
  160.4 4.4 %copy-start.4 = (bf16[1024,256]{0,1:T(8,128)(2,1)S(1)}, bf16[1024,256]{0,1:T(8,128)(2,1)}, u32[]{:S(2)}) copy-start(bf16[1024,256]{0,1:T(8,128)(2,1)} %copy-done.3) | copy-start | bytes 1572868
  176.7 13.4 %collective-permute-start.5 = (bf16[64,256]{0,1:T(8,128)(2,1)S(1)}, bf16[64,256]{0,1:T(8,128)(2,1)S(1)}, u32[]{:S(2)}, u32[]{:S(2)}) collective-permute-start(bf16[64,256]{0,1:T(8,128)(2,1)S(1)} %slice.179), channel_id=1, source_target_pairs={{0,16},{16,128},{128,144},{144,1},{1,17},{17,129},{129,145},{145,2... | collective-permute-start | bytes 98312 | tf_op jit(solution)/shard_map/ppermute | solution.py:92
  207.7 22.5 %collective-permute-start.6 = (bf16[256,256]{0,1:T(8,128)(2,1)S(1)}, bf16[256,256]{0,1:T(8,128)(2,1)S(1)}, u32[]{:S(2)}, u32[]{:S(2)}) collective-permute-start(bf16[256,256]{0,1:T(8,128)(2,1)S(1)} %add_convert_fusion.2), channel_id=1, source_target_pairs={{96,0},{64,1},{32,2},{0,3},{224,32},{192,33},{160,34},{128,35},{97... | collective-permute-start | bytes 393224 | tf_op jit(solution)/shard_map/ppermute | solution.py:117
  241.4 4.8 %collective-permute-start.7 = (bf16[64,256]{0,1:T(8,128)(2,1)S(1)}, bf16[64,256]{0,1:T(8,128)(2,1)S(1)}, u32[]{:S(2)}, u32[]{:S(2)}) collective-permute-start(bf16[64,256]{0,1:T(8,128)(2,1)S(1)} %slice.185), channel_id=1, source_target_pairs={{0,16},{16,128},{128,144},{144,1},{1,17},{17,129},{129,145},{145,2... | collective-permute-start | bytes 98312 | tf_op jit(solution)/shard_map/ppermute | solution.py:92
  271.9 27.7 %collective-permute-start.8 = (bf16[256,256]{0,1:T(8,128)(2,1)S(1)}, bf16[256,256]{0,1:T(8,128)(2,1)S(1)}, u32[]{:S(2)}, u32[]{:S(2)}) collective-permute-start(bf16[256,256]{0,1:T(8,128)(2,1)S(1)} %add_convert_fusion.1), channel_id=1, source_target_pairs={{96,0},{64,1},{32,2},{0,3},{224,32},{192,33},{160,34},{128,35},{97... | collective-permute-start | bytes 393224 | tf_op jit(solution)/shard_map/ppermute | solution.py:117
  281.1 5.0 %copy-start.2 = (bf16[8,1024,256]{2,1,0:T(8,128)(2,1)S(1)}, bf16[8,1024,256]{2,1,0:T(8,128)(2,1)}, u32[]{:S(2)}) copy-start(bf16[8,1024,256]{2,1,0:T(8,128)(2,1)} %all-gather.4.cloned.1.call-done) | copy-start | bytes 12582916
  311.2 27.8 %collective-permute-start.9 = (bf16[256,256]{0,1:T(8,128)(2,1)S(1)}, bf16[256,256]{0,1:T(8,128)(2,1)S(1)}, u32[]{:S(2)}, u32[]{:S(2)}) collective-permute-start(bf16[256,256]{0,1:T(8,128)(2,1)S(1)} %add_convert_fusion), channel_id=1, source_target_pairs={{96,0},{64,1},{32,2},{0,3},{224,32},{192,33},{160,34},{128,35},{97... | collective-permute-start | bytes 393224 | tf_op jit(solution)/shard_map/ppermute | solution.py:122
Sparse Core Ops, SparseCore 0:
  146.0 61.7 all-gather.3

commit v11 on v10

--- a/solution.py
+++ b/solution.py
@@ -54,7 +54,8 @@
     back = [(target, source) for source, target in there]
     forward = halo_pairs(n_y, n_zl, n_c, n_zh)
 
-    starts = REACH - offsets
+    backs = lax.optimization_barrier([[offsets[layer, k] for k in range(n_taps)] for layer in range(layers)])
+    starts = [[REACH - steps for steps in backs_of_layer] for backs_of_layer in backs]
 
     half = width // n_c
     share = lax.dynamic_slice(mixing, (0, c * half, (y * n_zh + n_zh - 1 - zp) * width), (layers, half, width))
@@ -104,7 +105,7 @@
         conv = jnp.zeros((row_count, values.shape[1]), jnp.float32)
         for k in range(n_taps):
             window = lax.dynamic_slice(
-                stored, (starts[layer, k], 0), (row_count, stored.shape[1]), allow_negative_indices=False
+                stored, (starts[layer][k], 0), (row_count, stored.shape[1]), allow_negative_indices=False
             )
             conv = conv + coeffs[layer, k] * window.astype(jnp.float32)
         gated = lax.optimization_barrier((conv * jax.nn.silu(normed[REACH:])).astype(jnp.bfloat16))

time: 348 us -> 342 us (0.983)
  other arithmetic: 18.4 us -> 10.5 us
  between operations: 13.8 us -> 21.2 us
  waiting for transfers between devices: 48.3 us -> 42.2 us
    convert_element_type x3, other arithmetic: 13.5 us -> 5.69 us  [body(): (conv * jax.nn.silu(normed[REACH:])).astype(jnp.bfloat16)]
    ppermute x1, waiting for transfers between devices: 25.9 us -> 18.9 us  [body(): returned.append(lax.ppermute(hidden, MOVED, back))]
    ppermute x2, waiting for transfers between devices: 18 us -> 22.7 us  [body(): lax.ppermute(ready, MOVED, back)]
    ppermute x2, waiting for transfers between devices: 4.34 us -> 0.51 us  [body(): before = lax.ppermute(hidden[row_count - REACH:], PLACE, forward)]
  transfers between devices with their start and end apart: 11 -> 11, of which waited for: 5 -> 4; matrix products, arithmetic and copies ran while one was open for 7% -> 5% of each run, Pallas kernels for 0% -> 0%
where the time goes in v11:
time: 342 us; the launch traced here: 340 us
  blocking collectives  197 us (58%)
  starting transfers between devices  60 us (18%)
  waiting for transfers between devices  42.2 us (12%)
  between operations  21.2 us (6%)
  other arithmetic  10.5 us (3%)
  matrix products  4.86 us (1%)
  local copies, waits for them, and re-layouts  4.13 us (1%)
    all_gather x1, blocking collectives, body(): got = lax.all_gather(sent, 'zh', axis=0)  75.3 us
    all_gather x3, blocking collectives, body(): lax.all_gather(jnp.concatenate([before, hidden], axis=0), 'zp', axis=1, t...  61.4 us
    all_to_all x3, blocking collectives, body(): terms = lax.all_to_all(partial, 'x', split_axis=0, concat_axis=0)  31.1 us
    ppermute x2, waiting for transfers between devices, body(): lax.ppermute(ready, MOVED, back)  22.7 us
    psum x3, blocking collectives, body(): squares = lax.psum(jnp.sum(values * values, axis=-1), 'x')  22.7 us
    ppermute x1, waiting for transfers between devices, body(): returned.append(lax.ppermute(hidden, MOVED, back))  18.9 us
    ppermute x1, starting transfers between devices, body(): lax.ppermute(signal[row_count - REACH:], SECTION + ('zh',), first_halo_pa...  16 us
    ppermute x2, starting transfers between devices, body(): before = lax.ppermute(hidden[row_count - REACH:], PLACE, forward)  13.9 us
  transfers between devices with their start and end apart: 11, of which 4 were waited for; matrix products, arithmetic and copies ran while one was open for 5% of the time, Pallas kernels for 0%

profile of v11, /device:TPU:97, one launch (start us, length us, event | category | flops | bytes accessed | tf_op | source)
XLA Modules:
  0.0 340.0 jit_solution(8260149145675103481)
XLA Ops:
  6.5 0.7 reduce-precision_convert_fusion
  7.3 0.1 pad.18.clone
  7.4 0.9 constant_dynamic-slice_fusion
  8.3 0.1 maximum_maximum_fusion
  8.5 75.3 %all-gather = bf16[1664,256]{1,0:T(8,128)(2,1)S(1)} all-gather(bf16[416,256]{1,0:T(8,128)(2,1)S(1)} %maximum_maximum_fusion), channel_id=2, replica_groups=mesh['y'=4,'zq'=2,'zp'=4,'c'=2,'x'=4,'zh'=4] {'zh'}, dimensions={0}, use_global_device_ids=true | all-gather | bytes 1064960 | tf_op jit(solution)/shard_map/all_gather | solution.py:74
  83.7 0.1 copy.11
  83.8 13.2 %collective-permute-start = (bf16[256,256]{0,1:T(8,128)(2,1)S(1)}, bf16[256,256]{0,1:T(8,128)(2,1)S(1)}, u32[]{:S(2)}, u32[]{:S(2)}) collective-permute-start(bf16[256,256]{0,1:T(8,128)(2,1)S(1)} %copy.11), channel_id=1, source_target_pairs={{0,96},{1,64},{2,32},{3,0},{32,224},{33,192},{34,160},{35,128},{64... | collective-permute-start | bytes 393224 | tf_op jit(solution)/shard_map/ppermute | solution.py:76
  97.1 0.1 slice.170
  97.2 16.0 %collective-permute-start.1 = (bf16[64,256]{0,1:T(8,128)(2,1)S(1)}, bf16[64,256]{0,1:T(8,128)(2,1)}, u32[]{:S(2)}, u32[]{:S(2)}) collective-permute-start(bf16[64,256]{0,1:T(8,128)(2,1)S(1)} %slice.170), channel_id=1, source_target_pairs={{0,112},{1,80},{2,48},{3,16},{16,224},{17,192},{18,160},{19,128},{... | collective-permute-start | bytes 98312 | tf_op jit(solution)/shard_map/ppermute | solution.py:77
  113.2 0.1 fusion.34
  113.2 2.2 all_gather.32
  115.4 2.2 all_gather.33
  117.6 2.2 all_gather.34
  119.8 0.2 copy.24
  120.0 0.0 collective-permute-done.1
  120.1 3.2 collective-permute-start.2
  123.3 3.4 collective-permute-start.3
  126.6 1.1 pad_maximum_fusion
  127.7 1.0 pad_maximum_fusion.2
  128.7 17.1 %all_gather.35 = bf16[320,1024]{0,1:T(8,128)(2,1)S(1)} all-gather(bf16[320,256]{0,1:T(8,128)(2,1)S(1)} %pad_maximum_fusion.2), channel_id=1, replica_groups=mesh['y'=4,'zq'=2,'zp'=4,'c'=2,'x'=4,'zh'=4] {'zp'}, dimensions={1}, use_global_device_ids=true | all-gather | bytes 819200 | tf_op jit(solution)/shard_map/all_gather | solution.py:94
  145.8 0.0 all-gather.4.cloned.1.call-update
  145.9 0.7 fusion.36
  146.6 3.6 %collective-permute-start.4 = (bf16[1024,256]{0,1:T(8,128)(2,1)S(1)}, bf16[1024,256]{0,1:T(8,128)(2,1)S(1)}, u32[]{:S(2)}, u32[]{:S(2)}) collective-permute-start(bf16[1024,256]{0,1:T(8,128)(2,1)S(1)} %copy.24), channel_id=1, source_target_pairs={{0,512},{256,768},{512,0},{768,256},{1,513},{257,769},{513,1},{769... | collective-permute-start | bytes 1572872 | tf_op jit(solution)/shard_map/ppermute | solution.py:43
  152.8 0.2 fusion.10
  153.1 8.8 %psum.21 = f32[320]{0:T(512)S(1)} all-reduce(f32[320]{0:T(512)S(1)} %fusion.10), channel_id=1, replica_groups=mesh['y'=4,'zq'=2,'zp'=4,'c'=2,'x'=4,'zh'=4] {'x'}, use_global_device_ids=true, to_apply=%region_1.2 | all-reduce | flops 320 | bytes 2560 | tf_op jit(solution)/shard_map/psum | solution.py:99
  161.8 0.2 convert_multiply_fusion.4
  162.0 1.9 multiply_convert_fusion.2
  163.9 1.8 fusion.18
  165.7 0.6 gather_fusion
  166.3 9.3 %all_to_all.15 = bf16[4,256,256]{1,2,0:T(8,128)(2,1)S(1)} all-to-all(bf16[4,256,256]{1,2,0:T(8,128)(2,1)S(1)} %gather_fusion), channel_id=1, replica_groups=mesh['y'=4,'zq'=2,'zp'=4,'c'=2,'x'=4,'zh'=4] {'x'}, dimensions={0} | all-to-all | bytes 1048576 | tf_op jit(solution)/shard_map/all_to_all | solution.py:120
  175.6 0.1 convert_reduce_fusion.2
  175.7 0.1 slice.179
  175.8 10.3 %collective-permute-start.5 = (bf16[64,256]{0,1:T(8,128)(2,1)S(1)}, bf16[64,256]{0,1:T(8,128)(2,1)S(1)}, u32[]{:S(2)}, u32[]{:S(2)}) collective-permute-start(bf16[64,256]{0,1:T(8,128)(2,1)S(1)} %slice.179), channel_id=1, source_target_pairs={{0,16},{16,128},{128,144},{144,1},{1,17},{17,129},{129,145},{145,2... | collective-permute-start | bytes 98312 | tf_op jit(solution)/shard_map/ppermute | solution.py:93
  188.7 0.5 collective-permute-done.5
  189.2 0.1 pad_maximum_fusion.3
  189.3 17.8 %all_gather.38 = bf16[320,1024]{0,1:T(8,128)(2,1)S(1)} all-gather(bf16[320,256]{0,1:T(8,128)(2,1)S(1)} %pad_maximum_fusion.3), channel_id=1, replica_groups=mesh['y'=4,'zq'=2,'zp'=4,'c'=2,'x'=4,'zh'=4] {'zp'}, dimensions={1}, use_global_device_ids=true | all-gather | bytes 819200 | tf_op jit(solution)/shard_map/all_gather | solution.py:94
  207.1 2.5 collective-permute-start.6
  209.5 0.2 fusion.11
  209.8 7.0 %psum.22 = f32[320]{0:T(512)S(1)} all-reduce(f32[320]{0:T(512)S(1)} %fusion.11), channel_id=1, replica_groups=mesh['y'=4,'zq'=2,'zp'=4,'c'=2,'x'=4,'zh'=4] {'x'}, use_global_device_ids=true, to_apply=%region_4.5 | all-reduce | flops 320 | bytes 2560 | tf_op jit(solution)/shard_map/psum | solution.py:99
  216.8 0.2 convert_multiply_fusion.2
  217.0 1.9 multiply_convert_fusion.1
  218.9 0.0 all-gather.4.cloned.1.call-done
  218.9 2.3 fusion.22
  221.3 5.9 %collective-permute-done.6 = bf16[256,256]{0,1:T(8,128)(2,1)S(1)} collective-permute-done((bf16[256,256]{0,1:T(8,128)(2,1)S(1)}, bf16[256,256]{0,1:T(8,128)(2,1)S(1)}, u32[]{:S(2)}, u32[]{:S(2)}) %collective-permute-start.6) | collective-permute-done | bytes 131104 | tf_op jit(solution)/shard_map/ppermute | solution.py:118
  227.2 10.3 %all_to_all.16 = bf16[4,256,256]{1,2,0:T(8,128)(2,1)S(1)} all-to-all(bf16[4,256,256]{1,2,0:T(8,128)(2,1)S(1)} %fusion.22), channel_id=1, replica_groups=mesh['y'=4,'zq'=2,'zp'=4,'c'=2,'x'=4,'zh'=4] {'x'}, dimensions={0} | all-to-all | bytes 1048576 | tf_op jit(solution)/shard_map/all_to_all | solution.py:120
  237.5 0.1 convert_reduce_fusion.1
  237.6 0.1 slice.185
  237.7 3.5 %collective-permute-start.7 = (bf16[64,256]{0,1:T(8,128)(2,1)S(1)}, bf16[64,256]{0,1:T(8,128)(2,1)S(1)}, u32[]{:S(2)}, u32[]{:S(2)}) collective-permute-start(bf16[64,256]{0,1:T(8,128)(2,1)S(1)} %slice.185), channel_id=1, source_target_pairs={{0,16},{16,128},{128,144},{144,1},{1,17},{17,129},{129,145},{145,2... | collective-permute-start | bytes 98312 | tf_op jit(solution)/shard_map/ppermute | solution.py:93
  243.7 0.0 collective-permute-done.7
  243.7 0.1 pad_maximum_fusion.4
  243.9 26.5 %all_gather.39 = bf16[320,1024]{0,1:T(8,128)(2,1)S(1)} all-gather(bf16[320,256]{0,1:T(8,128)(2,1)S(1)} %pad_maximum_fusion.4), channel_id=1, replica_groups=mesh['y'=4,'zq'=2,'zp'=4,'c'=2,'x'=4,'zh'=4] {'zp'}, dimensions={1}, use_global_device_ids=true | all-gather | bytes 819200 | tf_op jit(solution)/shard_map/all_gather | solution.py:94
  270.4 0.2 fusion.12
  270.6 2.4 collective-permute-start.8
  273.0 6.9 %psum.23 = f32[320]{0:T(512)S(1)} all-reduce(f32[320]{0:T(512)S(1)} %fusion.12), channel_id=1, replica_groups=mesh['y'=4,'zq'=2,'zp'=4,'c'=2,'x'=4,'zh'=4] {'x'}, use_global_device_ids=true, to_apply=%region_7.8 | all-reduce | flops 320 | bytes 2560 | tf_op jit(solution)/shard_map/psum | solution.py:99
  279.9 0.2 convert_multiply_fusion
  280.1 1.9 multiply_convert_fusion
  282.0 0.1 copy-done.2
  282.1 0.8 fusion.21
  282.9 16.8 %collective-permute-done.8 = bf16[256,256]{0,1:T(8,128)(2,1)S(1)} collective-permute-done((bf16[256,256]{0,1:T(8,128)(2,1)S(1)}, bf16[256,256]{0,1:T(8,128)(2,1)S(1)}, u32[]{:S(2)}, u32[]{:S(2)}) %collective-permute-start.8) | collective-permute-done | bytes 131104 | tf_op jit(solution)/shard_map/ppermute | solution.py:118
  299.7 11.5 %all_to_all.17 = bf16[4,256,256]{1,2,0:T(8,128)(2,1)S(1)} all-to-all(bf16[4,256,256]{1,2,0:T(8,128)(2,1)S(1)} %fusion.21), channel_id=1, replica_groups=mesh['y'=4,'zq'=2,'zp'=4,'c'=2,'x'=4,'zh'=4] {'x'}, dimensions={0} | all-to-all | bytes 1048576 | tf_op jit(solution)/shard_map/all_to_all | solution.py:120
  311.2 0.1 convert_reduce_fusion
  311.3 1.9 collective-permute-start.9
  313.2 18.9 %collective-permute-done.9 = bf16[256,256]{0,1:T(8,128)(2,1)S(1)} collective-permute-done((bf16[256,256]{0,1:T(8,128)(2,1)S(1)}, bf16[256,256]{0,1:T(8,128)(2,1)S(1)}, u32[]{:S(2)}, u32[]{:S(2)}) %collective-permute-start.9) | collective-permute-done | bytes 131104 | tf_op jit(solution)/shard_map/ppermute | solution.py:123
  332.2 0.9 copy.20
  (31 shorter events, 0.4 us)
Async XLA Ops:
  6.5 77.2 %copy-start = (bf16[256,256]{1,0:T(8,128)(2,1)S(1)}, bf16[256,256]{1,0:T(8,128)(2,1)}, u32[]{:S(2)}) copy-start(bf16[256,256]{1,0:T(8,128)(2,1)} %param.4) | copy-start | bytes 393220
  6.5 212.4 %all-gather.4.cloned.1.call-start = ((), (), s32[]{:S(2)}) async-start(), calls=%async_computation.3 | async-start | bytes 5242880 | tf_op jit(solution)/shard_map/all_gather | solution.py:97
  83.8 36.2 %collective-permute-start = (bf16[256,256]{0,1:T(8,128)(2,1)S(1)}, bf16[256,256]{0,1:T(8,128)(2,1)S(1)}, u32[]{:S(2)}, u32[]{:S(2)}) collective-permute-start(bf16[256,256]{0,1:T(8,128)(2,1)S(1)} %copy.11), channel_id=1, source_target_pairs={{0,96},{1,64},{2,32},{3,0},{32,224},{33,192},{34,160},{35,128},{64... | collective-permute-start | bytes 393224 | tf_op jit(solution)/shard_map/ppermute | solution.py:76
  97.2 22.9 %collective-permute-start.1 = (bf16[64,256]{0,1:T(8,128)(2,1)S(1)}, bf16[64,256]{0,1:T(8,128)(2,1)}, u32[]{:S(2)}, u32[]{:S(2)}) collective-permute-start(bf16[64,256]{0,1:T(8,128)(2,1)S(1)} %slice.170), channel_id=1, source_target_pairs={{0,112},{1,80},{2,48},{3,16},{16,224},{17,192},{18,160},{19,128},{... | collective-permute-start | bytes 98312 | tf_op jit(solution)/shard_map/ppermute | solution.py:77
  120.1 25.8 %collective-permute-start.2 = (bf16[1024,256]{0,1:T(8,128)(2,1)S(1)}, bf16[1024,256]{0,1:T(8,128)(2,1)S(1)}, u32[]{:S(2)}, u32[]{:S(2)}) collective-permute-start(bf16[1024,256]{0,1:T(8,128)(2,1)S(1)} %copy.24), channel_id=1, source_target_pairs={{0,256},{256,512},{512,768},{768,0},{1,257},{257,513},{513,769},{7... | collective-permute-start | bytes 1572872 | tf_op jit(solution)/shard_map/ppermute | solution.py:43
  123.3 22.6 %collective-permute-start.3 = (bf16[1024,256]{0,1:T(8,128)(2,1)S(1)}, bf16[1024,256]{0,1:T(8,128)(2,1)}, u32[]{:S(2)}, u32[]{:S(2)}) collective-permute-start(bf16[1024,256]{0,1:T(8,128)(2,1)S(1)} %copy.24), channel_id=1, source_target_pairs={{0,768},{256,0},{512,256},{768,512},{1,769},{257,1},{513,257},{769... | collective-permute-start | bytes 1572872 | tf_op jit(solution)/shard_map/ppermute | solution.py:43
  127.7 18.2 %copy-start.1 = (s32[3,4]{1,0:T(4,128)S(1)}, s32[3,4]{1,0:T(4,128)}, u32[]{:S(2)}) copy-start(s32[3,4]{1,0:T(4,128)} %param.7) | copy-start | bytes 148
  146.6 15.2 %collective-permute-start.4 = (bf16[1024,256]{0,1:T(8,128)(2,1)S(1)}, bf16[1024,256]{0,1:T(8,128)(2,1)S(1)}, u32[]{:S(2)}, u32[]{:S(2)}) collective-permute-start(bf16[1024,256]{0,1:T(8,128)(2,1)S(1)} %copy.24), channel_id=1, source_target_pairs={{0,512},{256,768},{512,0},{768,256},{1,513},{257,769},{513,1},{769... | collective-permute-start | bytes 1572872 | tf_op jit(solution)/shard_map/ppermute | solution.py:43
  175.8 13.4 %collective-permute-start.5 = (bf16[64,256]{0,1:T(8,128)(2,1)S(1)}, bf16[64,256]{0,1:T(8,128)(2,1)S(1)}, u32[]{:S(2)}, u32[]{:S(2)}) collective-permute-start(bf16[64,256]{0,1:T(8,128)(2,1)S(1)} %slice.179), channel_id=1, source_target_pairs={{0,16},{16,128},{128,144},{144,1},{1,17},{17,129},{129,145},{145,2... | collective-permute-start | bytes 98312 | tf_op jit(solution)/shard_map/ppermute | solution.py:93
  207.1 20.1 %collective-permute-start.6 = (bf16[256,256]{0,1:T(8,128)(2,1)S(1)}, bf16[256,256]{0,1:T(8,128)(2,1)S(1)}, u32[]{:S(2)}, u32[]{:S(2)}) collective-permute-start(bf16[256,256]{0,1:T(8,128)(2,1)S(1)} %add_convert_fusion.2), channel_id=1, source_target_pairs={{96,0},{64,1},{32,2},{0,3},{224,32},{192,33},{160,34},{128,35},{97... | collective-permute-start | bytes 393224 | tf_op jit(solution)/shard_map/ppermute | solution.py:118
  237.7 6.1 %collective-permute-start.7 = (bf16[64,256]{0,1:T(8,128)(2,1)S(1)}, bf16[64,256]{0,1:T(8,128)(2,1)S(1)}, u32[]{:S(2)}, u32[]{:S(2)}) collective-permute-start(bf16[64,256]{0,1:T(8,128)(2,1)S(1)} %slice.185), channel_id=1, source_target_pairs={{0,16},{16,128},{128,144},{144,1},{1,17},{17,129},{129,145},{145,2... | collective-permute-start | bytes 98312 | tf_op jit(solution)/shard_map/ppermute | solution.py:93
  270.6 29.1 %collective-permute-start.8 = (bf16[256,256]{0,1:T(8,128)(2,1)S(1)}, bf16[256,256]{0,1:T(8,128)(2,1)S(1)}, u32[]{:S(2)}, u32[]{:S(2)}) collective-permute-start(bf16[256,256]{0,1:T(8,128)(2,1)S(1)} %add_convert_fusion.1), channel_id=1, source_target_pairs={{96,0},{64,1},{32,2},{0,3},{224,32},{192,33},{160,34},{128,35},{97... | collective-permute-start | bytes 393224 | tf_op jit(solution)/shard_map/ppermute | solution.py:118
  279.9 2.2 copy-start.2
  311.3 20.9 %collective-permute-start.9 = (bf16[256,256]{0,1:T(8,128)(2,1)S(1)}, bf16[256,256]{0,1:T(8,128)(2,1)S(1)}, u32[]{:S(2)}, u32[]{:S(2)}) collective-permute-start(bf16[256,256]{0,1:T(8,128)(2,1)S(1)} %add_convert_fusion), channel_id=1, source_target_pairs={{96,0},{64,1},{32,2},{0,3},{224,32},{192,33},{160,34},{128,35},{97... | collective-permute-start | bytes 393224 | tf_op jit(solution)/shard_map/ppermute | solution.py:123
Sparse Core Ops, SparseCore 0:
  146.0 61.7 all-gather.3

commit v12 on v11

--- a/solution.py
+++ b/solution.py
@@ -71,10 +71,10 @@
         ],
         axis=0,
     )
+    before = lax.ppermute(signal[row_count - REACH :], SECTION + ("zh",), first_halo_pairs(n_y, n_zl, n_c, n_zh))
     got = lax.all_gather(sent, "zh", axis=0)
-    signal, got = lax.optimization_barrier((signal, got))
+    signal, before, got = lax.optimization_barrier((signal, before, got))
     hidden = lax.ppermute(signal, MOVED, there)
-    before = lax.ppermute(signal[row_count - REACH :], SECTION + ("zh",), first_halo_pairs(n_y, n_zl, n_c, n_zh))
     got = got[::-1]
     coeffs = got[:, layers * half :].astype(jnp.float32)
     coeffs = coeffs[:, :n_tap_rows] + coeffs[:, n_tap_rows : 2 * n_tap_rows]

time: 342 us -> 353 us (1.032)
  the two profiles are of different devices: /device:TPU:97 before, /device:TPU:121 now
where the time goes in v12:
time: 353 us; the launch traced here: 352 us
  blocking collectives  166 us (47%)
  starting transfers between devices  91.3 us (26%)
  waiting for transfers between devices  54.7 us (15%)
  between operations  21.4 us (6%)
  other arithmetic  9.57 us (3%)
  local copies, waits for them, and re-layouts  5.74 us (2%)
  matrix products  3.83 us (1%)
    all_gather x1, blocking collectives, body(): got = lax.all_gather(sent, 'zh', axis=0)  52.9 us
    all_gather x3, blocking collectives, body(): lax.all_gather(jnp.concatenate([before, hidden], axis=0), 'zp', axis=1, t...  51.9 us
    all_to_all x3, blocking collectives, body(): terms = lax.all_to_all(partial, 'x', split_axis=0, concat_axis=0)  31.5 us
    ppermute x2, starting transfers between devices, body(): before = lax.ppermute(hidden[row_count - REACH:], PLACE, forward)  30 us
    ppermute x1, starting transfers between devices, body(): lax.ppermute(signal[row_count - REACH:], SECTION + ('zh',), first_halo_pa...  26.6 us
    ppermute x2, waiting for transfers between devices, body(): lax.ppermute(ready, MOVED, back)  26.3 us
    psum x3, blocking collectives, body(): squares = lax.psum(jnp.sum(values * values, axis=-1), 'x')  22.8 us
    ppermute x1, waiting for transfers between devices, body(): returned.append(lax.ppermute(hidden, MOVED, back))  22.2 us
  transfers between devices with their start and end apart: 11, of which 5 were waited for; matrix products, arithmetic and copies ran while one was open for 4% of the time, Pallas kernels for 0%

profile of v12, /device:TPU:121, one launch (start us, length us, event | category | flops | bytes accessed | tf_op | source)
XLA Modules:
  0.0 352.4 jit_solution(6120852630794692389)
XLA Ops:
  6.5 0.8 slice.126
  7.3 0.1 copy.28
  7.4 26.6 %collective-permute-start = (bf16[64,256]{0,1:T(8,128)(2,1)S(1)}, bf16[64,256]{0,1:T(8,128)(2,1)S(1)}, u32[]{:S(2)}, u32[]{:S(2)}) collective-permute-start(bf16[64,256]{0,1:T(8,128)(2,1)S(1)} %copy.28), channel_id=1, source_target_pairs={{0,112},{1,80},{2,48},{3,16},{16,224},{17,192},{18,160},{19,128},{... | collective-permute-start | bytes 98312 | tf_op jit(solution)/shard_map/ppermute | solution.py:74
  34.0 0.7 reduce-precision_convert_fusion
  34.7 0.1 pad.18.clone
  34.8 0.9 constant_dynamic-slice_fusion
  35.8 0.1 maximum_maximum_fusion
  35.9 52.9 %all-gather = bf16[1664,256]{1,0:T(8,128)(2,1)S(1)} all-gather(bf16[416,256]{1,0:T(8,128)(2,1)S(1)} %maximum_maximum_fusion), channel_id=2, replica_groups=mesh['y'=4,'zq'=2,'zp'=4,'c'=2,'x'=4,'zh'=4] {'zh'}, dimensions={0}, use_global_device_ids=true | all-gather | bytes 1064960 | tf_op jit(solution)/shard_map/all_gather | solution.py:75
  88.8 0.1 fusion.34
  88.9 2.2 all_gather.32
  91.1 0.2 copy.24
  91.3 2.2 all_gather.33
  93.5 0.1 copy.12
  93.6 14.9 %collective-permute-start.1 = (bf16[256,256]{0,1:T(8,128)(2,1)S(1)}, bf16[256,256]{0,1:T(8,128)(2,1)S(1)}, u32[]{:S(2)}, u32[]{:S(2)}) collective-permute-start(bf16[256,256]{0,1:T(8,128)(2,1)S(1)} %copy.12), channel_id=1, source_target_pairs={{0,96},{1,64},{2,32},{3,0},{32,224},{33,192},{34,160},{35,128},{64... | collective-permute-start | bytes 393224 | tf_op jit(solution)/shard_map/ppermute | solution.py:77
  108.5 2.5 all_gather.34
  111.0 6.1 %collective-permute-done.1 = bf16[256,256]{0,1:T(8,128)(2,1)S(1)} collective-permute-done((bf16[256,256]{0,1:T(8,128)(2,1)S(1)}, bf16[256,256]{0,1:T(8,128)(2,1)S(1)}, u32[]{:S(2)}, u32[]{:S(2)}) %collective-permute-start.1) | collective-permute-done | bytes 131104 | tf_op jit(solution)/shard_map/ppermute | solution.py:77
  117.0 1.9 collective-permute-start.2
  118.9 3.4 collective-permute-start.3
  122.3 1.1 pad_maximum_fusion
  123.4 0.1 pad_maximum_fusion.2
  123.5 16.3 %all_gather.35 = bf16[320,1024]{0,1:T(8,128)(2,1)S(1)} all-gather(bf16[320,256]{0,1:T(8,128)(2,1)S(1)} %pad_maximum_fusion.2), channel_id=1, replica_groups=mesh['y'=4,'zq'=2,'zp'=4,'c'=2,'x'=4,'zh'=4] {'zp'}, dimensions={1}, use_global_device_ids=true | all-gather | bytes 819200 | tf_op jit(solution)/shard_map/all_gather | solution.py:94
  139.9 0.7 fusion.36
  143.2 3.7 %collective-permute-start.4 = (bf16[1024,256]{0,1:T(8,128)(2,1)S(1)}, bf16[1024,256]{0,1:T(8,128)(2,1)S(1)}, u32[]{:S(2)}, u32[]{:S(2)}) collective-permute-start(bf16[1024,256]{0,1:T(8,128)(2,1)S(1)} %copy.24), channel_id=1, source_target_pairs={{0,512},{256,768},{512,0},{768,256},{1,513},{257,769},{513,1},{769... | collective-permute-start | bytes 1572872 | tf_op jit(solution)/shard_map/ppermute | solution.py:43
  147.0 0.2 fusion.10
  147.3 8.8 %psum.21 = f32[320]{0:T(512)S(1)} all-reduce(f32[320]{0:T(512)S(1)} %fusion.10), channel_id=1, replica_groups=mesh['y'=4,'zq'=2,'zp'=4,'c'=2,'x'=4,'zh'=4] {'x'}, use_global_device_ids=true, to_apply=%region_1.2 | all-reduce | flops 320 | bytes 2560 | tf_op jit(solution)/shard_map/psum | solution.py:99
  156.0 0.8 copy-done.3
  156.8 0.2 convert_multiply_fusion.4
  157.1 1.9 multiply_convert_fusion.2
  158.9 0.7 fusion.18
  159.7 0.6 gather_fusion
  160.3 10.7 %all_to_all.15 = bf16[4,256,256]{1,2,0:T(8,128)(2,1)S(1)} all-to-all(bf16[4,256,256]{1,2,0:T(8,128)(2,1)S(1)} %gather_fusion), channel_id=1, replica_groups=mesh['y'=4,'zq'=2,'zp'=4,'c'=2,'x'=4,'zh'=4] {'x'}, dimensions={0} | all-to-all | bytes 1048576 | tf_op jit(solution)/shard_map/all_to_all | solution.py:120
  171.0 0.1 convert_reduce_fusion.2
  171.1 0.1 slice.178
  171.2 26.9 %collective-permute-start.5 = (bf16[64,256]{0,1:T(8,128)(2,1)S(1)}, bf16[64,256]{0,1:T(8,128)(2,1)S(1)}, u32[]{:S(2)}, u32[]{:S(2)}) collective-permute-start(bf16[64,256]{0,1:T(8,128)(2,1)S(1)} %slice.178), channel_id=1, source_target_pairs={{0,16},{16,128},{128,144},{144,1},{1,17},{17,129},{129,145},{145,2... | collective-permute-start | bytes 98312 | tf_op jit(solution)/shard_map/ppermute | solution.py:93
  200.5 0.1 collective-permute-done.5
  200.7 0.1 pad_maximum_fusion.3
  200.8 13.3 %all_gather.38 = bf16[320,1024]{0,1:T(8,128)(2,1)S(1)} all-gather(bf16[320,256]{0,1:T(8,128)(2,1)S(1)} %pad_maximum_fusion.3), channel_id=1, replica_groups=mesh['y'=4,'zq'=2,'zp'=4,'c'=2,'x'=4,'zh'=4] {'zp'}, dimensions={1}, use_global_device_ids=true | all-gather | bytes 819200 | tf_op jit(solution)/shard_map/all_gather | solution.py:94
  214.1 4.4 %collective-permute-start.6 = (bf16[256,256]{0,1:T(8,128)(2,1)S(1)}, bf16[256,256]{0,1:T(8,128)(2,1)S(1)}, u32[]{:S(2)}, u32[]{:S(2)}) collective-permute-start(bf16[256,256]{0,1:T(8,128)(2,1)S(1)} %add_convert_fusion.2), channel_id=1, source_target_pairs={{96,0},{64,1},{32,2},{0,3},{224,32},{192,33},{160,34},{128,35},{97... | collective-permute-start | bytes 393224 | tf_op jit(solution)/shard_map/ppermute | solution.py:118
  218.5 0.2 fusion.11
  218.8 7.2 %psum.22 = f32[320]{0:T(512)S(1)} all-reduce(f32[320]{0:T(512)S(1)} %fusion.11), channel_id=1, replica_groups=mesh['y'=4,'zq'=2,'zp'=4,'c'=2,'x'=4,'zh'=4] {'x'}, use_global_device_ids=true, to_apply=%region_4.5 | all-reduce | flops 320 | bytes 2560 | tf_op jit(solution)/shard_map/psum | solution.py:99
  226.0 0.2 convert_multiply_fusion.2
  226.2 1.9 multiply_convert_fusion.1
  228.0 0.0 all-gather.4.cloned.1.call-done
  228.1 2.4 fusion.22
  230.4 9.9 %collective-permute-done.6 = bf16[256,256]{0,1:T(8,128)(2,1)S(1)} collective-permute-done((bf16[256,256]{0,1:T(8,128)(2,1)S(1)}, bf16[256,256]{0,1:T(8,128)(2,1)S(1)}, u32[]{:S(2)}, u32[]{:S(2)}) %collective-permute-start.6) | collective-permute-done | bytes 131104 | tf_op jit(solution)/shard_map/ppermute | solution.py:118
  240.4 9.3 %all_to_all.16 = bf16[4,256,256]{1,2,0:T(8,128)(2,1)S(1)} all-to-all(bf16[4,256,256]{1,2,0:T(8,128)(2,1)S(1)} %fusion.22), channel_id=1, replica_groups=mesh['y'=4,'zq'=2,'zp'=4,'c'=2,'x'=4,'zh'=4] {'x'}, dimensions={0} | all-to-all | bytes 1048576 | tf_op jit(solution)/shard_map/all_to_all | solution.py:120
  249.7 0.1 convert_reduce_fusion.1
  249.8 0.1 slice.184
  249.9 3.1 collective-permute-start.7
  255.5 0.1 pad_maximum_fusion.4
  255.6 22.3 %all_gather.39 = bf16[320,1024]{0,1:T(8,128)(2,1)S(1)} all-gather(bf16[320,256]{0,1:T(8,128)(2,1)S(1)} %pad_maximum_fusion.4), channel_id=1, replica_groups=mesh['y'=4,'zq'=2,'zp'=4,'c'=2,'x'=4,'zh'=4] {'zp'}, dimensions={1}, use_global_device_ids=true | all-gather | bytes 819200 | tf_op jit(solution)/shard_map/all_gather | solution.py:94
  277.9 0.2 fusion.12
  278.1 4.7 %collective-permute-start.8 = (bf16[256,256]{0,1:T(8,128)(2,1)S(1)}, bf16[256,256]{0,1:T(8,128)(2,1)S(1)}, u32[]{:S(2)}, u32[]{:S(2)}) collective-permute-start(bf16[256,256]{0,1:T(8,128)(2,1)S(1)} %add_convert_fusion.1), channel_id=1, source_target_pairs={{96,0},{64,1},{32,2},{0,3},{224,32},{192,33},{160,34},{128,35},{97... | collective-permute-start | bytes 393224 | tf_op jit(solution)/shard_map/ppermute | solution.py:118
  282.8 6.9 %psum.23 = f32[320]{0:T(512)S(1)} all-reduce(f32[320]{0:T(512)S(1)} %fusion.12), channel_id=1, replica_groups=mesh['y'=4,'zq'=2,'zp'=4,'c'=2,'x'=4,'zh'=4] {'x'}, use_global_device_ids=true, to_apply=%region_7.8 | all-reduce | flops 320 | bytes 2560 | tf_op jit(solution)/shard_map/psum | solution.py:99
  289.7 0.2 convert_multiply_fusion
  289.9 1.9 multiply_convert_fusion
  291.8 0.1 copy-done.2
  291.9 0.8 fusion.21
  292.6 16.3 %collective-permute-done.8 = bf16[256,256]{0,1:T(8,128)(2,1)S(1)} collective-permute-done((bf16[256,256]{0,1:T(8,128)(2,1)S(1)}, bf16[256,256]{0,1:T(8,128)(2,1)S(1)}, u32[]{:S(2)}, u32[]{:S(2)}) %collective-permute-start.8) | collective-permute-done | bytes 131104 | tf_op jit(solution)/shard_map/ppermute | solution.py:118
  309.0 11.5 %all_to_all.17 = bf16[4,256,256]{1,2,0:T(8,128)(2,1)S(1)} all-to-all(bf16[4,256,256]{1,2,0:T(8,128)(2,1)S(1)} %fusion.21), channel_id=1, replica_groups=mesh['y'=4,'zq'=2,'zp'=4,'c'=2,'x'=4,'zh'=4] {'x'}, dimensions={0} | all-to-all | bytes 1048576 | tf_op jit(solution)/shard_map/all_to_all | solution.py:120
  320.4 0.1 convert_reduce_fusion
  320.5 1.9 collective-permute-start.9
  322.5 22.2 %collective-permute-done.9 = bf16[256,256]{0,1:T(8,128)(2,1)S(1)} collective-permute-done((bf16[256,256]{0,1:T(8,128)(2,1)S(1)}, bf16[256,256]{0,1:T(8,128)(2,1)S(1)}, u32[]{:S(2)}, u32[]{:S(2)}) %collective-permute-start.9) | collective-permute-done | bytes 131104 | tf_op jit(solution)/shard_map/ppermute | solution.py:123
  344.7 0.9 copy.20
  (36 shorter events, 0.4 us)
Async XLA Ops:
  6.5 221.5 %all-gather.4.cloned.1.call-start = ((), (), s32[]{:S(2)}) async-start(), calls=%async_computation.3 | async-start | bytes 5242880 | tf_op jit(solution)/shard_map/all_gather | solution.py:97
  7.4 81.4 %collective-permute-start = (bf16[64,256]{0,1:T(8,128)(2,1)S(1)}, bf16[64,256]{0,1:T(8,128)(2,1)S(1)}, u32[]{:S(2)}, u32[]{:S(2)}) collective-permute-start(bf16[64,256]{0,1:T(8,128)(2,1)S(1)} %copy.28), channel_id=1, source_target_pairs={{0,112},{1,80},{2,48},{3,16},{16,224},{17,192},{18,160},{19,128},{... | collective-permute-start | bytes 98312 | tf_op jit(solution)/shard_map/ppermute | solution.py:74
  91.1 2.4 copy-start
  93.6 23.4 %collective-permute-start.1 = (bf16[256,256]{0,1:T(8,128)(2,1)S(1)}, bf16[256,256]{0,1:T(8,128)(2,1)S(1)}, u32[]{:S(2)}, u32[]{:S(2)}) collective-permute-start(bf16[256,256]{0,1:T(8,128)(2,1)S(1)} %copy.12), channel_id=1, source_target_pairs={{0,96},{1,64},{2,32},{3,0},{32,224},{33,192},{34,160},{35,128},{64... | collective-permute-start | bytes 393224 | tf_op jit(solution)/shard_map/ppermute | solution.py:77
  117.0 22.8 %collective-permute-start.2 = (bf16[1024,256]{0,1:T(8,128)(2,1)S(1)}, bf16[1024,256]{0,1:T(8,128)(2,1)S(1)}, u32[]{:S(2)}, u32[]{:S(2)}) collective-permute-start(bf16[1024,256]{0,1:T(8,128)(2,1)S(1)} %copy.24), channel_id=1, source_target_pairs={{0,256},{256,512},{512,768},{768,0},{1,257},{257,513},{513,769},{7... | collective-permute-start | bytes 1572872 | tf_op jit(solution)/shard_map/ppermute | solution.py:43
  118.9 20.9 %collective-permute-start.3 = (bf16[1024,256]{0,1:T(8,128)(2,1)S(1)}, bf16[1024,256]{0,1:T(8,128)(2,1)S(1)}, u32[]{:S(2)}, u32[]{:S(2)}) collective-permute-start(bf16[1024,256]{0,1:T(8,128)(2,1)S(1)} %copy.24), channel_id=1, source_target_pairs={{0,768},{256,0},{512,256},{768,512},{1,769},{257,1},{513,257},{769... | collective-permute-start | bytes 1572872 | tf_op jit(solution)/shard_map/ppermute | solution.py:43
  123.4 16.5 %copy-start.1 = (s32[3,4]{1,0:T(4,128)S(1)}, s32[3,4]{1,0:T(4,128)}, u32[]{:S(2)}) copy-start(s32[3,4]{1,0:T(4,128)} %param.7) | copy-start | bytes 148
  143.2 12.9 %collective-permute-start.4 = (bf16[1024,256]{0,1:T(8,128)(2,1)S(1)}, bf16[1024,256]{0,1:T(8,128)(2,1)S(1)}, u32[]{:S(2)}, u32[]{:S(2)}) collective-permute-start(bf16[1024,256]{0,1:T(8,128)(2,1)S(1)} %copy.24), channel_id=1, source_target_pairs={{0,512},{256,768},{512,0},{768,256},{1,513},{257,769},{513,1},{769... | collective-permute-start | bytes 1572872 | tf_op jit(solution)/shard_map/ppermute | solution.py:43
  156.0 0.8 copy-start.3
  157.0 1.9 copy-start.4
  171.2 29.5 %collective-permute-start.5 = (bf16[64,256]{0,1:T(8,128)(2,1)S(1)}, bf16[64,256]{0,1:T(8,128)(2,1)S(1)}, u32[]{:S(2)}, u32[]{:S(2)}) collective-permute-start(bf16[64,256]{0,1:T(8,128)(2,1)S(1)} %slice.178), channel_id=1, source_target_pairs={{0,16},{16,128},{128,144},{144,1},{1,17},{17,129},{129,145},{145,2... | collective-permute-start | bytes 98312 | tf_op jit(solution)/shard_map/ppermute | solution.py:93
  214.1 26.2 %collective-permute-start.6 = (bf16[256,256]{0,1:T(8,128)(2,1)S(1)}, bf16[256,256]{0,1:T(8,128)(2,1)S(1)}, u32[]{:S(2)}, u32[]{:S(2)}) collective-permute-start(bf16[256,256]{0,1:T(8,128)(2,1)S(1)} %add_convert_fusion.2), channel_id=1, source_target_pairs={{96,0},{64,1},{32,2},{0,3},{224,32},{192,33},{160,34},{128,35},{97... | collective-permute-start | bytes 393224 | tf_op jit(solution)/shard_map/ppermute | solution.py:118
  249.9 5.6 %collective-permute-start.7 = (bf16[64,256]{0,1:T(8,128)(2,1)S(1)}, bf16[64,256]{0,1:T(8,128)(2,1)S(1)}, u32[]{:S(2)}, u32[]{:S(2)}) collective-permute-start(bf16[64,256]{0,1:T(8,128)(2,1)S(1)} %slice.184), channel_id=1, source_target_pairs={{0,16},{16,128},{128,144},{144,1},{1,17},{17,129},{129,145},{145,2... | collective-permute-start | bytes 98312 | tf_op jit(solution)/shard_map/ppermute | solution.py:93
  278.1 30.8 %collective-permute-start.8 = (bf16[256,256]{0,1:T(8,128)(2,1)S(1)}, bf16[256,256]{0,1:T(8,128)(2,1)S(1)}, u32[]{:S(2)}, u32[]{:S(2)}) collective-permute-start(bf16[256,256]{0,1:T(8,128)(2,1)S(1)} %add_convert_fusion.1), channel_id=1, source_target_pairs={{96,0},{64,1},{32,2},{0,3},{224,32},{192,33},{160,34},{128,35},{97... | collective-permute-start | bytes 393224 | tf_op jit(solution)/shard_map/ppermute | solution.py:118
  289.7 2.2 copy-start.2
  320.5 24.1 %collective-permute-start.9 = (bf16[256,256]{0,1:T(8,128)(2,1)S(1)}, bf16[256,256]{0,1:T(8,128)(2,1)S(1)}, u32[]{:S(2)}, u32[]{:S(2)}) collective-permute-start(bf16[256,256]{0,1:T(8,128)(2,1)S(1)} %add_convert_fusion), channel_id=1, source_target_pairs={{96,0},{64,1},{32,2},{0,3},{224,32},{192,33},{160,34},{128,35},{97... | collective-permute-start | bytes 393224 | tf_op jit(solution)/shard_map/ppermute | solution.py:123
Sparse Core Ops, SparseCore 0:
  140.0 72.7 all-gather.3
